TPU v7x, 128 devices: a whole 4x4x4 slice. The times are simulated.
128 devices in a mesh: gx: 4 (over y), gy: 4 (over x), gz: 8 (over z, core).
Axes of the slice: x: 4, y: 4, z: 4, core: 2. Of those that a mesh axis runs over, the one named last changes fastest.
Arguments:
- blocks: bfloat16 [32768, 64, 448], P(('gx', 'gy', 'gz')), may hold values from -1.1953125 to 1.1953125
- prolong: bfloat16 [32768, 4096], P(('gx', 'gy', 'gz')), may hold values from -0.75 to 0.75
- new_owner: int32 [32768], P(('gx', 'gy', 'gz')), may hold values from 0 to 127, as said below
- arrival: int32 [32768], P(('gx', 'gy', 'gz')), may hold values from 0 to 303, as said below
- columns: int32 [32768, 7], P(('gx', 'gy', 'gz')), may hold values from -1 to 639, as said below
- targets: int32 [32768, 7], P(('gx', 'gy', 'gz')), may hold values from 0 to 223, as said below
- ghost_lists: int32 [128, 6, 64], P(('gx', 'gy', 'gz')), may hold values from 0 to 255
- touched: int32 [128, 224], P(('gx', 'gy', 'gz')), may hold values from 0 to 63
Outputs:
- coarse: float32 [8192, 4096], P(('gx', 'gy', 'gz'))
Inputs may be any that keep to these rules, and one draw needn't show every extreme that they name: `new_owner`: every row's new owner is in the same gz column (same gx and gy index); two devices adjacent along gz swap the same number of rows both ways, between 4 and 6, and some adjacent pair swaps exactly 6; every other pair of distinct devices of a column swaps exactly 2 rows each way; so every device holds 256 rows after the move. `arrival`: below 256: an old row of the same device that stays; else 256 + p * 6 + r, the row of rank r among those that the device of gz index p of the column hands over; every staying and every handed-over row is named once. `columns`: entry 0 is the row's own new local index; entry k >= 1 is -1, a local row below 256, or 256 + (k - 1) * 64 + q, the q-th block sent by the neighbour in direction k - 1, which then exists. `targets`: a value v * 32 + q names, for v = 0, a coarse block of the device itself, and for v >= 1 one owned by its neighbour in direction v - 1, which then exists.
All inputs are finite; a program needn't handle non-finite values.
Results may differ from a plain program's by a relative error of at most 0.0029.
Values may be sent and summed in bfloat16 or wider, within the bound.
No kernel may reach another device: no remote copies, remote signals or barrier semaphores. Data moves between devices by JAX's collectives and lax.ppermute only.
A program may use at most 256 MiB of HBM per device.

v0:
```python
import jax
import jax.numpy as jnp
from jax import lax
from jax.sharding import Mesh
from jax.sharding import PartitionSpec as P

B = 64
NBR = 7
CAP = 6
GCAP = 64
UCAP = 32
U_DEV = 224
CE_DEV = 64
GZ = ("gz_0", "gz_1")
GX_GY_GZ = ("gx", "gy", "gz_0", "gz_1")


def in_blocks(value, dim, devices):
    lengths = value.shape
    tiles = value.reshape(*lengths[:dim], devices, lengths[dim] // devices, *lengths[dim + 1 :])
    return jnp.moveaxis(tiles, dim, 0)


def in_order(tiles, dim):
    tiles = jnp.moveaxis(tiles, 0, dim)
    lengths = tiles.shape
    return tiles.reshape(*lengths[:dim], lengths[dim] * lengths[dim + 1], *lengths[dim + 2 :])


def exchange_in_order(tiles, axes, sequence):
    lengths = [lax.axis_size(a) for a in axes]
    tiles = tiles.reshape(*lengths, *tiles.shape[1:])
    for k in sequence:
        tiles = lax.all_to_all(tiles, axes[k], split_axis=k, concat_axis=k, tiled=True)
    return tiles.reshape(-1, *tiles.shape[len(axes) :])


def core_and_chips(value, groups, sequence, split_dim, concat_dim):
    devices = lax.axis_size(groups[0]) * lax.axis_size(groups[1])
    tiles = in_blocks(value, split_dim, devices)
    return in_order(exchange_in_order(tiles, groups, sequence), concat_dim)


def shifted(value, axis, by):
    devices = lax.axis_size(axis)
    pairs = [(i, i + by) for i in range(devices) if 0 <= i + by < devices]
    return lax.ppermute(value, axis, pairs)


def rank_within(labels, label_count):
    onehot = (labels[:, None] == jnp.arange(label_count, dtype=jnp.int32)[None, :]).astype(
        jnp.int32
    )
    before = jnp.cumsum(onehot, axis=0) - onehot
    return jnp.sum(before * onehot, axis=1)


def shards(blocks, prolong, new_owner, arrival, columns, targets, ghost_lists, touched):
    row_count = blocks.shape[0]
    row_shape = blocks.shape[1:]
    block_area = prolong.shape[1]
    block_side = B
    layers = lax.axis_size(GZ)
    own_layer = lax.axis_index(GZ)
    peer_layer = new_owner % layers
    staying = peer_layer == own_layer
    row_ranks = rank_within(peer_layer, layers)
    slot_key = jnp.where(staying, layers * CAP, peer_layer * CAP + row_ranks)
    outgoing = jnp.zeros((layers * CAP + 1,) + row_shape, jnp.bfloat16).at[slot_key].set(blocks)
    incoming = core_and_chips(outgoing[: layers * CAP], ("gz_0", "gz_1"), (1, 0), 0, 0)
    row_table = jnp.concatenate([blocks, incoming], axis=0)
    arrived_rows = row_table[arrival]
    strides = (lax.axis_size("gy") * layers, layers, 1)
    outbound = prolong[ghost_lists[0].reshape(-1)].reshape(6, GCAP, block_area)
    ghost_parts = [prolong]
    for facing in range(6):
        stride = strides[facing // 2]
        orient = 1 - 2 * (facing % 2)
        ghost_parts.append(shifted(outbound[facing ^ 1], GX_GY_GZ, -orient * stride))
    block_table = jnp.concatenate(ghost_parts, axis=0)
    live_mask = columns >= 0
    own_block = prolong.reshape(row_count, block_side, block_side)
    left = jnp.einsum(
        "rba,rbx->rax", own_block, arrived_rows, preferred_element_type=jnp.float32
    ).astype(jnp.bfloat16)
    left = left.reshape(row_count, block_side, NBR, block_side)
    neighbour = block_table[jnp.maximum(columns, 0)].reshape(row_count, NBR, block_side, block_side)
    partial_blocks = jnp.einsum(
        "rakb,rkbc->rkac", left, neighbour, preferred_element_type=jnp.float32
    )
    onehot = (
        (targets[:, :, None] == jnp.arange(U_DEV, dtype=jnp.int32)[None, None, :])
        & live_mask[:, :, None]
    ).astype(jnp.float32)
    slot_sums = jnp.einsum(
        "rku,rkx->ux",
        onehot,
        partial_blocks.reshape(row_count, NBR, block_area),
        precision=lax.Precision.HIGHEST,
        preferred_element_type=jnp.float32,
    )
    touched_here = touched[0]
    collected_blocks = [slot_sums[:UCAP]]
    collected_index = [touched_here[:UCAP]]
    for facing in range(6):
        stride = strides[facing // 2]
        orient = 1 - 2 * (facing % 2)
        first_slot = (facing + 1) * UCAP
        got_blocks, got_index = shifted(
            (
                slot_sums[first_slot : first_slot + UCAP],
                touched_here[first_slot : first_slot + UCAP],
            ),
            GX_GY_GZ,
            orient * stride,
        )
        collected_blocks.append(got_blocks)
        collected_index.append(got_index)
    gathered_blocks = jnp.concatenate(collected_blocks, axis=0)
    gathered_index = jnp.concatenate(collected_index, axis=0)
    selector = (jnp.arange(CE_DEV, dtype=jnp.int32)[:, None] == gathered_index[None, :]).astype(
        jnp.float32
    )
    return jnp.dot(
        selector,
        gathered_blocks,
        precision=lax.Precision.HIGHEST,
        preferred_element_type=jnp.float32,
    )


def solution(mesh):
    split = Mesh(
        mesh.devices.reshape(mesh.shape["gx"], mesh.shape["gy"], 4, 2), ("gx", "gy", "gz_0", "gz_1")
    )
    return jax.shard_map(
        shards,
        mesh=split,
        in_specs=(
            P(GX_GY_GZ, None, None),
            P(GX_GY_GZ, None),
            P(GX_GY_GZ),
            P(GX_GY_GZ),
            P(GX_GY_GZ, None),
            P(GX_GY_GZ, None),
            P(GX_GY_GZ, None, None),
            P(GX_GY_GZ, None),
        ),
        out_specs=P(GX_GY_GZ, None),
        check_vma=False,
    )
```

profile of v0, /device:TPU:24, one launch (start us, length us, event | category | flops | bytes accessed | tf_op | source)
XLA Modules:
  0.0 491.3 jit_solution(6328455723693894660)
XLA Ops:
  0.8 9.4 %gather_fusion.1 = bf16[384,4096]{1,0:T(8,128)(2,1)S(1)} fusion(bf16[256,4096]{1,0:T(8,128)(2,1)} %param.9, s32[1024]{0:T(1024)S(1)} %pad_clamp_fusion.1), kind=kCustom, calls=%fused_computation.1 | custom fusion | bytes 6292992 | tf_op jit(solution)/shard_map/gather | solution.py:74
  11.9 3.4 collective-permute-start.6
  16.6 6.7 %collective-permute-start.8 = (bf16[64,4096]{1,0:T(8,128)(2,1)}, bf16[64,4096]{1,0:T(8,128)(2,1)}, u32[]{:S(2)}, u32[]{:S(2)}) collective-permute-start(bf16[64,4096]{1,0:T(8,128)(2,1)} %get-tuple-element.15), channel_id=1, source_target_pairs={{8,0},{9,1},{10,2},{11,3},{12,4},{13,5},{14,6},{15,7},{16,8},{17,9... | collective-permute-start | bytes 1572872 | tf_op jit(solution)/shard_map/ppermute | solution.py:47
  25.3 7.8 %collective-permute-start.10 = (bf16[64,4096]{1,0:T(8,128)(2,1)}, bf16[64,4096]{1,0:T(8,128)(2,1)}, u32[]{:S(2)}, u32[]{:S(2)}) collective-permute-start(bf16[64,4096]{1,0:T(8,128)(2,1)} %get-tuple-element.13), channel_id=1, source_target_pairs={{1,0},{2,1},{3,2},{4,3},{5,4},{6,5},{7,6},{8,7},{9,8},{10,9},{11,1... | collective-permute-start | bytes 1572872 | tf_op jit(solution)/shard_map/ppermute | solution.py:47
  34.0 23.3 %copy.25 = bf16[256,64,448]{2,1,0:T(8,128)(2,1)} copy(bf16[256,64,448]{0,2,1:T(8,128)(2,1)} %param.8) | data formatting | bytes 29360128 | tf_op args[0]
  57.9 26.9 %scatter_fusion = bf16[49,64,448]{2,1,0:T(8,128)(2,1)S(1)} fusion(bf16[49,64,448]{2,1,0:T(8,128)(2,1)S(1)} %broadcast_in_dim.12, s32[256]{0:T(256)S(1)} %compare_select_fusion.2, bf16[256,64,448]{2,1,0:T(8,128)(2,1)} %copy.25), kind=kCustom, calls=%fused_computation.3 | custom fusion | bytes 44041216 | tf_op jit(solution)/shard_map/scatter | solution.py:69
  85.4 6.3 %all_to_all.10 = bf16[4,2,6,64,448]{4,3,2,0,1:T(8,128)(2,1)S(1)} all-to-all(bf16[4,2,6,64,448]{4,3,2,0,1:T(8,128)(2,1)S(1)} %copy.23), channel_id=1, replica_groups=mesh['gx'=4,'gy'=4,'gz_0'=4,'gz_1'=2] {'gz_1'}, dimensions={1} | all-to-all | bytes 5505024 | tf_op jit(solution)/shard_map/all_to_all | solution.py:34
  93.8 4.8 all-to-all-start.1
  98.6 2.5 copy.26
  102.0 9.0 %copy.27 = bf16[256,64,64]{1,2,0:T(8,128)(2,1)} copy(bf16[256,64,64]{0,2,1:T(8,128)(2,1)} %bitcast.42) | data formatting | bytes 4194304 | tf_op jit(solution)/shard_map/reshape | solution.py:82
  112.4 2.2 collective-permute-start.11
  124.0 7.3 %collective-permute-done.11 = bf16[64,4096]{1,0:T(8,128)(2,1)S(1)} collective-permute-done((bf16[64,4096]{1,0:T(8,128)(2,1)S(1)}, bf16[64,4096]{1,0:T(8,128)(2,1)S(1)}, u32[]{:S(2)}, u32[]{:S(2)}) %collective-permute-start.11) | collective-permute-done | bytes 524320 | tf_op jit(solution)/shard_map/ppermute | solution.py:47
  132.1 28.6 %gather_fusion.2 = bf16[1792,4096]{1,0:T(8,128)(2,1)} fusion(bf16[640,4096]{1,0:T(8,128)(2,1)} %constant_dynamic-update-slice_fusion, s32[2048]{0:T(1024)S(1)} %pad_clamp_fusion), kind=kCustom, calls=%fused_computation.2 | custom fusion | bytes 29367296 | tf_op jit(solution)/shard_map/gather | solution.py:87
  160.7 40.3 %reshape.82 = bf16[256,7,64,64]{3,2,1,0:T(8,128)(2,1)} reshape(bf16[1792,4096]{1,0:T(8,128)(2,1)} %gather_fusion.2) | data formatting | bytes 29360128 | tf_op jit(solution)/shard_map/reshape | solution.py:87
  201.0 19.4 %pad_maximum_fusion = bf16[304,64,448]{2,1,0:T(8,128)(2,1)} fusion(bf16[48,64,448]{2,1,0:T(8,128)(2,1)} %bitcast.11, bf16[256,64,448]{2,1,0:T(8,128)(2,1)} %copy.25), kind=kLoop, calls=%fused_computation.4 | loop fusion | flops 8716288 | bytes 34865152 | tf_op jit(solution)/shard_map/concatenate | solution.py:71
  220.5 16.5 %gather_fusion = bf16[256,64,448]{2,1,0:T(8,128)(2,1)} fusion(bf16[304,64,448]{2,1,0:T(8,128)(2,1)} %pad_maximum_fusion, s32[1024]{0:T(1024)S(1)} %pad_clamp_fusion.2), kind=kCustom, calls=%fused_computation | custom fusion | bytes 29361152 | tf_op jit(solution)/shard_map/gather | solution.py:72
  237.0 12.9 %convert_bitcast_fusion = bf16[256,64,448]{2,1,0:T(8,128)(2,1)} fusion(bf16[256,64,64]{1,2,0:T(8,128)(2,1)} %copy.27, bf16[256,64,448]{2,1,0:T(8,128)(2,1)} %gather_fusion), kind=kOutput, calls=%fused_computation.5 | convolution fusion | flops 946864128 | bytes 31457280 | tf_op jit(solution)/shard_map/rba,rbx->rax/dot_general | solution.py:83
  249.9 23.6 %copy.28 = bf16[256,64,448]{0,2,1:T(8,128)(2,1)} copy(bf16[256,64,448]{2,1,0:T(8,128)(2,1)} %convert_bitcast_fusion) | data formatting | bytes 29360128 | tf_op jit(solution)/shard_map/convert_element_type | solution.py:85
  273.5 40.6 %copy.30 = bf16[256,64,7,64]{3,1,2,0:T(8,128)(2,1)} copy(bf16[256,64,7,64]{0,3,2,1:T(8,128)(2,1)} %bitcast.40) | data formatting | bytes 29360128 | tf_op jit(solution)/shard_map/reshape | solution.py:86
  314.1 38.2 %fusion.13 = f32[256,7,64,64]{3,2,1,0:T(8,128)} fusion(bf16[256,64,7,64]{3,1,2,0:T(8,128)(2,1)} %copy.30, bf16[256,7,64,64]{3,2,1,0:T(8,128)(2,1)} %reshape.82), kind=kOutput, calls=%fused_computation.58 | convolution fusion | flops 939524096 | bytes 58720256 | tf_op jit(solution)/shard_map/rakb,rkbc->rkac/dot_general | solution.py:88
  352.3 45.8 %copy.31 = f32[256,7,64,64]{0,3,2,1:T(8,128)} copy(f32[256,7,64,64]{3,2,1,0:T(8,128)} %fusion.13) | data formatting | bytes 58720256 | tf_op jit(solution)/shard_map/rakb,rkbc->rkac/dot_general | solution.py:88
  398.2 19.8 %convolution_bitcast_fusion = f32[224,4096]{1,0:T(8,128)S(1)} fusion(f32[256,7,4096]{0,2,1:T(8,128)} %bitcast.39, s32[256,7]{0,1:T(8,128)S(1)} %copy-done.5, pred[256,7]{0,1:T(8,128)(4,1)S(1)} %copy-done.6), kind=kOutput, calls=%fused_computation.6 | convolution fusion | flops 19730808832 | bytes 33039104 | tf_op jit(solution)/shard_map/rku,rkx->ux/dot_general | solution.py:95
  420.5 5.4 %collective-permute-start.13 = (f32[32,4096]{1,0:T(8,128)S(1)}, f32[32,4096]{1,0:T(8,128)}, u32[]{:S(2)}, u32[]{:S(2)}) collective-permute-start(f32[32,4096]{1,0:T(8,128)S(1)} %get-tuple-element.9), channel_id=1, source_target_pairs={{32,0},{33,1},{34,2},{35,3},{36,4},{37,5},{38,6},{39,7},{40,8},{41... | collective-permute-start | bytes 1572872 | tf_op jit(solution)/shard_map/ppermute | solution.py:47
  427.3 4.5 collective-permute-start.1
  433.8 6.0 %collective-permute-start.3 = (s32[32]{0:T(128)S(1)}, s32[32]{0:T(128)S(1)}, u32[]{:S(2)}, u32[]{:S(2)}) collective-permute-start(s32[32]{0:T(128)S(1)} %get-tuple-element.19), channel_id=1, source_target_pairs={{8,0},{9,1},{10,2},{11,3},{12,4},{13,5},{14,6},{15,7},{16,8},{17,9... | collective-permute-start | bytes 392 | tf_op jit(solution)/shard_map/ppermute | solution.py:47
  439.8 7.7 %collective-permute-start.4 = (s32[32]{0:T(128)S(1)}, s32[32]{0:T(128)S(1)}, u32[]{:S(2)}, u32[]{:S(2)}) collective-permute-start(s32[32]{0:T(128)S(1)} %get-tuple-element.24), channel_id=1, source_target_pairs={{0,1},{1,2},{2,3},{3,4},{4,5},{5,6},{6,7},{7,8},{8,9},{9,10},{10,1... | collective-permute-start | bytes 392 | tf_op jit(solution)/shard_map/ppermute | solution.py:47
  449.6 4.6 collective-permute-done.5
  456.3 6.0 %collective-permute-start.15 = (f32[32,4096]{1,0:T(8,128)S(1)}, f32[32,4096]{1,0:T(8,128)S(1)}, u32[]{:S(2)}, u32[]{:S(2)}) collective-permute-start(f32[32,4096]{1,0:T(8,128)S(1)} %get-tuple-element.7), channel_id=1, source_target_pairs={{8,0},{9,1},{10,2},{11,3},{12,4},{13,5},{14,6},{15,7},{16,8},{17,9... | collective-permute-start | bytes 1572872 | tf_op jit(solution)/shard_map/ppermute | solution.py:47
  462.3 3.7 collective-permute-start.16
  466.0 6.8 %collective-permute-start.17 = (f32[32,4096]{1,0:T(8,128)S(1)}, f32[32,4096]{1,0:T(8,128)S(1)}, u32[]{:S(2)}, u32[]{:S(2)}) collective-permute-start(f32[32,4096]{1,0:T(8,128)S(1)} %get-tuple-element.5), channel_id=1, source_target_pairs={{1,0},{2,1},{3,2},{4,3},{5,4},{6,5},{7,6},{8,7},{9,8},{10,9},{11,1... | collective-permute-start | bytes 1572872 | tf_op jit(solution)/shard_map/ppermute | solution.py:47
  478.2 6.9 %collective-permute-done.16 = f32[32,4096]{1,0:T(8,128)S(1)} collective-permute-done((f32[32,4096]{1,0:T(8,128)S(1)}, f32[32,4096]{1,0:T(8,128)S(1)}, u32[]{:S(2)}, u32[]{:S(2)}) %collective-permute-start.16) | collective-permute-done | bytes 524320 | tf_op jit(solution)/shard_map/ppermute | solution.py:47
  486.8 4.6 fusion.4
  (80 shorter events, 39.3 us)
Async XLA Ops:
  10.2 22.9 %copy-start.4 = (s32[256]{0:T(256)S(1)}, s32[256]{0:T(256)}, u32[]{:S(2)}) copy-start(s32[256]{0:T(256)} %param.10) | copy-start | bytes 3076
  11.9 100.5 %collective-permute-start.6 = (bf16[64,4096]{1,0:T(8,128)(2,1)}, bf16[64,4096]{1,0:T(8,128)(2,1)}, u32[]{:S(2)}, u32[]{:S(2)}) collective-permute-start(bf16[64,4096]{1,0:T(8,128)(2,1)} %get-tuple-element.17), channel_id=1, source_target_pairs={{32,0},{33,1},{34,2},{35,3},{36,4},{37,5},{38,6},{39,7},{40,8},{41... | collective-permute-start | bytes 1572872 | tf_op jit(solution)/shard_map/ppermute | solution.py:47
  15.3 101.2 %collective-permute-start.7 = (bf16[64,4096]{1,0:T(8,128)(2,1)}, bf16[64,4096]{1,0:T(8,128)(2,1)}, u32[]{:S(2)}, u32[]{:S(2)}) collective-permute-start(bf16[64,4096]{1,0:T(8,128)(2,1)} %get-tuple-element.16), channel_id=1, source_target_pairs={{0,32},{1,33},{2,34},{3,35},{4,36},{5,37},{6,38},{7,39},{8,40},{9,... | collective-permute-start | bytes 1572872 | tf_op jit(solution)/shard_map/ppermute | solution.py:47
  16.6 101.8 %collective-permute-start.8 = (bf16[64,4096]{1,0:T(8,128)(2,1)}, bf16[64,4096]{1,0:T(8,128)(2,1)}, u32[]{:S(2)}, u32[]{:S(2)}) collective-permute-start(bf16[64,4096]{1,0:T(8,128)(2,1)} %get-tuple-element.15), channel_id=1, source_target_pairs={{8,0},{9,1},{10,2},{11,3},{12,4},{13,5},{14,6},{15,7},{16,8},{17,9... | collective-permute-start | bytes 1572872 | tf_op jit(solution)/shard_map/ppermute | solution.py:47
  23.4 96.9 %collective-permute-start.9 = (bf16[64,4096]{1,0:T(8,128)(2,1)}, bf16[64,4096]{1,0:T(8,128)(2,1)}, u32[]{:S(2)}, u32[]{:S(2)}) collective-permute-start(bf16[64,4096]{1,0:T(8,128)(2,1)} %get-tuple-element.14), channel_id=1, source_target_pairs={{0,8},{1,9},{2,10},{3,11},{4,12},{5,13},{6,14},{7,15},{8,16},{9,17... | collective-permute-start | bytes 1572872 | tf_op jit(solution)/shard_map/ppermute | solution.py:47
  25.3 96.8 %collective-permute-start.10 = (bf16[64,4096]{1,0:T(8,128)(2,1)}, bf16[64,4096]{1,0:T(8,128)(2,1)}, u32[]{:S(2)}, u32[]{:S(2)}) collective-permute-start(bf16[64,4096]{1,0:T(8,128)(2,1)} %get-tuple-element.13), channel_id=1, source_target_pairs={{1,0},{2,1},{3,2},{4,3},{5,4},{6,5},{7,6},{8,7},{9,8},{10,9},{11,1... | collective-permute-start | bytes 1572872 | tf_op jit(solution)/shard_map/ppermute | solution.py:47
  91.7 6.9 %copy-start = (bf16[256,4096]{1,0:T(8,128)(2,1)S(1)}, bf16[256,4096]{1,0:T(8,128)(2,1)}, u32[]{:S(2)}) copy-start(bf16[256,4096]{1,0:T(8,128)(2,1)} %param.9) | copy-start | bytes 6291460
  93.8 7.3 %copy-start.2 = (s32[256,7]{0,1:T(8,128)S(1)}, s32[256,7]{0,1:T(8,128)}, u32[]{:S(2)}) copy-start(s32[256,7]{0,1:T(8,128)} %param.12) | copy-start | bytes 21508
  93.8 8.2 %copy-start.7 = (s32[256]{0:T(256)S(1)}, s32[256]{0:T(256)}, u32[]{:S(2)}) copy-start(s32[256]{0:T(256)} %param.11) | copy-start | bytes 3076
  93.8 107.3 %all-to-all-start.1 = ((bf16[4,2,6,64,448]{4,3,2,1,0:T(8,128)(2,1)}), bf16[4,2,6,64,448]{4,3,2,1,0:T(8,128)(2,1)}, u32[]{:S(2)}, u32[]{:S(2)}) async-start(bf16[4,2,6,64,448]{4,3,2,1,0:T(8,128)(2,1)} %copy.24), calls=%async_computation.1 | async-start | bytes 6291456 | tf_op jit(solution)/shard_map/all_to_all | solution.py:34
  102.0 10.4 %copy-start.1 = (bf16[64,4096]{1,0:T(8,128)(2,1)S(1)}, bf16[64,4096]{1,0:T(8,128)(2,1)}, u32[]{:S(2)}) copy-start(bf16[64,4096]{1,0:T(8,128)(2,1)} %get-tuple-element.12) | copy-start | bytes 1572868
  112.4 18.9 %collective-permute-start.11 = (bf16[64,4096]{1,0:T(8,128)(2,1)S(1)}, bf16[64,4096]{1,0:T(8,128)(2,1)S(1)}, u32[]{:S(2)}, u32[]{:S(2)}) collective-permute-start(bf16[64,4096]{1,0:T(8,128)(2,1)S(1)} %copy-done.1), channel_id=1, source_target_pairs={{0,1},{1,2},{2,3},{3,4},{4,5},{5,6},{6,7},{7,8},{8,9},{9,10},{10,1... | collective-permute-start | bytes 1572872 | tf_op jit(solution)/shard_map/ppermute | solution.py:47
  352.3 45.8 %copy-start.5 = (s32[256,7]{0,1:T(8,128)S(1)}, s32[256,7]{0,1:T(8,128)}, u32[]{:S(2)}) copy-start(s32[256,7]{0,1:T(8,128)} %param.13) | copy-start | bytes 21508
  352.3 45.8 %copy-start.6 = (pred[256,7]{0,1:T(8,128)(4,1)S(1)}, pred[256,7]{0,1:T(8,128)(4,1)}, u32[]{:S(2)}) copy-start(pred[256,7]{0,1:T(8,128)(4,1)} %broadcast_compare_fusion) | copy-start | bytes 5380
  418.0 8.0 %copy-start.3 = (s32[1,224]{1,0:T(1,128)S(1)}, s32[1,224]{1,0:T(1,128)}, u32[]{:S(2)}) copy-start(s32[1,224]{1,0:T(1,128)} %param.15) | copy-start | bytes 2692
  419.3 46.7 %collective-permute-start.12 = (f32[32,4096]{1,0:T(8,128)}, f32[32,4096]{1,0:T(8,128)}, u32[]{:S(2)}, u32[]{:S(2)}) collective-permute-start(f32[32,4096]{1,0:T(8,128)} %get-tuple-element.10), channel_id=1, source_target_pairs={{0,32},{1,33},{2,34},{3,35},{4,36},{5,37},{6,38},{7,39},{8,40},{9,... | collective-permute-start | bytes 1572872 | tf_op jit(solution)/shard_map/ppermute | solution.py:47
  420.5 54.1 %collective-permute-start.13 = (f32[32,4096]{1,0:T(8,128)S(1)}, f32[32,4096]{1,0:T(8,128)}, u32[]{:S(2)}, u32[]{:S(2)}) collective-permute-start(f32[32,4096]{1,0:T(8,128)S(1)} %get-tuple-element.9), channel_id=1, source_target_pairs={{32,0},{33,1},{34,2},{35,3},{36,4},{37,5},{38,6},{39,7},{40,8},{41... | collective-permute-start | bytes 1572872 | tf_op jit(solution)/shard_map/ppermute | solution.py:47
  426.0 7.8 %collective-permute-start = (s32[32]{0:T(128)S(1)}, s32[32]{0:T(128)S(1)}, u32[]{:S(2)}, u32[]{:S(2)}) collective-permute-start(s32[32]{0:T(128)S(1)} %get-tuple-element.22), channel_id=1, source_target_pairs={{0,32},{1,33},{2,34},{3,35},{4,36},{5,37},{6,38},{7,39},{8,40},{9,... | collective-permute-start | bytes 392 | tf_op jit(solution)/shard_map/ppermute | solution.py:47
  427.3 12.5 %collective-permute-start.1 = (s32[32]{0:T(128)S(1)}, s32[32]{0:T(128)S(1)}, u32[]{:S(2)}, u32[]{:S(2)}) collective-permute-start(s32[32]{0:T(128)S(1)} %get-tuple-element.21), channel_id=1, source_target_pairs={{32,0},{33,1},{34,2},{35,3},{36,4},{37,5},{38,6},{39,7},{40,8},{41... | collective-permute-start | bytes 392 | tf_op jit(solution)/shard_map/ppermute | solution.py:47
  431.8 15.7 %collective-permute-start.2 = (s32[32]{0:T(128)S(1)}, s32[32]{0:T(128)S(1)}, u32[]{:S(2)}, u32[]{:S(2)}) collective-permute-start(s32[32]{0:T(128)S(1)} %get-tuple-element.20), channel_id=1, source_target_pairs={{0,8},{1,9},{2,10},{3,11},{4,12},{5,13},{6,14},{7,15},{8,16},{9,17... | collective-permute-start | bytes 392 | tf_op jit(solution)/shard_map/ppermute | solution.py:47
  433.8 15.9 %collective-permute-start.3 = (s32[32]{0:T(128)S(1)}, s32[32]{0:T(128)S(1)}, u32[]{:S(2)}, u32[]{:S(2)}) collective-permute-start(s32[32]{0:T(128)S(1)} %get-tuple-element.19), channel_id=1, source_target_pairs={{8,0},{9,1},{10,2},{11,3},{12,4},{13,5},{14,6},{15,7},{16,8},{17,9... | collective-permute-start | bytes 392 | tf_op jit(solution)/shard_map/ppermute | solution.py:47
  439.8 9.8 %collective-permute-start.4 = (s32[32]{0:T(128)S(1)}, s32[32]{0:T(128)S(1)}, u32[]{:S(2)}, u32[]{:S(2)}) collective-permute-start(s32[32]{0:T(128)S(1)} %get-tuple-element.24), channel_id=1, source_target_pairs={{0,1},{1,2},{2,3},{3,4},{4,5},{5,6},{6,7},{7,8},{8,9},{9,10},{10,1... | collective-permute-start | bytes 392 | tf_op jit(solution)/shard_map/ppermute | solution.py:47
  447.5 6.7 %collective-permute-start.5 = (s32[32]{0:T(128)S(1)}, s32[32]{0:T(128)S(1)}, u32[]{:S(2)}, u32[]{:S(2)}) collective-permute-start(s32[32]{0:T(128)S(1)} %get-tuple-element.18), channel_id=1, source_target_pairs={{1,0},{2,1},{3,2},{4,3},{5,4},{6,5},{7,6},{8,7},{9,8},{10,9},{11,1... | collective-permute-start | bytes 392 | tf_op jit(solution)/shard_map/ppermute | solution.py:47
  454.3 22.2 %collective-permute-start.14 = (f32[32,4096]{1,0:T(8,128)S(1)}, f32[32,4096]{1,0:T(8,128)S(1)}, u32[]{:S(2)}, u32[]{:S(2)}) collective-permute-start(f32[32,4096]{1,0:T(8,128)S(1)} %get-tuple-element.8), channel_id=1, source_target_pairs={{0,8},{1,9},{2,10},{3,11},{4,12},{5,13},{6,14},{7,15},{8,16},{9,17... | collective-permute-start | bytes 1572872 | tf_op jit(solution)/shard_map/ppermute | solution.py:47
  456.3 21.1 %collective-permute-start.15 = (f32[32,4096]{1,0:T(8,128)S(1)}, f32[32,4096]{1,0:T(8,128)S(1)}, u32[]{:S(2)}, u32[]{:S(2)}) collective-permute-start(f32[32,4096]{1,0:T(8,128)S(1)} %get-tuple-element.7), channel_id=1, source_target_pairs={{8,0},{9,1},{10,2},{11,3},{12,4},{13,5},{14,6},{15,7},{16,8},{17,9... | collective-permute-start | bytes 1572872 | tf_op jit(solution)/shard_map/ppermute | solution.py:47
  462.3 22.8 %collective-permute-start.16 = (f32[32,4096]{1,0:T(8,128)S(1)}, f32[32,4096]{1,0:T(8,128)S(1)}, u32[]{:S(2)}, u32[]{:S(2)}) collective-permute-start(f32[32,4096]{1,0:T(8,128)S(1)} %get-tuple-element.6), channel_id=1, source_target_pairs={{0,1},{1,2},{2,3},{3,4},{4,5},{5,6},{6,7},{7,8},{8,9},{9,10},{10,1... | collective-permute-start | bytes 1572872 | tf_op jit(solution)/shard_map/ppermute | solution.py:47
  466.0 19.9 %collective-permute-start.17 = (f32[32,4096]{1,0:T(8,128)S(1)}, f32[32,4096]{1,0:T(8,128)S(1)}, u32[]{:S(2)}, u32[]{:S(2)}) collective-permute-start(f32[32,4096]{1,0:T(8,128)S(1)} %get-tuple-element.5), channel_id=1, source_target_pairs={{1,0},{2,1},{3,2},{4,3},{5,4},{6,5},{7,6},{8,7},{9,8},{10,9},{11,1... | collective-permute-start | bytes 1572872 | tf_op jit(solution)/shard_map/ppermute | solution.py:47
where the time goes:
time: 497 us; the launch traced here: 491 us
  local copies, waits for them, and re-layouts  292 us (59%)
  starting transfers between devices  76.8 us (15%)
  matrix products  75.5 us (15%)
  other arithmetic  21.5 us (4%)
  waiting for transfers between devices  18.8 us (4%)
  blocking collectives  6.26 us (1%)
    ppermute x18, starting transfers between devices, shifted(): return lax.ppermute(value, axis, pairs)  72 us
    dot_general x1, local copies, waits for them, and re-layouts, shards(): jnp.einsum('rakb,rkbc->rkac', left, neighbour, preferred_element_type=jnp...  45.8 us
    unnamed x29, local copies, waits for them, and re-layouts  42.9 us
    reshape x1, local copies, waits for them, and re-layouts, shards(): left = left.reshape(row_count, block_side, NBR, block_side)  40.6 us
    reshape x1, local copies, waits for them, and re-layouts, shards(): block_table[jnp.maximum(columns, 0)]  40.3 us
    dot_general x1, matrix products, shards(): jnp.einsum('rakb,rkbc->rkac', left, neighbour, preferred_element_type=jnp...  38.2 us
    gather x1, local copies, waits for them, and re-layouts, shards(): block_table[jnp.maximum(columns, 0)]  28.6 us
    scatter x1, local copies, waits for them, and re-layouts, shards(): jnp.zeros((layers * CAP + 1,) + row_shape, jnp.bfloat16).at[slot_key]  26.9 us
  transfers between devices with their start and end apart: 19, of which 3 were waited for; matrix products, arithmetic and copies ran while one was open for 31% of the time, Pallas kernels for 0%

commit v1 on v0

v1 whole, which is shorter than its diff:
```python
import functools

import jax
import jax.numpy as jnp
from jax import lax
from jax.experimental import pallas as pl
from jax.experimental.pallas import tpu as pltpu
from jax.sharding import PartitionSpec as P

B = 64
NBR = 7
CAP = 6
FAR = 2
NEAR = CAP - FAR
GCAP = 64
UCAP = 32
U_DEV = 224
CE_DEV = 64
ROWS = 256
LAYERS = 8
HALF = 32
LANES = 128
AXES = ("gx", "gy", "gz")
SENT = LAYERS * FAR + 2 * NEAR
SENT_PAD = 32
ROW_LEN = 3 * B + HALF
GHOST_LEN = GCAP * HALF
EXTRA = 16
TABLE = ROWS + 6 * GCAP
VMEM_LIMIT = 62 * 1024 * 1024
bf16 = jnp.bfloat16
f32 = jnp.float32


def lower_lanes(shape):
    return lax.broadcasted_iota(jnp.int32, shape, len(shape) - 1) < B


def swap_lanes(v):
    return jnp.concatenate([v[:, B:], v[:, :B]], axis=1)


def shifted(value, axis, by):
    devices = lax.axis_size(axis)
    pairs = [(i, i + by) for i in range(devices) if 0 <= i + by < devices]
    return lax.ppermute(value, axis, pairs)


def pack_kernel(lists, prolong, extra, halves, *rest):
    sends, work = rest[:6], rest[6]
    low = lower_lanes((16, LANES))

    def group(g, carry):
        rows = pl.ds(pl.multiple_of(g * 16, 16), 16)
        for s in range(16):
            near = prolong[rows, s * LANES : (s + 1) * LANES].astype(f32)
            far = prolong[rows, (s + 16) * LANES : (s + 17) * LANES].astype(f32)
            even = jnp.where(low, near, pltpu.roll(far, B, 1))
            odd = jnp.where(low, pltpu.roll(near, B, 1), far)
            work[pl.ds(2 * s, 16, stride=HALF), :] = even
            work[pl.ds(2 * s + 1, 16, stride=HALF), :] = odd
        for e in range(16):
            halves[pl.ds(pl.multiple_of((g * 16 + e) * HALF, HALF), HALF), :] = work[
                e * HALF : (e + 1) * HALF, :
            ].astype(bf16)
        return carry

    lax.fori_loop(0, ROWS // 16, group, 0)

    def pick(q, carry):
        for j in range(6):
            row = lists[j, q]
            sends[j][pl.ds(pl.multiple_of(q * HALF, HALF), HALF), :] = halves[
                pl.ds(pl.multiple_of(row * HALF, HALF), HALF), :
            ]
        return carry

    lax.fori_loop(0, GCAP, pick, 0, unroll=4)
    for j in range(6):
        sends[j][GHOST_LEN:, :] = extra[...]


def pack(lists, prolong, extra):
    return pl.pallas_call(
        pack_kernel,
        grid_spec=pltpu.PrefetchScalarGridSpec(
            num_scalar_prefetch=1,
            grid=(1,),
            in_specs=[
                pl.BlockSpec((ROWS, B * B), lambda i, s: (0, 0)),
                pl.BlockSpec((EXTRA, LANES), lambda i, s: (0, 0)),
            ],
            out_specs=[pl.BlockSpec((ROWS * HALF, LANES), lambda i, s: (0, 0))]
            + [pl.BlockSpec((GHOST_LEN + EXTRA, LANES), lambda i, s: (0, 0))] * 6,
            scratch_shapes=[pltpu.VMEM((16 * HALF, LANES), f32)],
        ),
        out_shape=[jax.ShapeDtypeStruct((ROWS * HALF, LANES), bf16)]
        + [jax.ShapeDtypeStruct((GHOST_LEN + EXTRA, LANES), bf16)] * 6,
        compiler_params=pltpu.CompilerParams(vmem_limit_bytes=VMEM_LIMIT),
        name="pack",
    )(lists, prolong, extra)


def to_halves(chunk):
    top, bottom = chunk[:HALF, :], chunk[HALF:, :]
    first = jnp.concatenate([top[:, :B], bottom[:, :B]], axis=1)
    second = jnp.concatenate([top[:, B:], bottom[:, B:]], axis=1)
    return first, second


def left_kernel(picks, blocks, halves, left, far, up, down, table, transposed):
    j = pl.program_id(0)
    total = ROWS + SENT_PAD
    eye = (
        lax.broadcasted_iota(jnp.int32, (B, B), 0) == lax.broadcasted_iota(jnp.int32, (B, B), 1)
    ).astype(bf16)

    @pl.when(j == 0)
    def _():
        def turn(i, carry):
            h = halves[pl.ds(pl.multiple_of(i * HALF, HALF), HALF), :]
            block = jnp.concatenate([h[:, :B], h[:, B:]], axis=0)
            transposed[i] = lax.dot_general(
                eye, block, (((1,), (1,)), ((), ())), preferred_element_type=f32
            ).astype(bf16)
            return carry

        lax.fori_loop(0, ROWS, turn, 0, unroll=8)

    def relay(a, carry):
        table[pl.ds(pl.multiple_of(a * total, 8), total), :] = lax.dot_general(
            picks[...], blocks[a], (((1,), (1,)), ((), ())), preferred_element_type=f32
        )
        return carry

    lax.fori_loop(0, B, relay, 0, unroll=2)

    def multiply(i, carry):
        rows = table[pl.ds(i, B, stride=total), :].astype(bf16)
        chunk = jnp.dot(transposed[i], rows, preferred_element_type=f32).astype(bf16)
        first, second = to_halves(chunk)
        left[0, i] = first
        left[1, i] = second
        return carry

    lax.fori_loop(0, ROWS, multiply, 0, unroll=8)

    def sent(r):
        return table[pl.ds(ROWS + r, B, stride=total), :].astype(bf16)

    for r in range(SENT):
        if r < LAYERS * FAR:
            out, base = far.at[r // FAR], (r % FAR) * ROW_LEN
        elif r < LAYERS * FAR + NEAR:
            out, base = up, (r - LAYERS * FAR) * ROW_LEN
        else:
            out, base = down, (r - LAYERS * FAR - NEAR) * ROW_LEN

        @pl.when(j < 3)
        def _():
            out[pl.ds(pl.multiple_of(base + j * B, HALF), B), :] = sent(r)

        @pl.when(j == 3)
        def _():
            out[base + 3 * B : base + ROW_LEN, :] = to_halves(sent(r))[0]


def make_left(picks, blocks, halves):
    whole = lambda shape: pl.BlockSpec(shape, lambda j: (0,) * len(shape))
    return pl.pallas_call(
        left_kernel,
        grid=(4,),
        in_specs=[
            whole((ROWS + SENT_PAD, ROWS)),
            pl.BlockSpec((B, LANES, ROWS), lambda j: (0, j, 0)),
            whole((ROWS * HALF, LANES)),
        ],
        out_specs=[
            pl.BlockSpec((2, ROWS, HALF, LANES), lambda j: (j, 0, 0, 0)),
            whole((LAYERS, FAR * ROW_LEN, LANES)),
            whole((NEAR * ROW_LEN, LANES)),
            whole((NEAR * ROW_LEN, LANES)),
        ],
        out_shape=[
            jax.ShapeDtypeStruct((NBR + 1, ROWS, HALF, LANES), bf16),
            jax.ShapeDtypeStruct((LAYERS, FAR * ROW_LEN, LANES), bf16),
            jax.ShapeDtypeStruct((NEAR * ROW_LEN, LANES), bf16),
            jax.ShapeDtypeStruct((NEAR * ROW_LEN, LANES), bf16),
        ],
        scratch_shapes=[
            pltpu.VMEM((B * (ROWS + SENT_PAD), LANES), f32),
            pltpu.VMEM((ROWS, B, B), bf16),
        ],
        compiler_params=pltpu.CompilerParams(
            vmem_limit_bytes=VMEM_LIMIT, dimension_semantics=("arbitrary",)
        ),
        name="left",
    )(picks, blocks, halves)


PARTS = 8


def sums_kernel(
    arrival, place, left_hbm, halves, g0, g1, g2, g3, g4, g5, far, up, down,
    own, s0, s1, s2, s3, s4, s5,
    left, packed, diagonal, even, odd, moved, left_sem, table_sem, moved_sem,
):
    ghosts = (g0, g1, g2, g3, g4, g5)
    sends = (s0, s1, s2, s3, s4, s5)
    layer = place[NBR, 0]
    part = ROWS // PARTS
    table_copies = [pltpu.make_async_copy(halves, packed.at[: ROWS * HALF, :], table_sem.at[0])]
    for j in range(6):
        first = (ROWS + j * GCAP) * HALF
        table_copies.append(
            pltpu.make_async_copy(
                ghosts[j].at[:GHOST_LEN, :],
                packed.at[first : first + GHOST_LEN, :],
                table_sem.at[1 + j],
            )
        )
    moved_copies = [
        pltpu.make_async_copy(far, moved.at[: LAYERS * FAR * ROW_LEN, :], moved_sem.at[0]),
        pltpu.make_async_copy(
            up,
            moved.at[LAYERS * FAR * ROW_LEN : (LAYERS * FAR + NEAR) * ROW_LEN, :],
            moved_sem.at[1],
        ),
        pltpu.make_async_copy(
            down, moved.at[(LAYERS * FAR + NEAR) * ROW_LEN :, :], moved_sem.at[2]
        ),
    ]
    left_copies = [
        pltpu.make_async_copy(
            left_hbm.at[:NBR, pl.ds(n * part, part)],
            left.at[:, pl.ds(n * part, part)],
            left_sem.at[n],
        )
        for n in range(PARTS)
    ]
    for copy in table_copies + moved_copies + left_copies:
        copy.start()

    def clear(u, carry):
        even[u] = jnp.zeros((HALF, LANES), f32)
        odd[u] = jnp.zeros((HALF, LANES), f32)
        return carry

    lax.fori_loop(0, U_DEV + 1, clear, 0, unroll=5)

    low = lower_lanes((HALF, LANES)).astype(f32).astype(bf16)
    high = (1 - lower_lanes((HALF, LANES)).astype(jnp.int32)).astype(f32).astype(bf16)

    def expand(c, carry):
        h = packed[pl.ds(pl.multiple_of(c * HALF, HALF), HALF), :]
        turned = swap_lanes(h)
        diagonal[c, 0:HALF, :] = h * low
        diagonal[c, HALF:B, :] = turned * low
        diagonal[c, B : B + HALF, :] = turned * high
        diagonal[c, B + HALF :, :] = h * high
        return carry

    table_copies[0].wait()
    lax.fori_loop(0, ROWS, expand, 0, unroll=4)
    for j in range(6):
        table_copies[1 + j].wait()
    lax.fori_loop(ROWS, TABLE, expand, 0, unroll=4)
    for copy in moved_copies + left_copies:
        copy.wait()

    def arrive(i, carry):
        code = arrival[i]

        @pl.when(code >= ROWS)
        def _():
            source = (code - ROWS) // CAP
            rank = (code - ROWS) % CAP
            near = jnp.where(source < layer, LAYERS * FAR, LAYERS * FAR + NEAR) + rank - FAR
            slot = jnp.where(rank < FAR, source * FAR + rank, near)
            base = pl.multiple_of(slot * ROW_LEN, HALF)
            block = diagonal[i, 0:B, 0:B]
            for j in range(4):
                if j < 3:
                    rows = moved[pl.ds(base + j * B, B), :]
                else:
                    h = moved[pl.ds(base + 3 * B, HALF), :]
                    rows = jnp.concatenate([h, swap_lanes(h)], axis=0)
                chunk = lax.dot_general(
                    block, rows, (((0,), (0,)), ((), ())), preferred_element_type=f32
                ).astype(bf16)
                first, second = to_halves(chunk)
                left[2 * j, i] = first
                if j < 3:
                    left[2 * j + 1, i] = second

        return carry

    lax.fori_loop(0, ROWS, arrive, 0)

    def products(n, carry):
        for r in range(4):
            i = n * 4 + r
            for k in range(NBR):
                code = place[k, i]
                u, c = code % 256, code // 256
                total = even if (k + r * NBR) % 2 == 0 else odd
                total[u] += jnp.dot(left[k, i], diagonal[c], preferred_element_type=f32)
        return carry

    lax.fori_loop(0, ROWS // 4, products, 0)
    own[...] = even[:UCAP] + odd[:UCAP]
    for j in range(6):
        first = (j + 1) * UCAP
        sends[j][...] = (even[first : first + UCAP] + odd[first : first + UCAP]).astype(bf16)


def make_sums(arrival, place, left, halves, ghosts, far, up, down):
    hbm = pl.BlockSpec(memory_space=pl.ANY)
    block = pl.BlockSpec((UCAP, HALF, LANES), lambda i, *s: (0, 0, 0))
    return pl.pallas_call(
        sums_kernel,
        grid_spec=pltpu.PrefetchScalarGridSpec(
            num_scalar_prefetch=2,
            grid=(1,),
            in_specs=[hbm] * 11,
            out_specs=[block] * 7,
            scratch_shapes=[
                pltpu.VMEM((NBR, ROWS, HALF, LANES), bf16),
                pltpu.VMEM((TABLE * HALF, LANES), bf16),
                pltpu.VMEM((TABLE, LANES, LANES), bf16),
                pltpu.VMEM((U_DEV + 1, HALF, LANES), f32),
                pltpu.VMEM((U_DEV + 1, HALF, LANES), f32),
                pltpu.VMEM((SENT * ROW_LEN, LANES), bf16),
                pltpu.SemaphoreType.DMA((PARTS,)),
                pltpu.SemaphoreType.DMA((7,)),
                pltpu.SemaphoreType.DMA((3,)),
            ],
        ),
        out_shape=[jax.ShapeDtypeStruct((UCAP, HALF, LANES), f32)]
        + [jax.ShapeDtypeStruct((UCAP, HALF, LANES), bf16)] * 6,
        compiler_params=pltpu.CompilerParams(vmem_limit_bytes=VMEM_LIMIT),
        name="sums",
    )(arrival, place, left, halves, *ghosts, far, up, down)


def final_kernel(numbers, own, r0, r1, r2, r3, r4, r5, out, total):
    parts = (own, r0, r1, r2, r3, r4, r5)
    total[...] = jnp.zeros_like(total)

    def add(q, carry):
        for v in range(7):
            rows = pl.ds(pl.multiple_of(numbers[v, q] * HALF, HALF), HALF)
            total[rows, :] += parts[v][q].astype(f32)
        return carry

    lax.fori_loop(0, UCAP, add, 0, unroll=2)
    low = lower_lanes((8, LANES))

    for g in range(CE_DEV // 8):
        for s in range(16):
            a = total[pl.ds(g * 8 * HALF + 2 * s, 8, stride=HALF), :]
            b = total[pl.ds(g * 8 * HALF + 2 * s + 1, 8, stride=HALF), :]
            out[g * 8 : g * 8 + 8, s * LANES : (s + 1) * LANES] = jnp.where(
                low, a, pltpu.roll(b, B, 1)
            )
            out[g * 8 : g * 8 + 8, (s + 16) * LANES : (s + 17) * LANES] = jnp.where(
                low, pltpu.roll(a, B, 1), b
            )


def make_final(numbers, parts):
    block = pl.BlockSpec((UCAP, HALF, LANES), lambda i, *s: (0, 0, 0))
    return pl.pallas_call(
        final_kernel,
        grid_spec=pltpu.PrefetchScalarGridSpec(
            num_scalar_prefetch=1,
            grid=(1,),
            in_specs=[block] * 7,
            out_specs=pl.BlockSpec((CE_DEV, B * B), lambda i, *s: (0, 0)),
            scratch_shapes=[pltpu.VMEM((CE_DEV * HALF, LANES), f32)],
        ),
        out_shape=jax.ShapeDtypeStruct((CE_DEV, B * B), f32),
        compiler_params=pltpu.CompilerParams(vmem_limit_bytes=VMEM_LIMIT),
        name="final",
    )(numbers, *parts)


def neighbour_shift(value, facing):
    axis = AXES[facing // 2]
    return shifted(value, axis, 1 - 2 * (facing % 2))


def shards(blocks, prolong, new_owner, arrival, columns, targets, ghost_lists, touched):
    own_layer = lax.axis_index("gz")
    touched_here = touched[0]

    extra = jnp.pad(touched_here, (0, EXTRA * LANES - U_DEV)).reshape(EXTRA, LANES).astype(bf16)
    halves, *outbound = pack(ghost_lists[0], prolong, extra)
    ghosts = [neighbour_shift(outbound[facing ^ 1], facing ^ 1) for facing in range(6)]

    peer = new_owner % LAYERS
    labels = jnp.arange(LAYERS, dtype=jnp.int32)
    onehot = peer[:, None] == labels[None, :]
    earlier = jnp.arange(ROWS)[None, :] < jnp.arange(ROWS)[:, None]
    same = peer[:, None] == peer[None, :]
    rank = jnp.sum((earlier & same).astype(jnp.int32), axis=1)
    near = jnp.where(peer > own_layer, LAYERS * FAR, LAYERS * FAR + NEAR) + rank - FAR
    slot = jnp.where(rank < FAR, peer * FAR + rank, near)
    slot = jnp.where(peer == own_layer, -1, slot)
    old = jnp.arange(ROWS, dtype=jnp.int32)
    picks = jnp.concatenate(
        [
            arrival[:, None] == old[None, :],
            jnp.arange(SENT_PAD, dtype=jnp.int32)[:, None] == slot[None, :],
        ],
        axis=0,
    ).astype(bf16)

    left, far, up, down = make_left(picks, jnp.transpose(blocks, (1, 2, 0)), halves)
    far_in = lax.all_to_all(far, "gz", split_axis=0, concat_axis=0, tiled=True)
    up_in = shifted(up, "gz", 1)
    down_in = shifted(down, "gz", -1)

    cols = columns.T
    place = jnp.where(cols >= 0, cols * 256 + targets.T, U_DEV)
    place = jnp.concatenate([place, jnp.full((1, ROWS), own_layer, jnp.int32)], axis=0)
    own, *sends = make_sums(
        arrival, place, left, halves, ghosts,
        far_in.reshape(LAYERS * FAR * ROW_LEN, LANES), up_in, down_in,
    )
    got = [neighbour_shift(sends[facing], facing) for facing in range(6)]

    numbers = [touched_here[:UCAP]]
    for facing in range(6):
        flat = ghosts[facing ^ 1][GHOST_LEN : GHOST_LEN + 2].reshape(-1)
        first = (facing + 1) * UCAP
        numbers.append(flat[first : first + UCAP].astype(jnp.int32))
    return make_final(jnp.stack(numbers), [own] + got)


def solution(mesh):
    return jax.shard_map(
        shards,
        mesh=mesh,
        in_specs=(
            P(AXES, None, None),
            P(AXES, None),
            P(AXES),
            P(AXES),
            P(AXES, None),
            P(AXES, None),
            P(AXES, None, None),
            P(AXES, None),
        ),
        out_specs=P(AXES, None),
        check_vma=False,
    )
```

time: 497 us -> 241 us (0.48)
  the two profiles are of different devices: /device:TPU:24 before, /device:TPU:34 now
where the time goes in v1:
time: 241 us; the launch traced here: 239 us
  Pallas kernels  158 us (66%)
  starting transfers between devices  44.1 us (18%)
  waiting for transfers between devices  26.7 us (11%)
  local copies, waits for them, and re-layouts  6.23 us (3%)
  other arithmetic  4.15 us (2%)
    pallas_call x1, Pallas kernels, make_left(): pl.pallas_call(left_kernel, grid=(4,), in_specs=[whole((ROWS + SENT_PAD,...  93.2 us
    pallas_call x1, Pallas kernels, make_sums(): pl.pallas_call(sums_kernel, grid_spec=pltpu.PrefetchScalarGridSpec(num_sc...  50.2 us
    ppermute x14, starting transfers between devices, shifted(): return lax.ppermute(value, axis, pairs)  38.7 us
    ppermute x14, waiting for transfers between devices, shifted(): return lax.ppermute(value, axis, pairs)  26.7 us
    pallas_call x1, Pallas kernels, pack(): pl.pallas_call(pack_kernel, grid_spec=pltpu.PrefetchScalarGridSpec(num_sc...  9.65 us
    all_to_all x1, starting transfers between devices, shards(): far_in = lax.all_to_all(far, 'gz', split_axis=0, concat_axis=0, tiled=True)  5.43 us
    pallas_call x1, Pallas kernels, make_final(): pl.pallas_call(final_kernel, grid_spec=pltpu.PrefetchScalarGridSpec(num_s...  4.95 us
  transfers between devices with their start and end apart: 15, of which 5 were waited for; matrix products, arithmetic and copies ran while one was open for 2% of the time, Pallas kernels for 39%

profile of v1, /device:TPU:34, one launch (start us, length us, event | category | flops | bytes accessed | tf_op | source)
XLA Modules:
  0.0 239.5 jit_solution(9091221953519903021)
XLA Ops:
  0.0 0.7 convert_reduce_fusion.1
  1.3 1.3 copy.11
  2.6 9.6 %pack.1 = (bf16[8192,128]{1,0:T(8,128)(2,1)}, bf16[2064,128]{1,0:T(8,128)(2,1)}, bf16[2064,128]{1,0:T(8,128)(2,1)}, bf16[2064,128]{1,0:T(8,128)(2,1)}, bf16[2064...) custom-call(s32[6,64]{1,0:T(8,128)} %bitcast.41, bf16[256,4096]{1,0:T(8,128)(2,1)} %prolong.1, ...), custom_call_target="tpu_custom_call" | custom-call | tf_op jit(solution)/shard_map/pack/pallas_call | solution.py:84
  12.2 1.9 collective-permute-start.4
  14.2 3.6 %collective-permute-start.5 = (bf16[2064,128]{1,0:T(8,128)(2,1)}, bf16[2064,128]{1,0:T(8,128)(2,1)S(1)}, u32[]{:S(2)}, u32[]{:S(2)}) collective-permute-start(bf16[2064,128]{1,0:T(8,128)(2,1)} %get-tuple-element.28), channel_id=1, source_target_pairs={{1,0},{2,1},{3,2},{4,3},{5,4},{6,5},{7,6},{9,8},{10,9},{11,10},{12... | collective-permute-start | bytes 1585160 | tf_op jit(solution)/shard_map/ppermute | solution.py:46
  17.8 0.7 and_select_fusion
  18.7 0.8 iota_compare_fusion.1
  19.5 0.7 compare_select_fusion.4
  20.2 0.7 add_convert_fusion.picks
  20.9 93.2 %left.1 = (bf16[8,256,32,128]{3,2,1,0:T(8,128)(2,1)}, bf16[8,448,128]{2,1,0:T(8,128)(2,1)}, bf16[896,128]{1,0:T(8,128)(2,1)}, bf16[896,128]{1,0:T(8,128)(2,1)}) custom-call(bf16[288,256]{1,0:T(8,128)(2,1)} %add_convert_fusion.picks, bf16[64,448,256]{2,1,0:T(8,128)(2,1)} %bitcast.39, bf16[8192,128]{1,0:T(8,128)(2,1)} %get-tuple-element.29.halves), custom_call_target="tpu_custom_call" | custom-call | tf_op jit(solution)/shard_map/left/pallas_call | solution.py:170
  114.0 2.3 collective-permute-start.6
  116.4 3.4 %collective-permute-start.7 = (bf16[896,128]{1,0:T(8,128)(2,1)}, bf16[896,128]{1,0:T(8,128)(2,1)S(1)}, u32[]{:S(2)}, u32[]{:S(2)}) collective-permute-start(bf16[896,128]{1,0:T(8,128)(2,1)} %get-tuple-element.33), channel_id=1, source_target_pairs={{1,0},{2,1},{3,2},{4,3},{5,4},{6,5},{7,6},{9,8},{10,9},{11,10},{12... | collective-permute-start | bytes 688136 | tf_op jit(solution)/shard_map/ppermute | solution.py:46
  119.7 5.4 %all-to-all-start = ((bf16[8,448,128]{2,1,0:T(8,128)(2,1)}), bf16[8,448,128]{2,1,0:T(8,128)(2,1)S(1)}, u32[]{:S(2)}, u32[]{:S(2)}) async-start(bf16[8,448,128]{2,1,0:T(8,128)(2,1)} %get-tuple-element.31), calls=%async_computation | async-start | bytes 1835008 | tf_op jit(solution)/shard_map/all_to_all | solution.py:421
  125.2 2.4 %collective-permute-start.3 = (bf16[2064,128]{1,0:T(8,128)(2,1)}, bf16[2064,128]{1,0:T(8,128)(2,1)S(1)}, u32[]{:S(2)}, u32[]{:S(2)}) collective-permute-start(bf16[2064,128]{1,0:T(8,128)(2,1)} %get-tuple-element.26), channel_id=1, source_target_pairs={{8,0},{16,8},{24,16},{9,1},{17,9},{25,17},{10,2},{18,10},{26,18},{... | collective-permute-start | bytes 1585160 | tf_op jit(solution)/shard_map/ppermute | solution.py:46
  128.2 3.4 %collective-permute-start.2 = (bf16[2064,128]{1,0:T(8,128)(2,1)}, bf16[2064,128]{1,0:T(8,128)(2,1)S(1)}, u32[]{:S(2)}, u32[]{:S(2)}) collective-permute-start(bf16[2064,128]{1,0:T(8,128)(2,1)} %get-tuple-element.25), channel_id=1, source_target_pairs={{0,8},{8,16},{16,24},{1,9},{9,17},{17,25},{2,10},{10,18},{18,26},{... | collective-permute-start | bytes 1585160 | tf_op jit(solution)/shard_map/ppermute | solution.py:46
  131.7 4.3 %collective-permute-start = (bf16[2064,128]{1,0:T(8,128)(2,1)}, bf16[2064,128]{1,0:T(8,128)(2,1)}, u32[]{:S(2)}, u32[]{:S(2)}) collective-permute-start(bf16[2064,128]{1,0:T(8,128)(2,1)} %get-tuple-element.23), channel_id=1, source_target_pairs={{0,32},{32,64},{64,96},{1,33},{33,65},{65,97},{2,34},{34,66},{66,9... | collective-permute-start | bytes 1585160 | tf_op jit(solution)/shard_map/ppermute | solution.py:46
  136.0 5.3 %collective-permute-done.3.g2 = bf16[2064,128]{1,0:T(8,128)(2,1)S(1)} collective-permute-done((bf16[2064,128]{1,0:T(8,128)(2,1)}, bf16[2064,128]{1,0:T(8,128)(2,1)S(1)}, u32[]{:S(2)}, u32[]{:S(2)}) %collective-permute-start.3) | collective-permute-done | bytes 528416 | tf_op jit(solution)/shard_map/ppermute | solution.py:46
  141.3 1.3 collective-permute-start.1
  142.6 1.5 collective-permute-done.2.g3
  144.2 12.3 %collective-permute-done.1.g0 = bf16[2064,128]{1,0:T(8,128)(2,1)S(1)} collective-permute-done((bf16[2064,128]{1,0:T(8,128)(2,1)}, bf16[2064,128]{1,0:T(8,128)(2,1)S(1)}, u32[]{:S(2)}, u32[]{:S(2)}) %collective-permute-start.1) | collective-permute-done | bytes 528416 | tf_op jit(solution)/shard_map/ppermute | solution.py:46
  156.6 0.7 copy-done.5
  158.4 50.2 %sums.1 = (f32[32,32,128]{2,1,0:T(8,128)}, bf16[32,32,128]{2,1,0:T(8,128)(2,1)}, bf16[32,32,128]{2,1,0:T(8,128)(2,1)}, bf16[32,32,128]{2,1,0:T(8,128)(2,1)}, bf1...) custom-call(s32[256]{0:T(256)} %arrival.1, s32[8,256]{1,0:T(8,128)} %concatenate.6.place, ...), custom_call_target="tpu_custom_call" | custom-call | tf_op jit(solution)/shard_map/sums/pallas_call | solution.py:321
  208.6 3.1 %collective-permute-start.10 = (bf16[32,32,128]{2,1,0:T(8,128)(2,1)}, bf16[32,32,128]{2,1,0:T(8,128)(2,1)S(1)}, u32[]{:S(2)}, u32[]{:S(2)}) collective-permute-start(bf16[32,32,128]{2,1,0:T(8,128)(2,1)} %get-tuple-element.37), channel_id=1, source_target_pairs={{0,8},{8,16},{16,24},{1,9},{9,17},{17,25},{2,10},{10,18},{18,26},{... | collective-permute-start | bytes 786440 | tf_op jit(solution)/shard_map/ppermute | solution.py:46
  212.5 2.7 %collective-permute-start.11 = (bf16[32,32,128]{2,1,0:T(8,128)(2,1)}, bf16[32,32,128]{2,1,0:T(8,128)(2,1)S(1)}, u32[]{:S(2)}, u32[]{:S(2)}) collective-permute-start(bf16[32,32,128]{2,1,0:T(8,128)(2,1)} %get-tuple-element.38), channel_id=1, source_target_pairs={{8,0},{16,8},{24,16},{9,1},{17,9},{25,17},{10,2},{18,10},{26,18},{... | collective-permute-start | bytes 786440 | tf_op jit(solution)/shard_map/ppermute | solution.py:46
  215.2 1.9 collective-permute-start.12
  217.1 3.6 %collective-permute-start.13 = (bf16[32,32,128]{2,1,0:T(8,128)(2,1)}, bf16[32,32,128]{2,1,0:T(8,128)(2,1)S(1)}, u32[]{:S(2)}, u32[]{:S(2)}) collective-permute-start(bf16[32,32,128]{2,1,0:T(8,128)(2,1)} %get-tuple-element.40), channel_id=1, source_target_pairs={{1,0},{2,1},{3,2},{4,3},{5,4},{6,5},{7,6},{9,8},{10,9},{11,10},{12... | collective-permute-start | bytes 786440 | tf_op jit(solution)/shard_map/ppermute | solution.py:46
  220.8 3.3 %collective-permute-start.8 = (bf16[32,32,128]{2,1,0:T(8,128)(2,1)}, bf16[32,32,128]{2,1,0:T(8,128)(2,1)S(1)}, u32[]{:S(2)}, u32[]{:S(2)}) collective-permute-start(bf16[32,32,128]{2,1,0:T(8,128)(2,1)} %get-tuple-element.35), channel_id=1, source_target_pairs={{0,32},{32,64},{64,96},{1,33},{33,65},{65,97},{2,34},{34,66},{66,9... | collective-permute-start | bytes 786440 | tf_op jit(solution)/shard_map/ppermute | solution.py:46
  224.2 1.3 collective-permute-start.9
  226.3 3.5 %collective-permute-done.8.r0 = bf16[32,32,128]{2,1,0:T(8,128)(2,1)S(1)} collective-permute-done((bf16[32,32,128]{2,1,0:T(8,128)(2,1)}, bf16[32,32,128]{2,1,0:T(8,128)(2,1)S(1)}, u32[]{:S(2)}, u32[]{:S(2)}) %collective-permute-start.8) | collective-permute-done | bytes 262176 | tf_op jit(solution)/shard_map/ppermute | solution.py:46
  229.7 4.1 %collective-permute-done.9.r1 = bf16[32,32,128]{2,1,0:T(8,128)(2,1)S(1)} collective-permute-done((bf16[32,32,128]{2,1,0:T(8,128)(2,1)}, bf16[32,32,128]{2,1,0:T(8,128)(2,1)S(1)}, u32[]{:S(2)}, u32[]{:S(2)}) %collective-permute-start.9) | collective-permute-done | bytes 262176 | tf_op jit(solution)/shard_map/ppermute | solution.py:46
  233.9 0.7 copy-done.11
  234.5 5.0 %final.1 = f32[64,4096]{1,0:T(8,128)} custom-call(s32[7,32]{1,0:T(8,128)} %stack.52.numbers, f32[32,32,128]{2,1,0:T(8,128)} %get-tuple-element.34.own, bf16[32,32,128]{2,1,0:T(8,128)(2,1)} %copy-done.10, bf16[32,32,128]{2,1,0:T(8,128)(2,1)} %copy-done.11, bf16[32,32,128]{2,1,0:T(8,128)(2,1)} %copy-done.6, bf16[32,32,128]{2,1,0:T(8,128)(2,1)} %copy-done.7, ...), custom_call_target="tpu_custom_call" | custom-call | tf_op jit(solution)/shard_map/final/pallas_call | solution.py:374
  (60 shorter events, 4.2 us)
Async XLA Ops:
  0.0 127.6 %copy-start.15 = (s32[256,7]{0,1:T(8,128)S(1)}, s32[256,7]{0,1:T(8,128)}, u32[]{:S(2)}) copy-start(s32[256,7]{0,1:T(8,128)} %param.12) | copy-start | bytes 21508
  0.0 127.6 %copy-start.14 = (s32[256,7]{0,1:T(8,128)S(1)}, s32[256,7]{0,1:T(8,128)}, u32[]{:S(2)}) copy-start(s32[256,7]{0,1:T(8,128)} %param.13) | copy-start | bytes 21508
  12.2 119.4 %collective-permute-start.4 = (bf16[2064,128]{1,0:T(8,128)(2,1)}, bf16[2064,128]{1,0:T(8,128)(2,1)S(1)}, u32[]{:S(2)}, u32[]{:S(2)}) collective-permute-start(bf16[2064,128]{1,0:T(8,128)(2,1)} %get-tuple-element.27), channel_id=1, source_target_pairs={{0,1},{1,2},{2,3},{3,4},{4,5},{5,6},{6,7},{8,9},{9,10},{10,11},{11... | collective-permute-start | bytes 1585160 | tf_op jit(solution)/shard_map/ppermute | solution.py:46
  14.2 114.1 %collective-permute-start.5 = (bf16[2064,128]{1,0:T(8,128)(2,1)}, bf16[2064,128]{1,0:T(8,128)(2,1)S(1)}, u32[]{:S(2)}, u32[]{:S(2)}) collective-permute-start(bf16[2064,128]{1,0:T(8,128)(2,1)} %get-tuple-element.28), channel_id=1, source_target_pairs={{1,0},{2,1},{3,2},{4,3},{5,4},{6,5},{7,6},{9,8},{10,9},{11,10},{12... | collective-permute-start | bytes 1585160 | tf_op jit(solution)/shard_map/ppermute | solution.py:46
  114.0 111.6 %slice-start = ((s32[1,224]{1,0:T(1,128)}), s32[1,32]{1,0:T(1,128)S(1)}, s32[]{:S(2)}) async-start(s32[1,224]{1,0:T(1,128)} %param.15), calls=%async_computation.1 | async-start | bytes 1024 | tf_op jit(solution)/shard_map/slice | solution.py:434
  114.0 42.5 %collective-permute-start.6 = (bf16[896,128]{1,0:T(8,128)(2,1)}, bf16[896,128]{1,0:T(8,128)(2,1)S(1)}, u32[]{:S(2)}, u32[]{:S(2)}) collective-permute-start(bf16[896,128]{1,0:T(8,128)(2,1)} %get-tuple-element.32), channel_id=1, source_target_pairs={{0,1},{1,2},{2,3},{3,4},{4,5},{5,6},{6,7},{8,9},{9,10},{10,11},{11... | collective-permute-start | bytes 688136 | tf_op jit(solution)/shard_map/ppermute | solution.py:46
  116.4 40.2 %collective-permute-start.7 = (bf16[896,128]{1,0:T(8,128)(2,1)}, bf16[896,128]{1,0:T(8,128)(2,1)S(1)}, u32[]{:S(2)}, u32[]{:S(2)}) collective-permute-start(bf16[896,128]{1,0:T(8,128)(2,1)} %get-tuple-element.33), channel_id=1, source_target_pairs={{1,0},{2,1},{3,2},{4,3},{5,4},{6,5},{7,6},{9,8},{10,9},{11,10},{12... | collective-permute-start | bytes 688136 | tf_op jit(solution)/shard_map/ppermute | solution.py:46
  119.7 37.6 %all-to-all-start = ((bf16[8,448,128]{2,1,0:T(8,128)(2,1)}), bf16[8,448,128]{2,1,0:T(8,128)(2,1)S(1)}, u32[]{:S(2)}, u32[]{:S(2)}) async-start(bf16[8,448,128]{2,1,0:T(8,128)(2,1)} %get-tuple-element.31), calls=%async_computation | async-start | bytes 1835008 | tf_op jit(solution)/shard_map/all_to_all | solution.py:421
  125.2 16.1 %collective-permute-start.3 = (bf16[2064,128]{1,0:T(8,128)(2,1)}, bf16[2064,128]{1,0:T(8,128)(2,1)S(1)}, u32[]{:S(2)}, u32[]{:S(2)}) collective-permute-start(bf16[2064,128]{1,0:T(8,128)(2,1)} %get-tuple-element.26), channel_id=1, source_target_pairs={{8,0},{16,8},{24,16},{9,1},{17,9},{25,17},{10,2},{18,10},{26,18},{... | collective-permute-start | bytes 1585160 | tf_op jit(solution)/shard_map/ppermute | solution.py:46
  128.2 29.8 %copy-start.2 = (bf16[2064,128]{1,0:T(8,128)(2,1)}, bf16[2064,128]{1,0:T(8,128)(2,1)S(1)}, u32[]{:S(2)}) copy-start(bf16[2064,128]{1,0:T(8,128)(2,1)S(1)} %collective-permute-done.5.g4) | copy-start | bytes 1585156
  128.2 15.8 %collective-permute-start.2 = (bf16[2064,128]{1,0:T(8,128)(2,1)}, bf16[2064,128]{1,0:T(8,128)(2,1)S(1)}, u32[]{:S(2)}, u32[]{:S(2)}) collective-permute-start(bf16[2064,128]{1,0:T(8,128)(2,1)} %get-tuple-element.25), channel_id=1, source_target_pairs={{0,8},{8,16},{16,24},{1,9},{9,17},{17,25},{2,10},{10,18},{18,26},{... | collective-permute-start | bytes 1585160 | tf_op jit(solution)/shard_map/ppermute | solution.py:46
  131.7 26.4 %copy-start.1 = (bf16[2064,128]{1,0:T(8,128)(2,1)}, bf16[2064,128]{1,0:T(8,128)(2,1)S(1)}, u32[]{:S(2)}) copy-start(bf16[2064,128]{1,0:T(8,128)(2,1)S(1)} %collective-permute-done.4.g5) | copy-start | bytes 1585156
  131.7 25.7 %collective-permute-start = (bf16[2064,128]{1,0:T(8,128)(2,1)}, bf16[2064,128]{1,0:T(8,128)(2,1)}, u32[]{:S(2)}, u32[]{:S(2)}) collective-permute-start(bf16[2064,128]{1,0:T(8,128)(2,1)} %get-tuple-element.23), channel_id=1, source_target_pairs={{0,32},{32,64},{64,96},{1,33},{33,65},{65,97},{2,34},{34,66},{66,9... | collective-permute-start | bytes 1585160 | tf_op jit(solution)/shard_map/ppermute | solution.py:46
  141.3 15.3 %copy-start.3 = (bf16[2064,128]{1,0:T(8,128)(2,1)}, bf16[2064,128]{1,0:T(8,128)(2,1)S(1)}, u32[]{:S(2)}) copy-start(bf16[2064,128]{1,0:T(8,128)(2,1)S(1)} %collective-permute-done.3.g2) | copy-start | bytes 1585156
  141.3 15.3 %collective-permute-start.1 = (bf16[2064,128]{1,0:T(8,128)(2,1)}, bf16[2064,128]{1,0:T(8,128)(2,1)S(1)}, u32[]{:S(2)}, u32[]{:S(2)}) collective-permute-start(bf16[2064,128]{1,0:T(8,128)(2,1)} %get-tuple-element.24), channel_id=1, source_target_pairs={{32,0},{64,32},{96,64},{33,1},{65,33},{97,65},{34,2},{66,34},{98,6... | collective-permute-start | bytes 1585160 | tf_op jit(solution)/shard_map/ppermute | solution.py:46
  144.1 12.5 %copy-start.4 = (bf16[2064,128]{1,0:T(8,128)(2,1)}, bf16[2064,128]{1,0:T(8,128)(2,1)S(1)}, u32[]{:S(2)}) copy-start(bf16[2064,128]{1,0:T(8,128)(2,1)S(1)} %collective-permute-done.2.g3) | copy-start | bytes 1585156
  156.6 0.8 copy-start.5
  156.6 0.9 copy-start.12
  157.3 0.7 copy-start.13
  157.4 0.9 copy-start
  208.6 15.5 %collective-permute-start.10 = (bf16[32,32,128]{2,1,0:T(8,128)(2,1)}, bf16[32,32,128]{2,1,0:T(8,128)(2,1)S(1)}, u32[]{:S(2)}, u32[]{:S(2)}) collective-permute-start(bf16[32,32,128]{2,1,0:T(8,128)(2,1)} %get-tuple-element.37), channel_id=1, source_target_pairs={{0,8},{8,16},{16,24},{1,9},{9,17},{17,25},{2,10},{10,18},{18,26},{... | collective-permute-start | bytes 786440 | tf_op jit(solution)/shard_map/ppermute | solution.py:46
  212.5 13.7 %collective-permute-start.11 = (bf16[32,32,128]{2,1,0:T(8,128)(2,1)}, bf16[32,32,128]{2,1,0:T(8,128)(2,1)S(1)}, u32[]{:S(2)}, u32[]{:S(2)}) collective-permute-start(bf16[32,32,128]{2,1,0:T(8,128)(2,1)} %get-tuple-element.38), channel_id=1, source_target_pairs={{8,0},{16,8},{24,16},{9,1},{17,9},{25,17},{10,2},{18,10},{26,18},{... | collective-permute-start | bytes 786440 | tf_op jit(solution)/shard_map/ppermute | solution.py:46
  215.2 11.0 %collective-permute-start.12 = (bf16[32,32,128]{2,1,0:T(8,128)(2,1)}, bf16[32,32,128]{2,1,0:T(8,128)(2,1)S(1)}, u32[]{:S(2)}, u32[]{:S(2)}) collective-permute-start(bf16[32,32,128]{2,1,0:T(8,128)(2,1)} %get-tuple-element.39), channel_id=1, source_target_pairs={{0,1},{1,2},{2,3},{3,4},{4,5},{5,6},{6,7},{8,9},{9,10},{10,11},{11... | collective-permute-start | bytes 786440 | tf_op jit(solution)/shard_map/ppermute | solution.py:46
  217.1 9.1 %collective-permute-start.13 = (bf16[32,32,128]{2,1,0:T(8,128)(2,1)}, bf16[32,32,128]{2,1,0:T(8,128)(2,1)S(1)}, u32[]{:S(2)}, u32[]{:S(2)}) collective-permute-start(bf16[32,32,128]{2,1,0:T(8,128)(2,1)} %get-tuple-element.40), channel_id=1, source_target_pairs={{1,0},{2,1},{3,2},{4,3},{5,4},{6,5},{7,6},{9,8},{10,9},{11,10},{12... | collective-permute-start | bytes 786440 | tf_op jit(solution)/shard_map/ppermute | solution.py:46
  220.8 8.9 %collective-permute-start.8 = (bf16[32,32,128]{2,1,0:T(8,128)(2,1)}, bf16[32,32,128]{2,1,0:T(8,128)(2,1)S(1)}, u32[]{:S(2)}, u32[]{:S(2)}) collective-permute-start(bf16[32,32,128]{2,1,0:T(8,128)(2,1)} %get-tuple-element.35), channel_id=1, source_target_pairs={{0,32},{32,64},{64,96},{1,33},{33,65},{65,97},{2,34},{34,66},{66,9... | collective-permute-start | bytes 786440 | tf_op jit(solution)/shard_map/ppermute | solution.py:46
  224.1 9.7 %copy-start.6 = (bf16[32,32,128]{2,1,0:T(8,128)(2,1)}, bf16[32,32,128]{2,1,0:T(8,128)(2,1)S(1)}, u32[]{:S(2)}) copy-start(bf16[32,32,128]{2,1,0:T(8,128)(2,1)S(1)} %collective-permute-done.10.r2) | copy-start | bytes 786436
  224.2 9.7 %collective-permute-start.9 = (bf16[32,32,128]{2,1,0:T(8,128)(2,1)}, bf16[32,32,128]{2,1,0:T(8,128)(2,1)S(1)}, u32[]{:S(2)}, u32[]{:S(2)}) collective-permute-start(bf16[32,32,128]{2,1,0:T(8,128)(2,1)} %get-tuple-element.36), channel_id=1, source_target_pairs={{32,0},{64,32},{96,64},{33,1},{65,33},{97,65},{34,2},{66,34},{98,6... | collective-permute-start | bytes 786440 | tf_op jit(solution)/shard_map/ppermute | solution.py:46
  226.2 7.6 %copy-start.7 = (bf16[32,32,128]{2,1,0:T(8,128)(2,1)}, bf16[32,32,128]{2,1,0:T(8,128)(2,1)S(1)}, u32[]{:S(2)}) copy-start(bf16[32,32,128]{2,1,0:T(8,128)(2,1)S(1)} %collective-permute-done.11.r3) | copy-start | bytes 786436
  226.2 7.6 %copy-start.8 = (bf16[32,32,128]{2,1,0:T(8,128)(2,1)}, bf16[32,32,128]{2,1,0:T(8,128)(2,1)S(1)}, u32[]{:S(2)}) copy-start(bf16[32,32,128]{2,1,0:T(8,128)(2,1)S(1)} %collective-permute-done.12.r4) | copy-start | bytes 786436
  226.2 7.6 %copy-start.9 = (bf16[32,32,128]{2,1,0:T(8,128)(2,1)}, bf16[32,32,128]{2,1,0:T(8,128)(2,1)S(1)}, u32[]{:S(2)}) copy-start(bf16[32,32,128]{2,1,0:T(8,128)(2,1)S(1)} %collective-permute-done.13.r5) | copy-start | bytes 786436
  229.7 4.1 %copy-start.10 = (bf16[32,32,128]{2,1,0:T(8,128)(2,1)}, bf16[32,32,128]{2,1,0:T(8,128)(2,1)S(1)}, u32[]{:S(2)}) copy-start(bf16[32,32,128]{2,1,0:T(8,128)(2,1)S(1)} %collective-permute-done.8.r0) | copy-start | bytes 786436
  233.8 0.7 copy-start.11

commit v2 on v1

v2 whole, which is shorter than its diff:
```python
import jax
import jax.numpy as jnp
from jax import lax
from jax.experimental import pallas as pl
from jax.experimental.pallas import tpu as pltpu
from jax.sharding import PartitionSpec as P


B = 64
NBR = 7
CAP = 6
FAR = 2
NEAR = CAP - FAR
GCAP = 64
UCAP = 32
U_DEV = 224
CE_DEV = 64
ROWS = 256
LAYERS = 8
HALF = 32
LANES = 128
AXES = ("gx", "gy", "gz")
SENT = LAYERS * FAR + 2 * NEAR
SENT_PAD = 32
ROW_LEN = 3 * B + HALF
GHOST_LEN = GCAP * HALF
EXTRA = 16
TABLE = ROWS + 6 * GCAP
VMEM_LIMIT = 62 * 1024 * 1024
PITCH = HALF + 1
bf16 = jnp.bfloat16
f32 = jnp.float32


def lower_lanes(shape):
    return lax.broadcasted_iota(jnp.int32, shape, len(shape) - 1) < B


def swap_lanes(v):
    return jnp.concatenate([v[:, B:], v[:, :B]], axis=1)


def shifted(value, axis, by):
    devices = lax.axis_size(axis)
    pairs = [(i, i + by) for i in range(devices) if 0 <= i + by < devices]
    return lax.ppermute(value, axis, pairs)


def pack_kernel(lists, prolong, extra, halves, *rest):
    sends, work = rest[:6], rest[6]
    low = lower_lanes((16, LANES))

    def group(g, carry):
        rows = pl.ds(pl.multiple_of(g * 16, 16), 16)
        for s in range(16):
            near = prolong[rows, s * LANES : (s + 1) * LANES].astype(f32)
            far = prolong[rows, (s + 16) * LANES : (s + 17) * LANES].astype(f32)
            even = jnp.where(low, near, pltpu.roll(far, B, 1))
            odd = jnp.where(low, pltpu.roll(near, B, 1), far)
            work[pl.ds(2 * s, 16, stride=PITCH), :] = even
            work[pl.ds(2 * s + 1, 16, stride=PITCH), :] = odd
        for e in range(16):
            halves[pl.ds(pl.multiple_of((g * 16 + e) * HALF, HALF), HALF), :] = work[
                e * PITCH : e * PITCH + HALF, :
            ].astype(bf16)
        return carry

    lax.fori_loop(0, ROWS // 16, group, 0)

    def pick(q, carry):
        for j in range(6):
            row = lists[j, q]
            sends[j][pl.ds(pl.multiple_of(q * HALF, HALF), HALF), :] = halves[
                pl.ds(pl.multiple_of(row * HALF, HALF), HALF), :
            ]
        return carry

    lax.fori_loop(0, GCAP, pick, 0, unroll=4)
    for j in range(6):
        sends[j][GHOST_LEN:, :] = extra[...]


def pack(lists, prolong, extra):
    return pl.pallas_call(
        pack_kernel,
        grid_spec=pltpu.PrefetchScalarGridSpec(
            num_scalar_prefetch=1,
            grid=(1,),
            in_specs=[
                pl.BlockSpec((ROWS, B * B), lambda i, s: (0, 0)),
                pl.BlockSpec((EXTRA, LANES), lambda i, s: (0, 0)),
            ],
            out_specs=[pl.BlockSpec((ROWS * HALF, LANES), lambda i, s: (0, 0))]
            + [pl.BlockSpec((GHOST_LEN + EXTRA, LANES), lambda i, s: (0, 0))] * 6,
            scratch_shapes=[pltpu.VMEM((16 * PITCH, LANES), f32)],
        ),
        out_shape=[jax.ShapeDtypeStruct((ROWS * HALF, LANES), bf16)]
        + [jax.ShapeDtypeStruct((GHOST_LEN + EXTRA, LANES), bf16)] * 6,
        compiler_params=pltpu.CompilerParams(vmem_limit_bytes=VMEM_LIMIT),
        cost_estimate=pl.CostEstimate(flops=0, transcendentals=0, bytes_accessed=8_000_000),
        name="pack",
    )(lists, prolong, extra)


STEPS = 4
A_STEP = B // STEPS
R_STEP = ROWS // STEPS
TOTAL = ROWS + SENT_PAD
SPAN = TOTAL + 1


def left_kernel(
    layer, labels, blocks, halves, left, far, up, down, table0, table1, transposed, picks
):
    j, step = pl.program_id(0), pl.program_id(1)
    tables = (table0, table1)
    square = (ROWS, ROWS)

    @pl.when((j == 0) & (step == 0))
    def _():
        eye = (
            lax.broadcasted_iota(jnp.int32, (B, B), 0)
            == lax.broadcasted_iota(jnp.int32, (B, B), 1)
        ).astype(bf16)

        low = lower_lanes((B, LANES))

        def turn(n, carry):
            tiles = []
            for q in range(4):
                h = halves[pl.ds(pl.multiple_of((n * 4 + q) * HALF, HALF), HALF), :]
                tiles += [h[:, :B], h[:, B:]]
            got = lax.dot_general(
                eye,
                jnp.concatenate(tiles, axis=0),
                (((1,), (1,)), ((), ())),
                preferred_element_type=f32,
            )
            for q in range(4):
                pair = got[:, (q // 2) * LANES : (q // 2 + 1) * LANES]
                mine = low if q % 2 == 0 else jnp.logical_not(low)
                transposed[n * 4 + q] = jnp.where(mine, pair, 0.0).astype(bf16)
            return carry

        lax.fori_loop(0, ROWS // 4, turn, 0, unroll=8)

        arrival, owner = labels[0:1, :], labels[1:2, :]
        down_rows = lax.broadcasted_iota(jnp.int32, square, 0)
        along = lax.broadcasted_iota(jnp.int32, square, 1)
        taken = (down_rows == arrival).astype(f32).astype(bf16)
        unit = (down_rows == along).astype(f32).astype(bf16)
        picks[:ROWS, :] = lax.dot_general(
            unit, taken, (((1,), (1,)), ((), ())), preferred_element_type=f32
        ).astype(bf16)
        peer = lax.rem(owner, LAYERS)
        member = lax.broadcasted_iota(jnp.int32, (16, ROWS), 0) == peer
        earlier = (down_rows < along).astype(f32).astype(bf16)
        before = jnp.dot(
            member.astype(f32).astype(bf16), earlier, preferred_element_type=f32
        )
        rank = jnp.sum(jnp.where(member, before, 0.0), axis=0, keepdims=True).astype(jnp.int32)
        near = jnp.where(peer > layer[0], LAYERS * FAR, LAYERS * FAR + NEAR) + rank - FAR
        slot = jnp.where(rank < FAR, peer * FAR + rank, near)
        slot = jnp.where(peer == layer[0], -1, slot)
        sent = lax.broadcasted_iota(jnp.int32, (SENT_PAD, ROWS), 0) == slot
        picks[ROWS:, :] = sent.astype(f32).astype(bf16)

    @pl.when(step < STEPS)
    def _():
        def relay(n, carry):
            rows = pl.ds((step * A_STEP + n) * SPAN, TOTAL)
            got = lax.dot_general(
                picks[...], blocks[n], (((1,), (1,)), ((), ())), preferred_element_type=f32
            )
            table0[rows, :] = got[:, :LANES]
            table1[rows, :] = got[:, LANES:]
            return carry

        lax.fori_loop(0, A_STEP, relay, 0, unroll=8)

    @pl.when(step >= STEPS)
    def _():
        keep = lower_lanes((B, LANES)) | (j == 0)

        def multiply(n, carry):
            i = (step - STEPS) * R_STEP + 2 * n
            rows = [
                jnp.concatenate(
                    [t[pl.ds(i + q, B, stride=SPAN), :].astype(bf16) for t in tables], axis=1
                )
                for q in range(2)
            ]
            pairs = jnp.concatenate([transposed[i], transposed[i + 1]], axis=0)
            got = jnp.dot(pairs, jnp.concatenate(rows, axis=0), preferred_element_type=f32)
            for q in range(2):
                part = got[q * B : (q + 1) * B]
                left[0, 2 * n + q] = part[:, :LANES].astype(bf16)
                left[1, 2 * n + q] = jnp.where(keep, part[:, LANES:], 0.0).astype(bf16)
            return carry

        lax.fori_loop(0, R_STEP // 2, multiply, 0, unroll=16)

    def place_of(r):
        if r < LAYERS * FAR:
            return far.at[r // FAR], (r % FAR) * ROW_LEN
        if r < LAYERS * FAR + NEAR:
            return up, (r - LAYERS * FAR) * ROW_LEN
        return down, (r - LAYERS * FAR - NEAR) * ROW_LEN

    @pl.when((step == STEPS) & (j == 0))
    def _():
        for r in range(SENT):
            out, base = place_of(r)
            for c in range(2):
                out[base + c * B : base + (c + 1) * B, :] = tables[c][
                    pl.ds(ROWS + r, B, stride=SPAN), :
                ].astype(bf16)

    @pl.when((step == STEPS) & (j == 1))
    def _():
        for r in range(SENT):
            out, base = place_of(r)
            out[base + 2 * B : base + 3 * B, :] = table0[
                pl.ds(ROWS + r, B, stride=SPAN), :
            ].astype(bf16)
            last = table1[pl.ds(ROWS + r, B, stride=SPAN), :].astype(bf16)
            out[base + 3 * B : base + ROW_LEN, :] = jnp.concatenate(
                [last[:HALF, :B], last[HALF:, :B]], axis=1
            )


def make_left(layer, labels, blocks, halves):
    whole = lambda shape: pl.BlockSpec(shape, lambda j, s, layer: (0,) * len(shape))
    return pl.pallas_call(
        left_kernel,
        grid_spec=pltpu.PrefetchScalarGridSpec(
            num_scalar_prefetch=1,
            grid=(2, 2 * STEPS),
            in_specs=[
                whole((2, ROWS)),
                pl.BlockSpec(
                    (A_STEP, 2 * LANES, ROWS),
                    lambda j, s, layer: (jnp.minimum(s, STEPS - 1), j, 0),
                ),
                whole((ROWS * HALF, LANES)),
            ],
            out_specs=[
                pl.BlockSpec(
                    (2, R_STEP, B, LANES),
                    lambda j, s, layer: (j, jnp.maximum(s - STEPS, 0), 0, 0),
                ),
                whole((LAYERS, FAR * ROW_LEN, LANES)),
                whole((NEAR * ROW_LEN, LANES)),
                whole((NEAR * ROW_LEN, LANES)),
            ],
            scratch_shapes=[
                pltpu.VMEM((B * SPAN, LANES), f32),
                pltpu.VMEM((B * SPAN, LANES), f32),
                pltpu.VMEM((ROWS, B, LANES), bf16),
                pltpu.VMEM((TOTAL, ROWS), bf16),
            ],
        ),
        out_shape=[
            jax.ShapeDtypeStruct((4, ROWS, B, LANES), bf16),
            jax.ShapeDtypeStruct((LAYERS, FAR * ROW_LEN, LANES), bf16),
            jax.ShapeDtypeStruct((NEAR * ROW_LEN, LANES), bf16),
            jax.ShapeDtypeStruct((NEAR * ROW_LEN, LANES), bf16),
        ],
        compiler_params=pltpu.CompilerParams(
            vmem_limit_bytes=VMEM_LIMIT, dimension_semantics=("arbitrary", "arbitrary")
        ),
        cost_estimate=pl.CostEstimate(
            flops=12_000_000_000, transcendentals=0, bytes_accessed=60_000_000
        ),
        name="left",
    )(layer, labels, blocks, halves)


PARTS = 8
UNROLL = 8


def sums_kernel(
    moved_rows, place, left_hbm, halves, g0, g1, g2, g3, g4, g5, far, up, down,
    own, s0, s1, s2, s3, s4, s5,
    left, packed, double, acc0, acc1, moved, left_sem, table_sem, moved_sem,
):
    ghosts = (g0, g1, g2, g3, g4, g5)
    sends = (s0, s1, s2, s3, s4, s5)
    totals = (acc0, acc1)
    part = ROWS // PARTS
    table_copies = [pltpu.make_async_copy(halves, packed.at[: ROWS * HALF, :], table_sem.at[0])]
    for j in range(6):
        first = (ROWS + j * GCAP) * HALF
        table_copies.append(
            pltpu.make_async_copy(
                ghosts[j].at[:GHOST_LEN, :],
                packed.at[first : first + GHOST_LEN, :],
                table_sem.at[1 + j],
            )
        )
    bounds = (0, LAYERS * FAR * ROW_LEN, (LAYERS * FAR + NEAR) * ROW_LEN, SENT * ROW_LEN)
    moved_copies = [
        pltpu.make_async_copy(ref, moved.at[bounds[n] : bounds[n + 1], :], moved_sem.at[n])
        for n, ref in enumerate((far, up, down))
    ]
    left_copies = [
        pltpu.make_async_copy(
            left_hbm.at[:, pl.ds(n * part, part)],
            left.at[:, pl.ds(n * part, part)],
            left_sem.at[n],
        )
        for n in range(PARTS)
    ]
    for copy in table_copies + moved_copies + left_copies:
        copy.start()

    def clear(u, carry):
        for total in totals:
            total[u] = jnp.zeros((B, LANES), f32)
        return carry

    lax.fori_loop(0, U_DEV + 1, clear, 0, unroll=5)

    def expand(c, carry):
        h = packed[pl.ds(pl.multiple_of(c * HALF, HALF), HALF), :]
        turned = swap_lanes(h)
        double[c, 0:HALF, :] = jnp.concatenate([h[:, :B], turned[:, B:]], axis=1)
        double[c, HALF:, :] = jnp.concatenate([turned[:, :B], h[:, B:]], axis=1)
        return carry

    table_copies[0].wait()
    lax.fori_loop(0, ROWS, expand, 0, unroll=8)
    for copy in table_copies[1:]:
        copy.wait()
    lax.fori_loop(ROWS, TABLE, expand, 0, unroll=8)
    for copy in moved_copies:
        copy.wait()

    def arrive(s, carry):
        block = double[moved_rows[0, s], :, :][:, :B]
        base = pl.multiple_of(s * ROW_LEN, HALF)
        h = moved[pl.ds(base + 3 * B, HALF), :]
        chunks = [moved[pl.ds(base + c * B, B), :] for c in range(3)]
        chunks.append(jnp.concatenate([h[:, :B], h[:, B:]], axis=0))
        got = lax.dot_general(
            block, jnp.concatenate(chunks, axis=1), (((0,), (0,)), ((), ())),
            preferred_element_type=f32,
        ).astype(bf16)
        for c in range(3):
            left[c, ROWS + s] = got[:, c * LANES : (c + 1) * LANES]
        left[3, ROWS + s] = jnp.concatenate(
            [got[:, 3 * LANES :], jnp.zeros((B, B), bf16)], axis=1
        )
        return carry

    lax.fori_loop(0, SENT, arrive, 0, unroll=4)

    zero = jnp.zeros((B, LANES), bf16)

    def row(i, n):
        codes = [place[k, n] for k in range(NBR)]
        for quad in range(2):
            some = codes[4 * quad : 4 * quad + 4]
            slots = [code & 255 for code in some]
            tiles = [double[code >> 8] for code in some]
            tiles += [zero] * (4 - len(tiles))
            upper = jnp.concatenate([tiles[0][:, :B], tiles[2][:, B:]], axis=1)
            lower = jnp.concatenate([tiles[1][:, :B], tiles[3][:, B:]], axis=1)
            weights = jnp.concatenate(
                [
                    jnp.concatenate([upper, zero], axis=1),
                    jnp.concatenate([zero, lower], axis=1),
                ],
                axis=0,
            )
            rows = jnp.concatenate([left[2 * quad, i], left[2 * quad + 1, i]], axis=0)
            got = jnp.dot(rows, weights, preferred_element_type=f32)
            for side in range(2):
                for part in range(2):
                    k = side + 2 * part
                    if k < len(some):
                        first = side * LANES + part * B
                        lanes = slice(part * B, (part + 1) * B)
                        value = got[part * B : (part + 1) * B, first : first + B]
                        totals[side][slots[k], :, lanes] += value

    def some_rows(n, carry):
        for r in range(UNROLL):
            i = n * UNROLL + r
            row(i, i)
        return carry

    for n in range(PARTS):
        left_copies[n].wait()
        lax.fori_loop(n * part // UNROLL, (n + 1) * part // UNROLL, some_rows, 0)

    def more_rows(n, carry):
        for r in range(UNROLL):
            s = n * UNROLL + r
            row(ROWS + s, ROWS + s)
        return carry

    lax.fori_loop(0, SENT // UNROLL, more_rows, 0)
    low = lower_lanes((HALF, LANES))
    for v in range(7):

        def gather(q, carry):
            u = v * UCAP + q
            value = acc0[u] + acc1[u]
            top, bottom = value[:HALF], value[HALF:]
            value = jnp.where(low, top, bottom) + pltpu.roll(jnp.where(low, bottom, top), B, 1)
            if v == 0:
                own[q] = value
            else:
                sends[v - 1][q] = value.astype(bf16)
            return carry

        lax.fori_loop(0, UCAP, gather, 0, unroll=4)


def make_sums(moved_rows, place, left, halves, ghosts, far, up, down):
    hbm = pl.BlockSpec(memory_space=pl.ANY)
    block = pl.BlockSpec((UCAP, HALF, LANES), lambda i, *s: (0, 0, 0))
    return pl.pallas_call(
        sums_kernel,
        grid_spec=pltpu.PrefetchScalarGridSpec(
            num_scalar_prefetch=2,
            grid=(1,),
            in_specs=[hbm] * 11,
            out_specs=[block] * 7,
            scratch_shapes=[
                pltpu.VMEM((4, ROWS + SENT, B, LANES), bf16),
                pltpu.VMEM((TABLE * HALF, LANES), bf16),
                pltpu.VMEM((TABLE, B, LANES), bf16),
            ]
            + [pltpu.VMEM((U_DEV + 1, B, LANES), f32)] * 2
            + [
                pltpu.VMEM((SENT * ROW_LEN, LANES), bf16),
                pltpu.SemaphoreType.DMA((PARTS,)),
                pltpu.SemaphoreType.DMA((7,)),
                pltpu.SemaphoreType.DMA((3,)),
            ],
        ),
        out_shape=[jax.ShapeDtypeStruct((UCAP, HALF, LANES), f32)]
        + [jax.ShapeDtypeStruct((UCAP, HALF, LANES), bf16)] * 6,
        compiler_params=pltpu.CompilerParams(vmem_limit_bytes=VMEM_LIMIT),
        cost_estimate=pl.CostEstimate(
            flops=8_000_000_000, transcendentals=0, bytes_accessed=30_000_000
        ),
        name="sums",
    )(moved_rows, place, left, halves, *ghosts, far, up, down)


def final_kernel(numbers, own, r0, r1, r2, r3, r4, r5, out, total):
    parts = (own, r0, r1, r2, r3, r4, r5)
    total[...] = jnp.zeros_like(total)

    def add(q, carry):
        for v in range(7):
            rows = pl.ds(numbers[v, q] * PITCH, HALF)
            total[rows, :] += parts[v][q].astype(f32)
        return carry

    lax.fori_loop(0, UCAP, add, 0, unroll=2)
    low = lower_lanes((8, LANES))

    for g in range(CE_DEV // 8):
        for s in range(16):
            a = total[pl.ds(g * 8 * PITCH + 2 * s, 8, stride=PITCH), :]
            b = total[pl.ds(g * 8 * PITCH + 2 * s + 1, 8, stride=PITCH), :]
            out[g * 8 : g * 8 + 8, s * LANES : (s + 1) * LANES] = jnp.where(
                low, a, pltpu.roll(b, B, 1)
            )
            out[g * 8 : g * 8 + 8, (s + 16) * LANES : (s + 17) * LANES] = jnp.where(
                low, pltpu.roll(a, B, 1), b
            )


def make_final(numbers, parts):
    block = pl.BlockSpec((UCAP, HALF, LANES), lambda i, *s: (0, 0, 0))
    return pl.pallas_call(
        final_kernel,
        grid_spec=pltpu.PrefetchScalarGridSpec(
            num_scalar_prefetch=1,
            grid=(1,),
            in_specs=[block] * 7,
            out_specs=pl.BlockSpec((CE_DEV, B * B), lambda i, *s: (0, 0)),
            scratch_shapes=[pltpu.VMEM((CE_DEV * PITCH, LANES), f32)],
        ),
        out_shape=jax.ShapeDtypeStruct((CE_DEV, B * B), f32),
        compiler_params=pltpu.CompilerParams(vmem_limit_bytes=VMEM_LIMIT),
        name="final",
    )(numbers, *parts)


def neighbour_shift(value, facing):
    axis = AXES[facing // 2]
    return shifted(value, axis, 1 - 2 * (facing % 2))


def one_shard(blocks, prolong, new_owner, arrival, columns, targets, ghost_lists, touched):
    own_layer = lax.axis_index("gz")
    touched_here = touched[0]

    extra = jnp.pad(touched_here, (0, EXTRA * LANES - U_DEV)).reshape(EXTRA, LANES).astype(bf16)
    halves, *outbound = pack(ghost_lists[0], prolong, extra)
    ghosts = []
    for facing in range(6):
        ghosts.append(neighbour_shift(outbound[facing ^ 1], facing ^ 1))

    left, far, up, down = make_left(
        own_layer[None], jnp.stack([arrival, new_owner]), jnp.transpose(blocks, (1, 2, 0)), halves
    )
    far_in = lax.all_to_all(far, "gz", split_axis=0, concat_axis=0, tiled=True)
    up_in = shifted(up, "gz", 1)
    down_in = shifted(down, "gz", -1)

    old = jnp.arange(ROWS, dtype=jnp.int32)
    labels = jnp.arange(LAYERS, dtype=jnp.int32)
    cols = columns.T
    place = jnp.where(cols >= 0, cols * 256 + targets.T, U_DEV)
    ranks = jnp.arange(FAR, dtype=jnp.int32)
    later = FAR + jnp.arange(NEAR, dtype=jnp.int32)
    codes = ROWS + jnp.concatenate(
        [
            (labels[:, None] * CAP + ranks[None, :]).reshape(-1),
            (own_layer - 1) * CAP + later,
            (own_layer + 1) * CAP + later,
        ]
    )
    match = (codes[:, None] == arrival[None, :]) & (codes[:, None] >= ROWS)
    row_of = jnp.sum(jnp.where(match, old[None, :] + 1, 0), axis=1) - 1
    taken = jnp.sum(jnp.where(match[None], place[:, None, :] + 1, 0), axis=2) - 1
    moved_place = jnp.where(row_of[None, :] >= 0, taken, U_DEV)
    place = jnp.concatenate([place, moved_place], axis=1)
    own, *sends = make_sums(
        jnp.maximum(row_of, 0)[None, :], place, left, halves, ghosts,
        far_in.reshape(LAYERS * FAR * ROW_LEN, LANES), up_in, down_in,
    )
    got = [neighbour_shift(sends[facing], facing) for facing in range(6)]

    numbers = [touched_here[:UCAP]]
    for facing in range(6):
        flat = ghosts[facing ^ 1][GHOST_LEN : GHOST_LEN + 2].reshape(-1)
        first = (facing + 1) * UCAP
        numbers.append(flat[first : first + UCAP].astype(jnp.int32))
    return make_final(jnp.stack(numbers), [own] + got)


def solution(mesh):
    return jax.shard_map(
        one_shard,
        mesh=mesh,
        in_specs=(
            P(AXES, None, None),
            P(AXES, None),
            P(AXES),
            P(AXES),
            P(AXES, None),
            P(AXES, None),
            P(AXES, None, None),
            P(AXES, None),
        ),
        out_specs=P(AXES, None),
        check_vma=False,
    )
```

time: 241 us -> 159 us (0.66)
  Pallas kernels: 158 us -> 74.5 us
  waiting for transfers between devices: 26.7 us -> 29.5 us
    pallas_call x1, Pallas kernels: 93.2 us -> 26.7 us  [make_left(): pl.pallas_call(left_kernel, grid_spec=pltpu.PrefetchScalarGridSpec(num_sc...]
    pallas_call x1, Pallas kernels: 50.2 us -> 35.5 us  [make_sums(): pl.pallas_call(sums_kernel, grid_spec=pltpu.PrefetchScalarGridSpec(num_sc...]
    ppermute x14, waiting for transfers between devices: 26.7 us -> 29.5 us  [shifted(): return lax.ppermute(value, axis, pairs)]
  transfers between devices with their start and end apart: 15 -> 15, of which waited for: 5 -> 5; matrix products, arithmetic and copies ran while one was open for 2% -> 2% of each run, Pallas kernels for 39% -> 0%
where the time goes in v2:
time: 159 us; the launch traced here: 158 us
  Pallas kernels  74.5 us (47%)
  starting transfers between devices  43.4 us (27%)
  waiting for transfers between devices  29.5 us (19%)
  local copies, waits for them, and re-layouts  5.65 us (4%)
  other arithmetic  4.22 us (3%)
    ppermute x14, starting transfers between devices, shifted(): return lax.ppermute(value, axis, pairs)  37.9 us
    pallas_call x1, Pallas kernels, make_sums(): pl.pallas_call(sums_kernel, grid_spec=pltpu.PrefetchScalarGridSpec(num_sc...  35.5 us
    ppermute x14, waiting for transfers between devices, shifted(): return lax.ppermute(value, axis, pairs)  29.5 us
    pallas_call x1, Pallas kernels, make_left(): pl.pallas_call(left_kernel, grid_spec=pltpu.PrefetchScalarGridSpec(num_sc...  26.7 us
    pallas_call x1, Pallas kernels, pack(): pl.pallas_call(pack_kernel, grid_spec=pltpu.PrefetchScalarGridSpec(num_sc...  7.7 us
    all_to_all x1, starting transfers between devices, one_shard(): far_in = lax.all_to_all(far, 'gz', split_axis=0, concat_axis=0, tiled=True)  5.43 us
    pallas_call x1, Pallas kernels, make_final(): pl.pallas_call(final_kernel, grid_spec=pltpu.PrefetchScalarGridSpec(num_s...  4.64 us
    unnamed x35, local copies, waits for them, and re-layouts  3.69 us
  transfers between devices with their start and end apart: 15, of which 5 were waited for; matrix products, arithmetic and copies ran while one was open for 2% of the time, Pallas kernels for 0%

profile of v2, /device:TPU:34, one launch (start us, length us, event | category | flops | bytes accessed | tf_op | source)
XLA Modules:
  0.0 157.6 jit_solution(9711491007763800489)
XLA Ops:
  0.0 0.7 convert_reduce_fusion
  1.3 1.3 copy.11
  2.6 1.3 pad_add_fusion.1.labels
  3.8 7.7 %pack.1 = (bf16[8192,128]{1,0:T(8,128)(2,1)}, bf16[2064,128]{1,0:T(8,128)(2,1)}, bf16[2064,128]{1,0:T(8,128)(2,1)}, bf16[2064,128]{1,0:T(8,128)(2,1)}, bf16[2064...) custom-call(s32[6,64]{1,0:T(8,128)} %bitcast.46, bf16[256,4096]{1,0:T(8,128)(2,1)} %prolong.1, ...), custom_call_target="tpu_custom_call" | custom-call | bytes 8000000 | tf_op jit(solution)/shard_map/pack/pallas_call | solution.py:84
  11.6 26.7 %left.1 = (bf16[4,256,64,128]{3,2,1,0:T(8,128)(2,1)}, bf16[8,448,128]{2,1,0:T(8,128)(2,1)}, bf16[896,128]{1,0:T(8,128)(2,1)}, bf16[896,128]{1,0:T(8,128)(2,1)}) custom-call(s32[1]{0:T(128)} %bitcast.15.layer, s32[2,256]{1,0:T(2,128)} %pad_add_fusion.1.labels, bf16[64,448,256]{2,1,0:T(8,128)(2,1)} %bitcast.49, bf16[8192,128]{1,0:T(8,128)(2,1)} %get-tuple-element.29.halves), custom_call_target="tpu_custom_call" | custom-call | flops 12000000000 | bytes 60000000 | tf_op jit(solution)/shard_map/left/pallas_call | solution.py:234
  38.3 1.9 %collective-permute-start.6 = (bf16[896,128]{1,0:T(8,128)(2,1)}, bf16[896,128]{1,0:T(8,128)(2,1)S(1)}, u32[]{:S(2)}, u32[]{:S(2)}) collective-permute-start(bf16[896,128]{1,0:T(8,128)(2,1)} %get-tuple-element.32), channel_id=1, source_target_pairs={{0,1},{1,2},{2,3},{3,4},{4,5},{5,6},{6,7},{8,9},{9,10},{10,11},{11... | collective-permute-start | bytes 688136 | tf_op jit(solution)/shard_map/ppermute | solution.py:46
  40.2 3.6 %collective-permute-start.7 = (bf16[896,128]{1,0:T(8,128)(2,1)}, bf16[896,128]{1,0:T(8,128)(2,1)}, u32[]{:S(2)}, u32[]{:S(2)}) collective-permute-start(bf16[896,128]{1,0:T(8,128)(2,1)} %get-tuple-element.33), channel_id=1, source_target_pairs={{1,0},{2,1},{3,2},{4,3},{5,4},{6,5},{7,6},{9,8},{10,9},{11,10},{12... | collective-permute-start | bytes 688136 | tf_op jit(solution)/shard_map/ppermute | solution.py:46
  43.8 5.4 %all-to-all-start = ((bf16[8,448,128]{2,1,0:T(8,128)(2,1)}), bf16[8,448,128]{2,1,0:T(8,128)(2,1)S(1)}, u32[]{:S(2)}, u32[]{:S(2)}) async-start(bf16[8,448,128]{2,1,0:T(8,128)(2,1)} %get-tuple-element.31), calls=%async_computation | async-start | bytes 1835008 | tf_op jit(solution)/shard_map/all_to_all | solution.py:515
  49.3 2.4 %collective-permute-start.3 = (bf16[2064,128]{1,0:T(8,128)(2,1)}, bf16[2064,128]{1,0:T(8,128)(2,1)S(1)}, u32[]{:S(2)}, u32[]{:S(2)}) collective-permute-start(bf16[2064,128]{1,0:T(8,128)(2,1)} %get-tuple-element.26), channel_id=1, source_target_pairs={{8,0},{16,8},{24,16},{9,1},{17,9},{25,17},{10,2},{18,10},{26,18},{... | collective-permute-start | bytes 1585160 | tf_op jit(solution)/shard_map/ppermute | solution.py:46
  51.7 1.9 %collective-permute-start.4 = (bf16[2064,128]{1,0:T(8,128)(2,1)}, bf16[2064,128]{1,0:T(8,128)(2,1)S(1)}, u32[]{:S(2)}, u32[]{:S(2)}) collective-permute-start(bf16[2064,128]{1,0:T(8,128)(2,1)} %get-tuple-element.27), channel_id=1, source_target_pairs={{0,1},{1,2},{2,3},{3,4},{4,5},{5,6},{6,7},{8,9},{9,10},{10,11},{11... | collective-permute-start | bytes 1585160 | tf_op jit(solution)/shard_map/ppermute | solution.py:46
  53.6 3.6 %collective-permute-start.5 = (bf16[2064,128]{1,0:T(8,128)(2,1)}, bf16[2064,128]{1,0:T(8,128)(2,1)S(1)}, u32[]{:S(2)}, u32[]{:S(2)}) collective-permute-start(bf16[2064,128]{1,0:T(8,128)(2,1)} %get-tuple-element.28), channel_id=1, source_target_pairs={{1,0},{2,1},{3,2},{4,3},{5,4},{6,5},{7,6},{9,8},{10,9},{11,10},{12... | collective-permute-start | bytes 1585160 | tf_op jit(solution)/shard_map/ppermute | solution.py:46
  58.7 0.6 pad_add_fusion.place
  59.3 6.3 %collective-permute-done.5.g4 = bf16[2064,128]{1,0:T(8,128)(2,1)S(1)} collective-permute-done((bf16[2064,128]{1,0:T(8,128)(2,1)}, bf16[2064,128]{1,0:T(8,128)(2,1)S(1)}, u32[]{:S(2)}, u32[]{:S(2)}) %collective-permute-start.5) | collective-permute-done | bytes 528416 | tf_op jit(solution)/shard_map/ppermute | solution.py:46
  65.6 3.4 %collective-permute-start.2 = (bf16[2064,128]{1,0:T(8,128)(2,1)}, bf16[2064,128]{1,0:T(8,128)(2,1)S(1)}, u32[]{:S(2)}, u32[]{:S(2)}) collective-permute-start(bf16[2064,128]{1,0:T(8,128)(2,1)} %get-tuple-element.25), channel_id=1, source_target_pairs={{0,8},{8,16},{16,24},{1,9},{9,17},{17,25},{2,10},{10,18},{18,26},{... | collective-permute-start | bytes 1585160 | tf_op jit(solution)/shard_map/ppermute | solution.py:46
  69.0 4.3 %collective-permute-start = (bf16[2064,128]{1,0:T(8,128)(2,1)S(1)}, bf16[2064,128]{1,0:T(8,128)(2,1)}, u32[]{:S(2)}, u32[]{:S(2)}) collective-permute-start(bf16[2064,128]{1,0:T(8,128)(2,1)S(1)} %copy-done.10), channel_id=1, source_target_pairs={{0,32},{32,64},{64,96},{1,33},{33,65},{65,97},{2,34},{34,66},{66,9... | collective-permute-start | bytes 1585160 | tf_op jit(solution)/shard_map/ppermute | solution.py:46
  73.3 1.3 collective-permute-start.1
  74.6 6.7 %collective-permute-done.2.g3 = bf16[2064,128]{1,0:T(8,128)(2,1)S(1)} collective-permute-done((bf16[2064,128]{1,0:T(8,128)(2,1)}, bf16[2064,128]{1,0:T(8,128)(2,1)S(1)}, u32[]{:S(2)}, u32[]{:S(2)}) %collective-permute-start.2) | collective-permute-done | bytes 528416 | tf_op jit(solution)/shard_map/ppermute | solution.py:46
  81.5 8.1 %collective-permute-done.1.g0 = bf16[2064,128]{1,0:T(8,128)(2,1)S(1)} collective-permute-done((bf16[2064,128]{1,0:T(8,128)(2,1)}, bf16[2064,128]{1,0:T(8,128)(2,1)S(1)}, u32[]{:S(2)}, u32[]{:S(2)}) %collective-permute-start.1) | collective-permute-done | bytes 528416 | tf_op jit(solution)/shard_map/ppermute | solution.py:46
  89.6 0.8 copy-done.15
  90.5 0.8 copy-done
  91.4 35.5 %sums.1 = (f32[32,32,128]{2,1,0:T(8,128)}, bf16[32,32,128]{2,1,0:T(8,128)(2,1)}, bf16[32,32,128]{2,1,0:T(8,128)(2,1)}, bf16[32,32,128]{2,1,0:T(8,128)(2,1)}, bf1...) custom-call(s32[1,24]{1,0:T(1,128)} %maximum_bitcast_fusion.moved_rows, ...), custom_call_target="tpu_custom_call" | custom-call | flops 8000000000 | bytes 30000000 | tf_op jit(solution)/shard_map/sums/pallas_call | solution.py:425
  126.8 3.1 %collective-permute-start.10 = (bf16[32,32,128]{2,1,0:T(8,128)(2,1)}, bf16[32,32,128]{2,1,0:T(8,128)(2,1)S(1)}, u32[]{:S(2)}, u32[]{:S(2)}) collective-permute-start(bf16[32,32,128]{2,1,0:T(8,128)(2,1)} %get-tuple-element.37), channel_id=1, source_target_pairs={{0,8},{8,16},{16,24},{1,9},{9,17},{17,25},{2,10},{10,18},{18,26},{... | collective-permute-start | bytes 786440 | tf_op jit(solution)/shard_map/ppermute | solution.py:46
  130.0 0.7 slice_bitcast_fusion.5
  130.7 2.7 %collective-permute-start.11 = (bf16[32,32,128]{2,1,0:T(8,128)(2,1)}, bf16[32,32,128]{2,1,0:T(8,128)(2,1)S(1)}, u32[]{:S(2)}, u32[]{:S(2)}) collective-permute-start(bf16[32,32,128]{2,1,0:T(8,128)(2,1)} %get-tuple-element.38), channel_id=1, source_target_pairs={{8,0},{16,8},{24,16},{9,1},{17,9},{25,17},{10,2},{18,10},{26,18},{... | collective-permute-start | bytes 786440 | tf_op jit(solution)/shard_map/ppermute | solution.py:46
  133.4 1.9 %collective-permute-start.12 = (bf16[32,32,128]{2,1,0:T(8,128)(2,1)}, bf16[32,32,128]{2,1,0:T(8,128)(2,1)S(1)}, u32[]{:S(2)}, u32[]{:S(2)}) collective-permute-start(bf16[32,32,128]{2,1,0:T(8,128)(2,1)} %get-tuple-element.39), channel_id=1, source_target_pairs={{0,1},{1,2},{2,3},{3,4},{4,5},{5,6},{6,7},{8,9},{9,10},{10,11},{11... | collective-permute-start | bytes 786440 | tf_op jit(solution)/shard_map/ppermute | solution.py:46
  135.4 3.6 %collective-permute-start.13 = (bf16[32,32,128]{2,1,0:T(8,128)(2,1)}, bf16[32,32,128]{2,1,0:T(8,128)(2,1)S(1)}, u32[]{:S(2)}, u32[]{:S(2)}) collective-permute-start(bf16[32,32,128]{2,1,0:T(8,128)(2,1)} %get-tuple-element.40), channel_id=1, source_target_pairs={{1,0},{2,1},{3,2},{4,3},{5,4},{6,5},{7,6},{9,8},{10,9},{11,10},{12... | collective-permute-start | bytes 786440 | tf_op jit(solution)/shard_map/ppermute | solution.py:46
  139.0 2.7 %collective-permute-start.8 = (bf16[32,32,128]{2,1,0:T(8,128)(2,1)}, bf16[32,32,128]{2,1,0:T(8,128)(2,1)S(1)}, u32[]{:S(2)}, u32[]{:S(2)}) collective-permute-start(bf16[32,32,128]{2,1,0:T(8,128)(2,1)} %get-tuple-element.35), channel_id=1, source_target_pairs={{0,32},{32,64},{64,96},{1,33},{33,65},{65,97},{2,34},{34,66},{66,9... | collective-permute-start | bytes 786440 | tf_op jit(solution)/shard_map/ppermute | solution.py:46
  141.8 1.3 collective-permute-start.9
  143.9 4.3 %collective-permute-done.8.r0 = bf16[32,32,128]{2,1,0:T(8,128)(2,1)S(1)} collective-permute-done((bf16[32,32,128]{2,1,0:T(8,128)(2,1)}, bf16[32,32,128]{2,1,0:T(8,128)(2,1)S(1)}, u32[]{:S(2)}, u32[]{:S(2)}) %collective-permute-start.8) | collective-permute-done | bytes 262176 | tf_op jit(solution)/shard_map/ppermute | solution.py:46
  148.2 4.0 %collective-permute-done.9.r1 = bf16[32,32,128]{2,1,0:T(8,128)(2,1)S(1)} collective-permute-done((bf16[32,32,128]{2,1,0:T(8,128)(2,1)}, bf16[32,32,128]{2,1,0:T(8,128)(2,1)S(1)}, u32[]{:S(2)}, u32[]{:S(2)}) %collective-permute-start.9) | collective-permute-done | bytes 262176 | tf_op jit(solution)/shard_map/ppermute | solution.py:46
  152.3 0.7 copy-done.6
  152.9 4.6 %final.1 = f32[64,4096]{1,0:T(8,128)} custom-call(s32[7,32]{1,0:T(8,128)} %stack.59.numbers, f32[32,32,128]{2,1,0:T(8,128)} %get-tuple-element.34.own, bf16[32,32,128]{2,1,0:T(8,128)(2,1)} %copy-done.5, bf16[32,32,128]{2,1,0:T(8,128)(2,1)} %copy-done.6, bf16[32,32,128]{2,1,0:T(8,128)(2,1)} %copy-done.1, bf16[32,32,128]{2,1,0:T(8,128)(2,1)} %copy-done.2, ...), custom_call_target="tpu_custom_call" | custom-call | tf_op jit(solution)/shard_map/final/pallas_call | solution.py:482
  (69 shorter events, 3.1 us)
Async XLA Ops:
  11.5 46.0 %copy-start.7 = (s32[256]{0:T(256)S(1)}, s32[256]{0:T(256)}, u32[]{:S(2)}) copy-start(s32[256]{0:T(256)} %param.11) | copy-start | bytes 3076
  11.5 46.3 %copy-start.8 = (s32[256,7]{0,1:T(8,128)S(1)}, s32[256,7]{0,1:T(8,128)}, u32[]{:S(2)}) copy-start(s32[256,7]{0,1:T(8,128)} %param.13) | copy-start | bytes 21508
  11.5 46.3 %copy-start.9 = (s32[256,7]{0,1:T(8,128)S(1)}, s32[256,7]{0,1:T(8,128)}, u32[]{:S(2)}) copy-start(s32[256,7]{0,1:T(8,128)} %param.12) | copy-start | bytes 21508
  11.6 57.5 %copy-start.10 = (bf16[2064,128]{1,0:T(8,128)(2,1)S(1)}, bf16[2064,128]{1,0:T(8,128)(2,1)}, u32[]{:S(2)}) copy-start(bf16[2064,128]{1,0:T(8,128)(2,1)} %get-tuple-element.23) | copy-start | bytes 1585156
  38.3 51.3 %collective-permute-start.6 = (bf16[896,128]{1,0:T(8,128)(2,1)}, bf16[896,128]{1,0:T(8,128)(2,1)S(1)}, u32[]{:S(2)}, u32[]{:S(2)}) collective-permute-start(bf16[896,128]{1,0:T(8,128)(2,1)} %get-tuple-element.32), channel_id=1, source_target_pairs={{0,1},{1,2},{2,3},{3,4},{4,5},{5,6},{6,7},{8,9},{9,10},{10,11},{11... | collective-permute-start | bytes 688136 | tf_op jit(solution)/shard_map/ppermute | solution.py:46
  40.2 49.4 %collective-permute-start.7 = (bf16[896,128]{1,0:T(8,128)(2,1)}, bf16[896,128]{1,0:T(8,128)(2,1)}, u32[]{:S(2)}, u32[]{:S(2)}) collective-permute-start(bf16[896,128]{1,0:T(8,128)(2,1)} %get-tuple-element.33), channel_id=1, source_target_pairs={{1,0},{2,1},{3,2},{4,3},{5,4},{6,5},{7,6},{9,8},{10,9},{11,10},{12... | collective-permute-start | bytes 688136 | tf_op jit(solution)/shard_map/ppermute | solution.py:46
  43.8 46.6 %all-to-all-start = ((bf16[8,448,128]{2,1,0:T(8,128)(2,1)}), bf16[8,448,128]{2,1,0:T(8,128)(2,1)S(1)}, u32[]{:S(2)}, u32[]{:S(2)}) async-start(bf16[8,448,128]{2,1,0:T(8,128)(2,1)} %get-tuple-element.31), calls=%async_computation | async-start | bytes 1835008 | tf_op jit(solution)/shard_map/all_to_all | solution.py:515
  49.3 24.1 %collective-permute-start.3 = (bf16[2064,128]{1,0:T(8,128)(2,1)}, bf16[2064,128]{1,0:T(8,128)(2,1)S(1)}, u32[]{:S(2)}, u32[]{:S(2)}) collective-permute-start(bf16[2064,128]{1,0:T(8,128)(2,1)} %get-tuple-element.26), channel_id=1, source_target_pairs={{8,0},{16,8},{24,16},{9,1},{17,9},{25,17},{10,2},{18,10},{26,18},{... | collective-permute-start | bytes 1585160 | tf_op jit(solution)/shard_map/ppermute | solution.py:46
  51.7 17.3 %collective-permute-start.4 = (bf16[2064,128]{1,0:T(8,128)(2,1)}, bf16[2064,128]{1,0:T(8,128)(2,1)S(1)}, u32[]{:S(2)}, u32[]{:S(2)}) collective-permute-start(bf16[2064,128]{1,0:T(8,128)(2,1)} %get-tuple-element.27), channel_id=1, source_target_pairs={{0,1},{1,2},{2,3},{3,4},{4,5},{5,6},{6,7},{8,9},{9,10},{10,11},{11... | collective-permute-start | bytes 1585160 | tf_op jit(solution)/shard_map/ppermute | solution.py:46
  53.6 11.9 %collective-permute-start.5 = (bf16[2064,128]{1,0:T(8,128)(2,1)}, bf16[2064,128]{1,0:T(8,128)(2,1)S(1)}, u32[]{:S(2)}, u32[]{:S(2)}) collective-permute-start(bf16[2064,128]{1,0:T(8,128)(2,1)} %get-tuple-element.28), channel_id=1, source_target_pairs={{1,0},{2,1},{3,2},{4,3},{5,4},{6,5},{7,6},{9,8},{10,9},{11,10},{12... | collective-permute-start | bytes 1585160 | tf_op jit(solution)/shard_map/ppermute | solution.py:46
  65.6 15.7 %copy-start.13 = (bf16[2064,128]{1,0:T(8,128)(2,1)}, bf16[2064,128]{1,0:T(8,128)(2,1)S(1)}, u32[]{:S(2)}) copy-start(bf16[2064,128]{1,0:T(8,128)(2,1)S(1)} %collective-permute-done.5.g4) | copy-start | bytes 1585156
  65.6 15.7 %collective-permute-start.2 = (bf16[2064,128]{1,0:T(8,128)(2,1)}, bf16[2064,128]{1,0:T(8,128)(2,1)S(1)}, u32[]{:S(2)}, u32[]{:S(2)}) collective-permute-start(bf16[2064,128]{1,0:T(8,128)(2,1)} %get-tuple-element.25), channel_id=1, source_target_pairs={{0,8},{8,16},{16,24},{1,9},{9,17},{17,25},{2,10},{10,18},{18,26},{... | collective-permute-start | bytes 1585160 | tf_op jit(solution)/shard_map/ppermute | solution.py:46
  69.0 21.4 %copy-start.12 = (bf16[2064,128]{1,0:T(8,128)(2,1)}, bf16[2064,128]{1,0:T(8,128)(2,1)S(1)}, u32[]{:S(2)}) copy-start(bf16[2064,128]{1,0:T(8,128)(2,1)S(1)} %collective-permute-done.4.g5) | copy-start | bytes 1585156
  69.0 21.4 %collective-permute-start = (bf16[2064,128]{1,0:T(8,128)(2,1)S(1)}, bf16[2064,128]{1,0:T(8,128)(2,1)}, u32[]{:S(2)}, u32[]{:S(2)}) collective-permute-start(bf16[2064,128]{1,0:T(8,128)(2,1)S(1)} %copy-done.10), channel_id=1, source_target_pairs={{0,32},{32,64},{64,96},{1,33},{33,65},{65,97},{2,34},{34,66},{66,9... | collective-permute-start | bytes 1585160 | tf_op jit(solution)/shard_map/ppermute | solution.py:46
  73.3 17.1 %copy-start.11 = (bf16[2064,128]{1,0:T(8,128)(2,1)}, bf16[2064,128]{1,0:T(8,128)(2,1)S(1)}, u32[]{:S(2)}) copy-start(bf16[2064,128]{1,0:T(8,128)(2,1)S(1)} %collective-permute-done.3.g2) | copy-start | bytes 1585156
  73.3 16.3 %collective-permute-start.1 = (bf16[2064,128]{1,0:T(8,128)(2,1)}, bf16[2064,128]{1,0:T(8,128)(2,1)S(1)}, u32[]{:S(2)}, u32[]{:S(2)}) collective-permute-start(bf16[2064,128]{1,0:T(8,128)(2,1)} %get-tuple-element.24), channel_id=1, source_target_pairs={{32,0},{64,32},{96,64},{33,1},{65,33},{97,65},{34,2},{66,34},{98,6... | collective-permute-start | bytes 1585160 | tf_op jit(solution)/shard_map/ppermute | solution.py:46
  81.3 8.3 %copy-start.14 = (bf16[2064,128]{1,0:T(8,128)(2,1)}, bf16[2064,128]{1,0:T(8,128)(2,1)S(1)}, u32[]{:S(2)}) copy-start(bf16[2064,128]{1,0:T(8,128)(2,1)S(1)} %collective-permute-done.2.g3) | copy-start | bytes 1585156
  89.6 0.8 copy-start.15
  89.6 0.9 copy-start.16
  90.4 0.9 copy-start
  91.3 51.9 %slice-start = ((s32[1,224]{1,0:T(1,128)}), s32[1,32]{1,0:T(1,128)S(1)}, s32[]{:S(2)}) async-start(s32[1,224]{1,0:T(1,128)} %param.15), calls=%async_computation.1 | async-start | bytes 1024 | tf_op jit(solution)/shard_map/slice | solution.py:543
  126.8 14.9 %collective-permute-start.10 = (bf16[32,32,128]{2,1,0:T(8,128)(2,1)}, bf16[32,32,128]{2,1,0:T(8,128)(2,1)S(1)}, u32[]{:S(2)}, u32[]{:S(2)}) collective-permute-start(bf16[32,32,128]{2,1,0:T(8,128)(2,1)} %get-tuple-element.37), channel_id=1, source_target_pairs={{0,8},{8,16},{16,24},{1,9},{9,17},{17,25},{2,10},{10,18},{18,26},{... | collective-permute-start | bytes 786440 | tf_op jit(solution)/shard_map/ppermute | solution.py:46
  130.7 13.1 %collective-permute-start.11 = (bf16[32,32,128]{2,1,0:T(8,128)(2,1)}, bf16[32,32,128]{2,1,0:T(8,128)(2,1)S(1)}, u32[]{:S(2)}, u32[]{:S(2)}) collective-permute-start(bf16[32,32,128]{2,1,0:T(8,128)(2,1)} %get-tuple-element.38), channel_id=1, source_target_pairs={{8,0},{16,8},{24,16},{9,1},{17,9},{25,17},{10,2},{18,10},{26,18},{... | collective-permute-start | bytes 786440 | tf_op jit(solution)/shard_map/ppermute | solution.py:46
  133.4 10.4 %collective-permute-start.12 = (bf16[32,32,128]{2,1,0:T(8,128)(2,1)}, bf16[32,32,128]{2,1,0:T(8,128)(2,1)S(1)}, u32[]{:S(2)}, u32[]{:S(2)}) collective-permute-start(bf16[32,32,128]{2,1,0:T(8,128)(2,1)} %get-tuple-element.39), channel_id=1, source_target_pairs={{0,1},{1,2},{2,3},{3,4},{4,5},{5,6},{6,7},{8,9},{9,10},{10,11},{11... | collective-permute-start | bytes 786440 | tf_op jit(solution)/shard_map/ppermute | solution.py:46
  135.4 8.5 %collective-permute-start.13 = (bf16[32,32,128]{2,1,0:T(8,128)(2,1)}, bf16[32,32,128]{2,1,0:T(8,128)(2,1)S(1)}, u32[]{:S(2)}, u32[]{:S(2)}) collective-permute-start(bf16[32,32,128]{2,1,0:T(8,128)(2,1)} %get-tuple-element.40), channel_id=1, source_target_pairs={{1,0},{2,1},{3,2},{4,3},{5,4},{6,5},{7,6},{9,8},{10,9},{11,10},{12... | collective-permute-start | bytes 786440 | tf_op jit(solution)/shard_map/ppermute | solution.py:46
  139.0 9.2 %collective-permute-start.8 = (bf16[32,32,128]{2,1,0:T(8,128)(2,1)}, bf16[32,32,128]{2,1,0:T(8,128)(2,1)S(1)}, u32[]{:S(2)}, u32[]{:S(2)}) collective-permute-start(bf16[32,32,128]{2,1,0:T(8,128)(2,1)} %get-tuple-element.35), channel_id=1, source_target_pairs={{0,32},{32,64},{64,96},{1,33},{33,65},{65,97},{2,34},{34,66},{66,9... | collective-permute-start | bytes 786440 | tf_op jit(solution)/shard_map/ppermute | solution.py:46
  141.8 10.5 %copy-start.1 = (bf16[32,32,128]{2,1,0:T(8,128)(2,1)}, bf16[32,32,128]{2,1,0:T(8,128)(2,1)S(1)}, u32[]{:S(2)}) copy-start(bf16[32,32,128]{2,1,0:T(8,128)(2,1)S(1)} %collective-permute-done.10.r2) | copy-start | bytes 786436
  141.8 10.5 %collective-permute-start.9 = (bf16[32,32,128]{2,1,0:T(8,128)(2,1)}, bf16[32,32,128]{2,1,0:T(8,128)(2,1)S(1)}, u32[]{:S(2)}, u32[]{:S(2)}) collective-permute-start(bf16[32,32,128]{2,1,0:T(8,128)(2,1)} %get-tuple-element.36), channel_id=1, source_target_pairs={{32,0},{64,32},{96,64},{33,1},{65,33},{97,65},{34,2},{66,34},{98,6... | collective-permute-start | bytes 786440 | tf_op jit(solution)/shard_map/ppermute | solution.py:46
  143.8 8.4 %copy-start.2 = (bf16[32,32,128]{2,1,0:T(8,128)(2,1)}, bf16[32,32,128]{2,1,0:T(8,128)(2,1)S(1)}, u32[]{:S(2)}) copy-start(bf16[32,32,128]{2,1,0:T(8,128)(2,1)S(1)} %collective-permute-done.11.r3) | copy-start | bytes 786436
  143.8 8.4 %copy-start.3 = (bf16[32,32,128]{2,1,0:T(8,128)(2,1)}, bf16[32,32,128]{2,1,0:T(8,128)(2,1)S(1)}, u32[]{:S(2)}) copy-start(bf16[32,32,128]{2,1,0:T(8,128)(2,1)S(1)} %collective-permute-done.12.r4) | copy-start | bytes 786436
  143.9 8.4 %copy-start.4 = (bf16[32,32,128]{2,1,0:T(8,128)(2,1)}, bf16[32,32,128]{2,1,0:T(8,128)(2,1)S(1)}, u32[]{:S(2)}) copy-start(bf16[32,32,128]{2,1,0:T(8,128)(2,1)S(1)} %collective-permute-done.13.r5) | copy-start | bytes 786436
  148.2 4.1 %copy-start.5 = (bf16[32,32,128]{2,1,0:T(8,128)(2,1)}, bf16[32,32,128]{2,1,0:T(8,128)(2,1)S(1)}, u32[]{:S(2)}) copy-start(bf16[32,32,128]{2,1,0:T(8,128)(2,1)S(1)} %collective-permute-done.8.r0) | copy-start | bytes 786436
  (1 other events, 0.7 us)

commit v3 on v2

v3 whole, which is shorter than its diff:
```python
import jax
import jax.numpy as jnp
from jax import lax
from jax.experimental import pallas as pl
from jax.experimental.pallas import tpu as pltpu
from jax.sharding import PartitionSpec as P


B = 64
NBR = 7
CAP = 6
FAR = 2
NEAR = CAP - FAR
GCAP = 64
UCAP = 32
U_DEV = 224
CE_DEV = 64
ROWS = 256
LAYERS = 8
HALF = 32
LANES = 128
AXES = ("gx", "gy", "gz")
SENT = LAYERS * FAR + 2 * NEAR
SENT_PAD = 32
ROW_LEN = 3 * B + HALF
GHOST_LEN = GCAP * HALF
EXTRA = 16
TABLE = ROWS + 6 * GCAP
VMEM_LIMIT = 62 * 1024 * 1024
PITCH = HALF + 1
bf16 = jnp.bfloat16
f32 = jnp.float32


def lower_lanes(shape):
    return lax.broadcasted_iota(jnp.int32, shape, len(shape) - 1) < B


def swap_lanes(v):
    return jnp.concatenate([v[:, B:], v[:, :B]], axis=1)


def shifted(value, axis, by):
    devices = lax.axis_size(axis)
    pairs = [(i, i + by) for i in range(devices) if 0 <= i + by < devices]
    return lax.ppermute(value, axis, pairs)


NEAR_AT = GHOST_LEN + EXTRA
SEND_LEN = [NEAR_AT] * 4 + [NEAR_AT + NEAR * ROW_LEN] * 2
P_PARTS = 4
X_PARTS = 8
NT = (((1,), (1,)), ((), ()))


def pack_kernel(
    layer, lists, owner, touched, prolong_hbm, blocks, halves_out, o0, o1, o2, o3, o4, o5, far_out,
    prolong, halves, v0, v1, v2, v3, v4, v5, far, work, planes, strip0, strip1, strip2, strip3,
    in_sem, plane_sem, out_sem,
):
    sends, outs = (v0, v1, v2, v3, v4, v5), (o0, o1, o2, o3, o4, o5)
    strips = (strip0, strip1, strip2, strip3)
    count, deep = ROWS // P_PARTS, B // X_PARTS

    def prolong_copy(n):
        rows = pl.ds(n * count, count)
        return pltpu.make_async_copy(prolong_hbm.at[rows], prolong.at[rows], in_sem.at[n])

    def plane_copy(n):
        some = pl.ds(n * deep, deep)
        return pltpu.make_async_copy(blocks.at[some], planes.at[some], plane_sem.at[n])

    for n in range(P_PARTS):
        prolong_copy(n).start()
    for n in range(X_PARTS):
        plane_copy(n).start()

    square = (ROWS, ROWS)
    peer = lax.rem(owner[...], LAYERS)
    member = lax.broadcasted_iota(jnp.int32, (16, ROWS), 0) == peer
    earlier = (
        lax.broadcasted_iota(jnp.int32, square, 0) < lax.broadcasted_iota(jnp.int32, square, 1)
    )
    before = jnp.dot(
        member.astype(f32).astype(bf16),
        earlier.astype(f32).astype(bf16),
        preferred_element_type=f32,
    )
    rank = jnp.sum(jnp.where(member, before, 0.0), axis=0, keepdims=True).astype(jnp.int32)
    near_slot = jnp.where(peer > layer[0], LAYERS * FAR, LAYERS * FAR + NEAR) + rank - FAR
    slot = jnp.where(rank < FAR, peer * FAR + rank, near_slot)
    slot = jnp.where(peer == layer[0], -1, slot)
    sent = lax.broadcasted_iota(jnp.int32, (SENT_PAD, ROWS), 0) == slot
    picks = sent.astype(f32).astype(bf16)

    low = lower_lanes((16, LANES))

    def group(g, carry):
        rows = pl.ds(pl.multiple_of(g * 16, 16), 16)
        for s in range(16):
            near = prolong[rows, s * LANES : (s + 1) * LANES].astype(f32)
            far_half = prolong[rows, (s + 16) * LANES : (s + 17) * LANES].astype(f32)
            even = jnp.where(low, near, pltpu.roll(far_half, B, 1))
            odd = jnp.where(low, pltpu.roll(near, B, 1), far_half)
            work[pl.ds(2 * s, 16, stride=PITCH), :] = even
            work[pl.ds(2 * s + 1, 16, stride=PITCH), :] = odd
        for e in range(16):
            halves[pl.ds(pl.multiple_of((g * 16 + e) * HALF, HALF), HALF), :] = work[
                e * PITCH : e * PITCH + HALF, :
            ].astype(bf16)
        return carry

    for n in range(P_PARTS):
        prolong_copy(n).wait()
        lax.fori_loop(n * count // 16, (n + 1) * count // 16, group, 0)
    out_copies = [pltpu.make_async_copy(halves, halves_out, out_sem.at[6])]
    out_copies[0].start()

    top = touched[:, :LANES]
    rest = jnp.concatenate(
        [touched[:, LANES:], jnp.zeros((1, 2 * LANES - U_DEV), jnp.int32)], axis=1
    )
    at = lax.broadcasted_iota(jnp.int32, (EXTRA, LANES), 0)
    extra = jnp.where(at == 0, top, jnp.where(at == 1, rest, 0)).astype(f32).astype(bf16)

    def pick(q, carry):
        for j in range(6):
            row = lists[j, 0, q]
            sends[j][pl.ds(pl.multiple_of(q * HALF, HALF), HALF), :] = halves[
                pl.ds(pl.multiple_of(row * HALF, HALF), HALF), :
            ]
        return carry

    lax.fori_loop(0, GCAP, pick, 0, unroll=4)
    for j in range(6):
        sends[j][GHOST_LEN:NEAR_AT, :] = extra
        out_copies.append(pltpu.make_async_copy(sends[j], outs[j], out_sem.at[j]))
        if j < 4:
            out_copies[-1].start()

    def some_planes(n, carry):
        plane_copy(n).wait()
        for d in range(deep):
            a = n * deep + d
            got = lax.dot_general(picks, planes[a], NT, preferred_element_type=f32)
            rows = pl.ds(a * PITCH, SENT_PAD)
            for c in range(3):
                strips[c][rows, :] = got[:, c * LANES : (c + 1) * LANES]
            strips[3][rows, :B] = got[:, 3 * LANES :]
        return carry

    lax.fori_loop(0, X_PARTS, some_planes, 0)
    for r in range(SENT):
        if r < LAYERS * FAR:
            out, base = far, r * ROW_LEN
        elif r < LAYERS * FAR + NEAR:
            out, base = v4, NEAR_AT + (r - LAYERS * FAR) * ROW_LEN
        else:
            out, base = v5, NEAR_AT + (r - LAYERS * FAR - NEAR) * ROW_LEN
        got = [strip[pl.ds(r, B, stride=PITCH), :].astype(bf16) for strip in strips]
        for c in range(3):
            out[base + c * B : base + (c + 1) * B, :] = got[c]
        out[base + 3 * B : base + ROW_LEN, :] = jnp.concatenate(
            [got[3][:HALF, :B], got[3][HALF:, :B]], axis=1
        )
    out_copies.append(pltpu.make_async_copy(far, far_out, out_sem.at[7]))
    for copy in out_copies[5:]:
        copy.start()
    for copy in out_copies:
        copy.wait()


def pack(layer, lists, owner, touched, prolong, blocks):
    hbm = pl.BlockSpec(memory_space=pl.ANY)
    shapes = [(ROWS * HALF, LANES)] + [(n, LANES) for n in SEND_LEN]
    shapes += [(LAYERS * FAR * ROW_LEN, LANES)]
    return pl.pallas_call(
        pack_kernel,
        grid_spec=pltpu.PrefetchScalarGridSpec(
            num_scalar_prefetch=2,
            grid=(1,),
            in_specs=[
                pl.BlockSpec((1, ROWS), lambda i, *s: (0, 0)),
                pl.BlockSpec((1, U_DEV), lambda i, *s: (0, 0)),
                hbm,
                hbm,
            ],
            out_specs=[hbm] * 8,
            scratch_shapes=[pltpu.VMEM((ROWS, B * B), bf16)]
            + [pltpu.VMEM(shape, bf16) for shape in shapes]
            + [
                pltpu.VMEM((16 * PITCH, LANES), f32),
                pltpu.VMEM((B, NBR * B, ROWS), bf16),
            ]
            + [pltpu.VMEM((B * PITCH, LANES), f32)] * 4
            + [
                pltpu.SemaphoreType.DMA((P_PARTS,)),
                pltpu.SemaphoreType.DMA((X_PARTS,)),
                pltpu.SemaphoreType.DMA((8,)),
            ],
        ),
        out_shape=[jax.ShapeDtypeStruct(shape, bf16) for shape in shapes],
        compiler_params=pltpu.CompilerParams(vmem_limit_bytes=VMEM_LIMIT),
        cost_estimate=pl.CostEstimate(
            flops=2_000_000_000, transcendentals=0, bytes_accessed=23_000_000
        ),
        name="pack",
    )(layer, lists, owner, touched, prolong, blocks)


STEPS = 4
A_STEP = B // STEPS
R_STEP = ROWS // STEPS
TOTAL = ROWS
SPAN = TOTAL + 1


def left_kernel(arrival, blocks, halves, left, table0, table1, transposed, picks):
    j, step = pl.program_id(0), pl.program_id(1)
    tables = (table0, table1)
    square = (ROWS, ROWS)

    @pl.when((j == 0) & (step == 0))
    def _():
        eye = (
            lax.broadcasted_iota(jnp.int32, (B, B), 0)
            == lax.broadcasted_iota(jnp.int32, (B, B), 1)
        ).astype(bf16)

        low = lower_lanes((B, LANES))

        def turn(n, carry):
            tiles = []
            for q in range(4):
                h = halves[pl.ds(pl.multiple_of((n * 4 + q) * HALF, HALF), HALF), :]
                tiles += [h[:, :B], h[:, B:]]
            got = lax.dot_general(
                eye,
                jnp.concatenate(tiles, axis=0),
                (((1,), (1,)), ((), ())),
                preferred_element_type=f32,
            )
            for q in range(4):
                pair = got[:, (q // 2) * LANES : (q // 2 + 1) * LANES]
                mine = low if q % 2 == 0 else jnp.logical_not(low)
                transposed[n * 4 + q] = jnp.where(mine, pair, 0.0).astype(bf16)
            return carry

        lax.fori_loop(0, ROWS // 4, turn, 0, unroll=8)

        down_rows = lax.broadcasted_iota(jnp.int32, square, 0)
        along = lax.broadcasted_iota(jnp.int32, square, 1)
        taken = (down_rows == arrival[...]).astype(f32).astype(bf16)
        unit = (down_rows == along).astype(f32).astype(bf16)
        picks[...] = lax.dot_general(unit, taken, NT, preferred_element_type=f32).astype(bf16)

    @pl.when(step < STEPS)
    def _():
        def relay(n, carry):
            rows = pl.ds((step * A_STEP + n) * SPAN, TOTAL)
            got = lax.dot_general(
                picks[...], blocks[n], (((1,), (1,)), ((), ())), preferred_element_type=f32
            )
            table0[rows, :] = got[:, :LANES]
            table1[rows, :] = got[:, LANES:]
            return carry

        lax.fori_loop(0, A_STEP, relay, 0, unroll=8)

    @pl.when(step >= STEPS)
    def _():
        keep = lower_lanes((B, LANES)) | (j == 0)

        def multiply(n, carry):
            i = (step - STEPS) * R_STEP + 2 * n
            rows = [
                jnp.concatenate(
                    [t[pl.ds(i + q, B, stride=SPAN), :].astype(bf16) for t in tables], axis=1
                )
                for q in range(2)
            ]
            pairs = jnp.concatenate([transposed[i], transposed[i + 1]], axis=0)
            got = jnp.dot(pairs, jnp.concatenate(rows, axis=0), preferred_element_type=f32)
            for q in range(2):
                part = got[q * B : (q + 1) * B]
                left[0, 2 * n + q] = part[:, :LANES].astype(bf16)
                left[1, 2 * n + q] = jnp.where(keep, part[:, LANES:], 0.0).astype(bf16)
            return carry

        lax.fori_loop(0, R_STEP // 2, multiply, 0, unroll=16)


def make_left(arrival, blocks, halves):
    whole = lambda shape: pl.BlockSpec(shape, lambda j, s: (0,) * len(shape))
    return pl.pallas_call(
        left_kernel,
        grid=(2, 2 * STEPS),
        in_specs=[
            whole((1, ROWS)),
            pl.BlockSpec(
                (A_STEP, 2 * LANES, ROWS), lambda j, s: (jnp.minimum(s, STEPS - 1), j, 0)
            ),
            whole((ROWS * HALF, LANES)),
        ],
        out_specs=pl.BlockSpec(
            (2, R_STEP, B, LANES), lambda j, s: (j, jnp.maximum(s - STEPS, 0), 0, 0)
        ),
        out_shape=jax.ShapeDtypeStruct((4, ROWS, B, LANES), bf16),
        scratch_shapes=[
            pltpu.VMEM((B * SPAN, LANES), f32),
            pltpu.VMEM((B * SPAN, LANES), f32),
            pltpu.VMEM((ROWS, B, LANES), bf16),
            pltpu.VMEM((ROWS, ROWS), bf16),
        ],
        compiler_params=pltpu.CompilerParams(
            vmem_limit_bytes=VMEM_LIMIT, dimension_semantics=("arbitrary", "arbitrary")
        ),
        cost_estimate=pl.CostEstimate(
            flops=12_000_000_000, transcendentals=0, bytes_accessed=60_000_000
        ),
        name="left",
    )(arrival, blocks, halves)


PARTS = 8
UNROLL = 16
TALL = B + 1


def sums_kernel(
    moved_rows, columns, targets, left_hbm, halves, g0, g1, g2, g3, g4, g5, far,
    own, fine, s0, s1, s2, s3, s4, s5,
    left, packed, double, acc0, acc1, moved, left_sem, table_sem, moved_sem,
):
    ghosts = (g0, g1, g2, g3, g4, g5)
    sends = (s0, s1, s2, s3, s4, s5)
    totals = (acc0, acc1)
    part = ROWS // PARTS
    table_copies = [pltpu.make_async_copy(halves, packed.at[: ROWS * HALF, :], table_sem.at[0])]
    for j in range(6):
        first = (ROWS + j * GCAP) * HALF
        table_copies.append(
            pltpu.make_async_copy(
                ghosts[j].at[:GHOST_LEN, :],
                packed.at[first : first + GHOST_LEN, :],
                table_sem.at[1 + j],
            )
        )
    first, second = LAYERS * FAR * ROW_LEN, (LAYERS * FAR + NEAR) * ROW_LEN
    moved_copies = [
        pltpu.make_async_copy(far, moved.at[:first, :], moved_sem.at[0]),
        pltpu.make_async_copy(g5.at[NEAR_AT:, :], moved.at[first:second, :], moved_sem.at[1]),
        pltpu.make_async_copy(g4.at[NEAR_AT:, :], moved.at[second:, :], moved_sem.at[2]),
    ]

    def left_copy(n):
        rows = pl.ds(n * part, part)
        return pltpu.make_async_copy(left_hbm.at[:, rows], left.at[:, rows], left_sem.at[n])

    for copy in table_copies + moved_copies:
        copy.start()
    for n in range(PARTS):
        left_copy(n).start()

    def clear(u, carry):
        for total in totals:
            total[pl.ds(u * TALL, TALL), :] = jnp.zeros((TALL, LANES), f32)
        return carry

    lax.fori_loop(0, U_DEV + 1, clear, 0, unroll=5)

    def expand(c, carry):
        h = packed[pl.ds(pl.multiple_of(c * HALF, HALF), HALF), :]
        turned = swap_lanes(h)
        double[c, 0:HALF, :] = jnp.concatenate([h[:, :B], turned[:, B:]], axis=1)
        double[c, HALF:, :] = jnp.concatenate([turned[:, :B], h[:, B:]], axis=1)
        return carry

    table_copies[0].wait()
    lax.fori_loop(0, ROWS, expand, 0, unroll=8)
    for copy in table_copies[1:]:
        copy.wait()
    lax.fori_loop(ROWS, TABLE, expand, 0, unroll=8)
    for copy in moved_copies:
        copy.wait()

    def arrive(s, carry):
        block = double[jnp.maximum(moved_rows[0, s], 0), :, :][:, :B]
        base = pl.multiple_of(s * ROW_LEN, HALF)
        h = moved[pl.ds(base + 3 * B, HALF), :]
        chunks = [moved[pl.ds(base + c * B, B), :] for c in range(3)]
        chunks.append(jnp.concatenate([h[:, :B], h[:, B:]], axis=0))
        got = lax.dot_general(
            block, jnp.concatenate(chunks, axis=1), (((0,), (0,)), ((), ())),
            preferred_element_type=f32,
        ).astype(bf16)
        for c in range(3):
            left[c, ROWS + s] = got[:, c * LANES : (c + 1) * LANES]
        left[3, ROWS + s] = jnp.concatenate(
            [got[:, 3 * LANES :], jnp.zeros((B, B), bf16)], axis=1
        )
        return carry

    lax.fori_loop(0, SENT, arrive, 0, unroll=4)

    zero = jnp.zeros((B, LANES), bf16)

    def row(i, n, valid):
        cols = [columns[k, n] for k in range(NBR)]
        slots_of = [
            jnp.where((cols[k] >= 0) & valid, targets[k, n], U_DEV) for k in range(NBR)
        ]
        for quad in range(2):
            some = cols[4 * quad : 4 * quad + 4]
            slots = slots_of[4 * quad : 4 * quad + 4]
            tiles = [double[jnp.maximum(col, 0)] for col in some]
            tiles += [zero] * (4 - len(tiles))
            upper = jnp.concatenate([tiles[0][:, :B], tiles[2][:, B:]], axis=1)
            lower = jnp.concatenate([tiles[1][:, :B], tiles[3][:, B:]], axis=1)
            weights = jnp.concatenate(
                [
                    jnp.concatenate([upper, zero], axis=1),
                    jnp.concatenate([zero, lower], axis=1),
                ],
                axis=0,
            )
            rows = jnp.concatenate([left[2 * quad, i], left[2 * quad + 1, i]], axis=0)
            got = jnp.dot(rows, weights, preferred_element_type=f32)
            for side in range(2):
                for part in range(2):
                    k = side + 2 * part
                    if k < len(some):
                        first = side * LANES + part * B
                        lanes = slice(part * B, (part + 1) * B)
                        value = got[part * B : (part + 1) * B, first : first + B]
                        totals[side][pl.ds(slots[k] * TALL, B), lanes] += value

    def some_rows(n, carry):
        for r in range(UNROLL):
            row(n * UNROLL + r, n * UNROLL + r, True)
        return carry

    def one_part(n, carry):
        left_copy(n).wait()
        lax.fori_loop(n * (part // UNROLL), (n + 1) * (part // UNROLL), some_rows, 0)
        return carry

    lax.fori_loop(0, PARTS, one_part, 0)

    def more_rows(n, carry):
        for r in range(8):
            source = moved_rows[0, n * 8 + r]
            row(ROWS + n * 8 + r, jnp.maximum(source, 0), source >= 0)
        return carry

    lax.fori_loop(0, SENT // 8, more_rows, 0)
    low = lower_lanes((16, LANES))

    def summed(u, b):
        rows = [pl.ds((u + 8 * n) * TALL + b, 8, stride=TALL) for n in range(2)]
        return jnp.concatenate([acc0[r, :] + acc1[r, :] for r in rows], axis=0)

    for v in range(7):
        for half in range(2):
            u, at = v * UCAP + half * 16, slice(half * 16, half * 16 + 16)

            def gather(s, carry):
                a, b = summed(u, 2 * s), summed(u, 2 * s + 1)
                value = jnp.where(low, a, b) + pltpu.roll(jnp.where(low, b, a), B, 1)
                lanes = pl.ds(pl.multiple_of(s * LANES, LANES), LANES)
                coarse = value.astype(bf16)
                if v == 0:
                    own[at, lanes] = coarse
                    fine[at, lanes] = (value - coarse.astype(f32)).astype(bf16)
                else:
                    sends[v - 1][at, lanes] = coarse
                return carry

            lax.fori_loop(0, HALF, gather, 0, unroll=8)


def make_sums(moved_rows, columns, targets, left, halves, ghosts, far):
    hbm = pl.BlockSpec(memory_space=pl.ANY)
    return pl.pallas_call(
        sums_kernel,
        grid_spec=pltpu.PrefetchScalarGridSpec(
            num_scalar_prefetch=3,
            grid=(1,),
            in_specs=[hbm] * 9,
            out_specs=[pl.BlockSpec((UCAP, B * B), lambda i, *s: (0, 0))] * 8,
            scratch_shapes=[
                pltpu.VMEM((4, ROWS + SENT, B, LANES), bf16),
                pltpu.VMEM((TABLE * HALF, LANES), bf16),
                pltpu.VMEM((TABLE, B, LANES), bf16),
            ]
            + [pltpu.VMEM(((U_DEV + 1) * TALL, LANES), f32)] * 2
            + [
                pltpu.VMEM((SENT * ROW_LEN, LANES), bf16),
                pltpu.SemaphoreType.DMA((PARTS,)),
                pltpu.SemaphoreType.DMA((7,)),
                pltpu.SemaphoreType.DMA((3,)),
            ],
        ),
        out_shape=[jax.ShapeDtypeStruct((UCAP, B * B), bf16)] * 8,
        compiler_params=pltpu.CompilerParams(vmem_limit_bytes=VMEM_LIMIT),
        cost_estimate=pl.CostEstimate(
            flops=8_000_000_000, transcendentals=0, bytes_accessed=30_000_000
        ),
        name="sums",
    )(moved_rows, columns, targets, left, halves, *ghosts, far)


def final_kernel(
    touched, own, fine, r0, r1, r2, r3, r4, r5, g0, g1, g2, g3, g4, g5, out,
    stack, numbers, sem, number_sem,
):
    parts = (own, r0, r1, r2, r3, r4, r5, fine)
    ghosts = (g0, g1, g2, g3, g4, g5)
    copies = [
        pltpu.make_async_copy(
            ghosts[f ^ 1].at[GHOST_LEN:NEAR_AT, :], numbers.at[f], number_sem.at[f]
        )
        for f in range(6)
    ]
    copies += [
        pltpu.make_async_copy(parts[v], stack.at[v * UCAP : (v + 1) * UCAP, :], sem.at[v])
        for v in range(8)
    ]
    for copy in copies:
        copy.start()
    lane = lax.broadcasted_iota(jnp.int32, (1, LANES), 1) // UCAP
    wide = touched[...]
    for copy in copies:
        copy.wait()
    given = [numbers[f].astype(f32) for f in range(6)]
    first = wide[:, :LANES].astype(f32)
    for f in range(3):
        first = jnp.where(lane == f + 1, given[f][0:1, :], first)
    second = jnp.concatenate([wide[:, :UCAP]] * 4, axis=1).astype(f32)
    for f in range(3, 6):
        second = jnp.where(lane == f - 3, given[f][1:2, :], second)
    row = lax.broadcasted_iota(jnp.int32, (CE_DEV, LANES), 0).astype(f32)
    select = jnp.concatenate(
        [(row == first).astype(f32), (row == second).astype(f32)], axis=1
    ).astype(bf16)
    for n in range(8):
        lanes = slice(n * 4 * LANES, (n + 1) * 4 * LANES)
        out[:, lanes] = jnp.dot(select, stack[:, lanes], preferred_element_type=f32)


def make_final(touched, own, fine, got, ghosts):
    hbm = pl.BlockSpec(memory_space=pl.ANY)
    return pl.pallas_call(
        final_kernel,
        grid=(1,),
        in_specs=[pl.BlockSpec((1, U_DEV), lambda i: (0, 0))] + [hbm] * 14,
        out_specs=pl.BlockSpec((CE_DEV, B * B), lambda i: (0, 0)),
        scratch_shapes=[
            pltpu.VMEM((8 * UCAP, B * B), bf16),
            pltpu.VMEM((6, EXTRA, LANES), bf16),
            pltpu.SemaphoreType.DMA((8,)),
            pltpu.SemaphoreType.DMA((6,)),
        ],
        out_shape=jax.ShapeDtypeStruct((CE_DEV, B * B), f32),
        compiler_params=pltpu.CompilerParams(vmem_limit_bytes=VMEM_LIMIT),
        name="final",
    )(touched, own, fine, *got, *ghosts)


def neighbour_shift(value, facing):
    axis = AXES[facing // 2]
    return shifted(value, axis, 1 - 2 * (facing % 2))


def one_shard(blocks, prolong, new_owner, arrival, columns, targets, ghost_lists, touched):
    own_layer = lax.axis_index("gz")
    planes = jnp.transpose(blocks, (1, 2, 0))
    halves, *outbound, far = pack(
        own_layer[None], jnp.transpose(ghost_lists, (1, 0, 2)), new_owner[None], touched,
        prolong, planes,
    )
    ghosts = []
    for facing in range(6):
        ghosts.append(neighbour_shift(outbound[facing ^ 1], facing ^ 1))
    far_in = lax.all_to_all(
        far.reshape(LAYERS, FAR * ROW_LEN, LANES), "gz", split_axis=0, concat_axis=0, tiled=True
    )
    left = make_left(arrival[None], planes, halves)

    old = jnp.arange(ROWS, dtype=jnp.int32)
    labels = jnp.arange(LAYERS, dtype=jnp.int32)
    ranks = jnp.arange(FAR, dtype=jnp.int32)
    later = FAR + jnp.arange(NEAR, dtype=jnp.int32)
    codes = ROWS + jnp.concatenate(
        [
            (labels[:, None] * CAP + ranks[None, :]).reshape(-1),
            (own_layer - 1) * CAP + later,
            (own_layer + 1) * CAP + later,
        ]
    )
    match = (codes[:, None] == arrival[None, :]) & (codes[:, None] >= ROWS)
    row_of = jnp.sum(jnp.where(match, old[None, :] + 1, 0), axis=1) - 1
    own, fine, *sends = make_sums(
        row_of[None, :], columns.T, targets.T, left, halves, ghosts,
        far_in.reshape(LAYERS * FAR * ROW_LEN, LANES),
    )
    got = [neighbour_shift(sends[facing], facing) for facing in range(6)]
    return make_final(touched, own, fine, got, ghosts)


def solution(mesh):
    return jax.shard_map(
        one_shard,
        mesh=mesh,
        in_specs=(
            P(AXES, None, None),
            P(AXES, None),
            P(AXES),
            P(AXES),
            P(AXES, None),
            P(AXES, None),
            P(AXES, None, None),
            P(AXES, None),
        ),
        out_specs=P(AXES, None),
        check_vma=False,
    )
```

time: 159 us -> 142 us (0.89)
  the two profiles are of different devices: /device:TPU:34 before, /device:TPU:23 now
where the time goes in v3:
time: 142 us; the launch traced here: 141 us
  Pallas kernels  77.7 us (55%)
  starting transfers between devices  39.8 us (28%)
  waiting for transfers between devices  19.7 us (14%)
  local copies, waits for them, and re-layouts  2.74 us (2%)
    ppermute x12, starting transfers between devices, shifted(): return lax.ppermute(value, axis, pairs)  33.8 us
    pallas_call x1, Pallas kernels, make_sums(): pl.pallas_call(sums_kernel, grid_spec=pltpu.PrefetchScalarGridSpec(num_sc...  33.5 us
    pallas_call x1, Pallas kernels, make_left(): pl.pallas_call(left_kernel, grid=(2, 2 * STEPS), in_specs=[whole((1, ROWS...  25.6 us
    ppermute x12, waiting for transfers between devices, shifted(): return lax.ppermute(value, axis, pairs)  19.7 us
    pallas_call x1, Pallas kernels, pack(): pl.pallas_call(pack_kernel, grid_spec=pltpu.PrefetchScalarGridSpec(num_sc...  14.8 us
    all_to_all x1, starting transfers between devices, one_shard(): lax.all_to_all(far.reshape(LAYERS, FAR * ROW_LEN, LANES), 'gz', split_axi...  5.99 us
    pallas_call x1, Pallas kernels, make_final(): pl.pallas_call(final_kernel, grid=(1,), in_specs=[pl.BlockSpec((1, U_DEV)...  3.82 us
  transfers between devices with their start and end apart: 13, of which 3 were waited for; matrix products, arithmetic and copies ran while one was open for 1% of the time, Pallas kernels for 18%

profile of v3, /device:TPU:23, one launch (start us, length us, event | category | flops | bytes accessed | tf_op | source)
XLA Modules:
  0.0 141.2 jit_solution(7049209487444034779)
XLA Ops:
  0.0 14.8 %pack.1 = (bf16[8192,128]{1,0:T(8,128)(2,1)}, bf16[2064,128]{1,0:T(8,128)(2,1)}, bf16[2064,128]{1,0:T(8,128)(2,1)}, bf16[2064,128]{1,0:T(8,128)(2,1)}, bf16[2064...) custom-call(s32[1]{0:T(128)} %bitcast.5.layer, ...), custom_call_target="tpu_custom_call" | custom-call | flops 2000000000 | bytes 23000000 | tf_op jit(solution)/shard_map/pack/pallas_call | solution.py:177
  14.8 6.0 %all-to-all-start = ((bf16[8,448,128]{2,1,0:T(8,128)(2,1)}), bf16[8,448,128]{2,1,0:T(8,128)(2,1)S(1)}, u32[]{:S(2)}, u32[]{:S(2)}) async-start(bf16[8,448,128]{2,1,0:T(8,128)(2,1)} %bitcast.14), calls=%async_computation | async-start | bytes 1835008 | tf_op jit(solution)/shard_map/all_to_all | solution.py:585
  20.8 2.1 %collective-permute-start = (bf16[2064,128]{1,0:T(8,128)(2,1)}, bf16[2064,128]{1,0:T(8,128)(2,1)}, u32[]{:S(2)}, u32[]{:S(2)}) collective-permute-start(bf16[2064,128]{1,0:T(8,128)(2,1)} %get-tuple-element.22), channel_id=1, source_target_pairs={{32,0},{64,32},{96,64},{33,1},{65,33},{97,65},{34,2},{66,34},{98,6... | collective-permute-start | bytes 1585160 | tf_op jit(solution)/shard_map/ppermute | solution.py:46
  22.9 4.0 %collective-permute-start.1 = (bf16[2064,128]{1,0:T(8,128)(2,1)}, bf16[2064,128]{1,0:T(8,128)(2,1)}, u32[]{:S(2)}, u32[]{:S(2)}) collective-permute-start(bf16[2064,128]{1,0:T(8,128)(2,1)} %get-tuple-element.23), channel_id=1, source_target_pairs={{0,32},{32,64},{64,96},{1,33},{33,65},{65,97},{2,34},{34,66},{66,9... | collective-permute-start | bytes 1585160 | tf_op jit(solution)/shard_map/ppermute | solution.py:46
  26.9 3.2 %collective-permute-start.2 = (bf16[2064,128]{1,0:T(8,128)(2,1)}, bf16[2064,128]{1,0:T(8,128)(2,1)}, u32[]{:S(2)}, u32[]{:S(2)}) collective-permute-start(bf16[2064,128]{1,0:T(8,128)(2,1)} %get-tuple-element.24), channel_id=1, source_target_pairs={{8,0},{16,8},{24,16},{9,1},{17,9},{25,17},{10,2},{18,10},{26,18},{... | collective-permute-start | bytes 1585160 | tf_op jit(solution)/shard_map/ppermute | solution.py:46
  30.1 2.7 %collective-permute-start.4 = (bf16[2960,128]{1,0:T(8,128)(2,1)}, bf16[2960,128]{1,0:T(8,128)(2,1)S(1)}, u32[]{:S(2)}, u32[]{:S(2)}) collective-permute-start(bf16[2960,128]{1,0:T(8,128)(2,1)} %get-tuple-element.26), channel_id=1, source_target_pairs={{1,0},{2,1},{3,2},{4,3},{5,4},{6,5},{7,6},{9,8},{10,9},{11,10},{12... | collective-permute-start | bytes 2273288 | tf_op jit(solution)/shard_map/ppermute | solution.py:46
  32.9 3.5 %collective-permute-start.5 = (bf16[2960,128]{1,0:T(8,128)(2,1)}, bf16[2960,128]{1,0:T(8,128)(2,1)}, u32[]{:S(2)}, u32[]{:S(2)}) collective-permute-start(bf16[2960,128]{1,0:T(8,128)(2,1)} %get-tuple-element.27), channel_id=1, source_target_pairs={{0,1},{1,2},{2,3},{3,4},{4,5},{5,6},{6,7},{8,9},{9,10},{10,11},{11... | collective-permute-start | bytes 2273288 | tf_op jit(solution)/shard_map/ppermute | solution.py:46
  36.4 0.0 copy-start.9
  36.4 25.6 %left.1.left_hbm = bf16[4,256,64,128]{3,2,1,0:T(8,128)(2,1)} custom-call(s32[1,256]{1,0:T(1,128)} %bitcast.17, bf16[64,448,256]{2,1,0:T(8,128)(2,1)} %bitcast.12, bf16[8192,128]{1,0:T(8,128)(2,1)} %get-tuple-element.21.halves), custom_call_target="tpu_custom_call" | custom-call | flops 12000000000 | bytes 60000000 | tf_op jit(solution)/shard_map/left/pallas_call | solution.py:295
  62.0 0.1 iota_add_fusion
  62.1 0.1 add.81
  62.2 0.0 collective-permute-done.g0
  62.2 1.3 collective-permute-start.3
  63.5 0.1 broadcast_compare_fusion
  63.6 0.2 select_reduce_fusion
  63.7 0.6 add_bitcast_fusion.moved_rows
  64.3 13.8 %collective-permute-done.3.g3 = bf16[2064,128]{1,0:T(8,128)(2,1)S(1)} collective-permute-done((bf16[2064,128]{1,0:T(8,128)(2,1)}, bf16[2064,128]{1,0:T(8,128)(2,1)S(1)}, u32[]{:S(2)}, u32[]{:S(2)}) %collective-permute-start.3) | collective-permute-done | bytes 528416 | tf_op jit(solution)/shard_map/ppermute | solution.py:46
  78.1 0.8 copy-done.2
  79.0 0.0 copy-start
  79.0 0.8 copy-done.1
  79.8 0.3 copy-done
  80.1 33.5 %sums.1 = (bf16[32,4096]{1,0:T(8,128)(2,1)}, bf16[32,4096]{1,0:T(8,128)(2,1)}, bf16[32,4096]{1,0:T(8,128)(2,1)}, bf16[32,4096]{1,0:T(8,128)(2,1)}, bf16[32,4096]...) custom-call(s32[1,24]{1,0:T(1,128)} %add_bitcast_fusion.moved_rows, ...), custom_call_target="tpu_custom_call" | custom-call | flops 8000000000 | bytes 30000000 | tf_op jit(solution)/shard_map/sums/pallas_call | solution.py:484
  113.7 1.9 %collective-permute-start.6 = (bf16[32,4096]{1,0:T(8,128)(2,1)}, bf16[32,4096]{1,0:T(8,128)(2,1)S(1)}, u32[]{:S(2)}, u32[]{:S(2)}) collective-permute-start(bf16[32,4096]{1,0:T(8,128)(2,1)} %get-tuple-element.31), channel_id=1, source_target_pairs={{0,32},{32,64},{64,96},{1,33},{33,65},{65,97},{2,34},{34,66},{66,9... | collective-permute-start | bytes 786440 | tf_op jit(solution)/shard_map/ppermute | solution.py:46
  115.6 3.4 %collective-permute-start.7 = (bf16[32,4096]{1,0:T(8,128)(2,1)}, bf16[32,4096]{1,0:T(8,128)(2,1)S(1)}, u32[]{:S(2)}, u32[]{:S(2)}) collective-permute-start(bf16[32,4096]{1,0:T(8,128)(2,1)} %get-tuple-element.32), channel_id=1, source_target_pairs={{32,0},{64,32},{96,64},{33,1},{65,33},{97,65},{34,2},{66,34},{98,6... | collective-permute-start | bytes 786440 | tf_op jit(solution)/shard_map/ppermute | solution.py:46
  119.0 1.3 collective-permute-start.8
  120.3 4.0 %collective-permute-start.9 = (bf16[32,4096]{1,0:T(8,128)(2,1)}, bf16[32,4096]{1,0:T(8,128)(2,1)S(1)}, u32[]{:S(2)}, u32[]{:S(2)}) collective-permute-start(bf16[32,4096]{1,0:T(8,128)(2,1)} %get-tuple-element.34), channel_id=1, source_target_pairs={{8,0},{16,8},{24,16},{9,1},{17,9},{25,17},{10,2},{18,10},{26,18},{... | collective-permute-start | bytes 786440 | tf_op jit(solution)/shard_map/ppermute | solution.py:46
  124.3 4.4 %collective-permute-start.10 = (bf16[32,4096]{1,0:T(8,128)(2,1)}, bf16[32,4096]{1,0:T(8,128)(2,1)S(1)}, u32[]{:S(2)}, u32[]{:S(2)}) collective-permute-start(bf16[32,4096]{1,0:T(8,128)(2,1)} %get-tuple-element.35), channel_id=1, source_target_pairs={{0,1},{1,2},{2,3},{3,4},{4,5},{5,6},{6,7},{8,9},{9,10},{10,11},{11... | collective-permute-start | bytes 786440 | tf_op jit(solution)/shard_map/ppermute | solution.py:46
  128.8 1.9 %collective-permute-start.11 = (bf16[32,4096]{1,0:T(8,128)(2,1)}, bf16[32,4096]{1,0:T(8,128)(2,1)S(1)}, u32[]{:S(2)}, u32[]{:S(2)}) collective-permute-start(bf16[32,4096]{1,0:T(8,128)(2,1)} %get-tuple-element.36), channel_id=1, source_target_pairs={{1,0},{2,1},{3,2},{4,3},{5,4},{6,5},{7,6},{9,8},{10,9},{11,10},{12... | collective-permute-start | bytes 786440 | tf_op jit(solution)/shard_map/ppermute | solution.py:46
  130.7 1.6 %collective-permute-done.10.r4 = bf16[32,4096]{1,0:T(8,128)(2,1)S(1)} collective-permute-done((bf16[32,4096]{1,0:T(8,128)(2,1)}, bf16[32,4096]{1,0:T(8,128)(2,1)S(1)}, u32[]{:S(2)}, u32[]{:S(2)}) %collective-permute-start.10) | collective-permute-done | bytes 262176 | tf_op jit(solution)/shard_map/ppermute | solution.py:46
  132.3 4.3 %collective-permute-done.11.r5 = bf16[32,4096]{1,0:T(8,128)(2,1)S(1)} collective-permute-done((bf16[32,4096]{1,0:T(8,128)(2,1)}, bf16[32,4096]{1,0:T(8,128)(2,1)S(1)}, u32[]{:S(2)}, u32[]{:S(2)}) %collective-permute-start.11) | collective-permute-done | bytes 262176 | tf_op jit(solution)/shard_map/ppermute | solution.py:46
  136.7 0.7 copy-done.8
  137.3 3.8 %final.1 = f32[64,4096]{1,0:T(8,128)} custom-call(s32[1,224]{1,0:T(1,128)} %touched.3, bf16[32,4096]{1,0:T(8,128)(2,1)} %get-tuple-element.29.own, bf16[32,4096]{1,0:T(8,128)(2,1)} %get-tuple-element.30.fine, bf16[32,4096]{1,0:T(8,128)(2,1)} %copy-done.3, bf16[32,4096]{1,0:T(8,128)(2,1)} %copy-done.4, bf16[32,4096]{1,0:T(8,128)(2,1)} %copy-done.5, ...), custom_call_target="tpu_custom_call" | custom-call | tf_op jit(solution)/shard_map/final/pallas_call | solution.py:553
  (26 shorter events, 0.1 us)
Async XLA Ops:
  14.8 64.1 %all-to-all-start = ((bf16[8,448,128]{2,1,0:T(8,128)(2,1)}), bf16[8,448,128]{2,1,0:T(8,128)(2,1)S(1)}, u32[]{:S(2)}, u32[]{:S(2)}) async-start(bf16[8,448,128]{2,1,0:T(8,128)(2,1)} %bitcast.14), calls=%async_computation | async-start | bytes 1835008 | tf_op jit(solution)/shard_map/all_to_all | solution.py:585
  20.8 41.4 %collective-permute-start = (bf16[2064,128]{1,0:T(8,128)(2,1)}, bf16[2064,128]{1,0:T(8,128)(2,1)}, u32[]{:S(2)}, u32[]{:S(2)}) collective-permute-start(bf16[2064,128]{1,0:T(8,128)(2,1)} %get-tuple-element.22), channel_id=1, source_target_pairs={{32,0},{64,32},{96,64},{33,1},{65,33},{97,65},{34,2},{66,34},{98,6... | collective-permute-start | bytes 1585160 | tf_op jit(solution)/shard_map/ppermute | solution.py:46
  22.9 41.5 %collective-permute-start.1 = (bf16[2064,128]{1,0:T(8,128)(2,1)}, bf16[2064,128]{1,0:T(8,128)(2,1)}, u32[]{:S(2)}, u32[]{:S(2)}) collective-permute-start(bf16[2064,128]{1,0:T(8,128)(2,1)} %get-tuple-element.23), channel_id=1, source_target_pairs={{0,32},{32,64},{64,96},{1,33},{33,65},{65,97},{2,34},{34,66},{66,9... | collective-permute-start | bytes 1585160 | tf_op jit(solution)/shard_map/ppermute | solution.py:46
  26.9 37.5 %collective-permute-start.2 = (bf16[2064,128]{1,0:T(8,128)(2,1)}, bf16[2064,128]{1,0:T(8,128)(2,1)}, u32[]{:S(2)}, u32[]{:S(2)}) collective-permute-start(bf16[2064,128]{1,0:T(8,128)(2,1)} %get-tuple-element.24), channel_id=1, source_target_pairs={{8,0},{16,8},{24,16},{9,1},{17,9},{25,17},{10,2},{18,10},{26,18},{... | collective-permute-start | bytes 1585160 | tf_op jit(solution)/shard_map/ppermute | solution.py:46
  30.1 48.0 %collective-permute-start.4 = (bf16[2960,128]{1,0:T(8,128)(2,1)}, bf16[2960,128]{1,0:T(8,128)(2,1)S(1)}, u32[]{:S(2)}, u32[]{:S(2)}) collective-permute-start(bf16[2960,128]{1,0:T(8,128)(2,1)} %get-tuple-element.26), channel_id=1, source_target_pairs={{1,0},{2,1},{3,2},{4,3},{5,4},{6,5},{7,6},{9,8},{10,9},{11,10},{12... | collective-permute-start | bytes 2273288 | tf_op jit(solution)/shard_map/ppermute | solution.py:46
  32.9 46.1 %collective-permute-start.5 = (bf16[2960,128]{1,0:T(8,128)(2,1)}, bf16[2960,128]{1,0:T(8,128)(2,1)}, u32[]{:S(2)}, u32[]{:S(2)}) collective-permute-start(bf16[2960,128]{1,0:T(8,128)(2,1)} %get-tuple-element.27), channel_id=1, source_target_pairs={{0,1},{1,2},{2,3},{3,4},{4,5},{5,6},{6,7},{8,9},{9,10},{10,11},{11... | collective-permute-start | bytes 2273288 | tf_op jit(solution)/shard_map/ppermute | solution.py:46
  36.4 27.1 %copy-start.9 = (s32[256]{0:T(256)S(1)}, s32[256]{0:T(256)}, u32[]{:S(2)}) copy-start(s32[256]{0:T(256)} %param.11) | copy-start | bytes 3076
  62.2 16.0 %collective-permute-start.3 = (bf16[2064,128]{1,0:T(8,128)(2,1)}, bf16[2064,128]{1,0:T(8,128)(2,1)S(1)}, u32[]{:S(2)}, u32[]{:S(2)}) collective-permute-start(bf16[2064,128]{1,0:T(8,128)(2,1)} %get-tuple-element.25), channel_id=1, source_target_pairs={{0,8},{8,16},{16,24},{1,9},{9,17},{17,25},{2,10},{10,18},{18,26},{... | collective-permute-start | bytes 1585160 | tf_op jit(solution)/shard_map/ppermute | solution.py:46
  78.1 0.8 copy-start.2
  79.0 0.9 copy-start.1
  79.0 1.2 copy-start
  113.7 15.1 %collective-permute-start.6 = (bf16[32,4096]{1,0:T(8,128)(2,1)}, bf16[32,4096]{1,0:T(8,128)(2,1)S(1)}, u32[]{:S(2)}, u32[]{:S(2)}) collective-permute-start(bf16[32,4096]{1,0:T(8,128)(2,1)} %get-tuple-element.31), channel_id=1, source_target_pairs={{0,32},{32,64},{64,96},{1,33},{33,65},{65,97},{2,34},{34,66},{66,9... | collective-permute-start | bytes 786440 | tf_op jit(solution)/shard_map/ppermute | solution.py:46
  115.6 15.1 %collective-permute-start.7 = (bf16[32,4096]{1,0:T(8,128)(2,1)}, bf16[32,4096]{1,0:T(8,128)(2,1)S(1)}, u32[]{:S(2)}, u32[]{:S(2)}) collective-permute-start(bf16[32,4096]{1,0:T(8,128)(2,1)} %get-tuple-element.32), channel_id=1, source_target_pairs={{32,0},{64,32},{96,64},{33,1},{65,33},{97,65},{34,2},{66,34},{98,6... | collective-permute-start | bytes 786440 | tf_op jit(solution)/shard_map/ppermute | solution.py:46
  119.0 11.7 %collective-permute-start.8 = (bf16[32,4096]{1,0:T(8,128)(2,1)}, bf16[32,4096]{1,0:T(8,128)(2,1)S(1)}, u32[]{:S(2)}, u32[]{:S(2)}) collective-permute-start(bf16[32,4096]{1,0:T(8,128)(2,1)} %get-tuple-element.33), channel_id=1, source_target_pairs={{0,8},{8,16},{16,24},{1,9},{9,17},{17,25},{2,10},{10,18},{18,26},{... | collective-permute-start | bytes 786440 | tf_op jit(solution)/shard_map/ppermute | solution.py:46
  120.3 10.4 %collective-permute-start.9 = (bf16[32,4096]{1,0:T(8,128)(2,1)}, bf16[32,4096]{1,0:T(8,128)(2,1)S(1)}, u32[]{:S(2)}, u32[]{:S(2)}) collective-permute-start(bf16[32,4096]{1,0:T(8,128)(2,1)} %get-tuple-element.34), channel_id=1, source_target_pairs={{8,0},{16,8},{24,16},{9,1},{17,9},{25,17},{10,2},{18,10},{26,18},{... | collective-permute-start | bytes 786440 | tf_op jit(solution)/shard_map/ppermute | solution.py:46
  124.3 8.1 %collective-permute-start.10 = (bf16[32,4096]{1,0:T(8,128)(2,1)}, bf16[32,4096]{1,0:T(8,128)(2,1)S(1)}, u32[]{:S(2)}, u32[]{:S(2)}) collective-permute-start(bf16[32,4096]{1,0:T(8,128)(2,1)} %get-tuple-element.35), channel_id=1, source_target_pairs={{0,1},{1,2},{2,3},{3,4},{4,5},{5,6},{6,7},{8,9},{9,10},{10,11},{11... | collective-permute-start | bytes 786440 | tf_op jit(solution)/shard_map/ppermute | solution.py:46
  128.7 7.9 %copy-start.3 = (bf16[32,4096]{1,0:T(8,128)(2,1)}, bf16[32,4096]{1,0:T(8,128)(2,1)S(1)}, u32[]{:S(2)}) copy-start(bf16[32,4096]{1,0:T(8,128)(2,1)S(1)} %collective-permute-done.6.r0) | copy-start | bytes 786436
  128.8 7.9 %collective-permute-start.11 = (bf16[32,4096]{1,0:T(8,128)(2,1)}, bf16[32,4096]{1,0:T(8,128)(2,1)S(1)}, u32[]{:S(2)}, u32[]{:S(2)}) collective-permute-start(bf16[32,4096]{1,0:T(8,128)(2,1)} %get-tuple-element.36), channel_id=1, source_target_pairs={{1,0},{2,1},{3,2},{4,3},{5,4},{6,5},{7,6},{9,8},{10,9},{11,10},{12... | collective-permute-start | bytes 786440 | tf_op jit(solution)/shard_map/ppermute | solution.py:46
  130.7 6.0 %copy-start.4 = (bf16[32,4096]{1,0:T(8,128)(2,1)}, bf16[32,4096]{1,0:T(8,128)(2,1)S(1)}, u32[]{:S(2)}) copy-start(bf16[32,4096]{1,0:T(8,128)(2,1)S(1)} %collective-permute-done.7.r1) | copy-start | bytes 786436
  130.7 6.0 %copy-start.5 = (bf16[32,4096]{1,0:T(8,128)(2,1)}, bf16[32,4096]{1,0:T(8,128)(2,1)S(1)}, u32[]{:S(2)}) copy-start(bf16[32,4096]{1,0:T(8,128)(2,1)S(1)} %collective-permute-done.8.r2) | copy-start | bytes 786436
  130.7 5.9 %copy-start.6 = (bf16[32,4096]{1,0:T(8,128)(2,1)}, bf16[32,4096]{1,0:T(8,128)(2,1)S(1)}, u32[]{:S(2)}) copy-start(bf16[32,4096]{1,0:T(8,128)(2,1)S(1)} %collective-permute-done.9.r3) | copy-start | bytes 786436
  132.3 4.3 %copy-start.7 = (bf16[32,4096]{1,0:T(8,128)(2,1)}, bf16[32,4096]{1,0:T(8,128)(2,1)S(1)}, u32[]{:S(2)}) copy-start(bf16[32,4096]{1,0:T(8,128)(2,1)S(1)} %collective-permute-done.10.r4) | copy-start | bytes 786436
  136.7 0.7 copy-start.8

commit v4 on v3

--- a/solution.py
+++ b/solution.py
@@ -36,10 +36,6 @@
     return lax.broadcasted_iota(jnp.int32, shape, len(shape) - 1) < B
 
 
-def swap_lanes(v):
-    return jnp.concatenate([v[:, B:], v[:, :B]], axis=1)
-
-
 def shifted(value, axis, by):
     devices = lax.axis_size(axis)
     pairs = [(i, i + by) for i in range(devices) if 0 <= i + by < devices]
@@ -72,9 +68,6 @@
 
     for n in range(P_PARTS):
         prolong_copy(n).start()
-    for n in range(X_PARTS):
-        plane_copy(n).start()
-
     square = (ROWS, ROWS)
     peer = lax.rem(owner[...], LAYERS)
     member = lax.broadcasted_iota(jnp.int32, (16, ROWS), 0) == peer
@@ -112,6 +105,9 @@
 
     for n in range(P_PARTS):
         prolong_copy(n).wait()
+        if n == 0:
+            for m in range(X_PARTS):
+                plane_copy(m).start()
         lax.fori_loop(n * count // 16, (n + 1) * count // 16, group, 0)
     out_copies = [pltpu.make_async_copy(halves, halves_out, out_sem.at[6])]
     out_copies[0].start()
@@ -123,20 +119,12 @@
     at = lax.broadcasted_iota(jnp.int32, (EXTRA, LANES), 0)
     extra = jnp.where(at == 0, top, jnp.where(at == 1, rest, 0)).astype(f32).astype(bf16)
 
-    def pick(q, carry):
+    def pick(q):
         for j in range(6):
             row = lists[j, 0, q]
             sends[j][pl.ds(pl.multiple_of(q * HALF, HALF), HALF), :] = halves[
                 pl.ds(pl.multiple_of(row * HALF, HALF), HALF), :
             ]
-        return carry
-
-    lax.fori_loop(0, GCAP, pick, 0, unroll=4)
-    for j in range(6):
-        sends[j][GHOST_LEN:NEAR_AT, :] = extra
-        out_copies.append(pltpu.make_async_copy(sends[j], outs[j], out_sem.at[j]))
-        if j < 4:
-            out_copies[-1].start()
 
     def some_planes(n, carry):
         plane_copy(n).wait()
@@ -147,9 +135,15 @@
             for c in range(3):
                 strips[c][rows, :] = got[:, c * LANES : (c + 1) * LANES]
             strips[3][rows, :B] = got[:, 3 * LANES :]
+            pick(a)
         return carry
 
     lax.fori_loop(0, X_PARTS, some_planes, 0)
+    for j in range(6):
+        sends[j][GHOST_LEN:NEAR_AT, :] = extra
+        out_copies.append(pltpu.make_async_copy(sends[j], outs[j], out_sem.at[j]))
+        if j < 4:
+            out_copies[-1].start()
     for r in range(SENT):
         if r < LAYERS * FAR:
             out, base = far, r * ROW_LEN
@@ -254,23 +248,28 @@
         unit = (down_rows == along).astype(f32).astype(bf16)
         picks[...] = lax.dot_general(unit, taken, NT, preferred_element_type=f32).astype(bf16)
 
-    @pl.when(step < STEPS)
-    def _():
-        def relay(n, carry):
+    def relay(width):
+        def plane(n, carry):
             rows = pl.ds((step * A_STEP + n) * SPAN, TOTAL)
             got = lax.dot_general(
-                picks[...], blocks[n], (((1,), (1,)), ((), ())), preferred_element_type=f32
+                picks[...], blocks[n, :width], NT, preferred_element_type=f32
             )
             table0[rows, :] = got[:, :LANES]
-            table1[rows, :] = got[:, LANES:]
+            table1[rows, : width - LANES] = got[:, LANES:]
             return carry
 
-        lax.fori_loop(0, A_STEP, relay, 0, unroll=8)
+        lax.fori_loop(0, A_STEP, plane, 0, unroll=16)
+
+    @pl.when((step < STEPS) & (j == 0))
+    def _():
+        relay(2 * LANES)
+
+    @pl.when((step < STEPS) & (j == 1))
+    def _():
+        relay(LANES + B)
 
     @pl.when(step >= STEPS)
     def _():
-        keep = lower_lanes((B, LANES)) | (j == 0)
-
         def multiply(n, carry):
             i = (step - STEPS) * R_STEP + 2 * n
             rows = [
@@ -284,10 +283,10 @@
             for q in range(2):
                 part = got[q * B : (q + 1) * B]
                 left[0, 2 * n + q] = part[:, :LANES].astype(bf16)
-                left[1, 2 * n + q] = jnp.where(keep, part[:, LANES:], 0.0).astype(bf16)
+                left[1, 2 * n + q] = part[:, LANES:].astype(bf16)
             return carry
 
-        lax.fori_loop(0, R_STEP // 2, multiply, 0, unroll=16)
+        lax.fori_loop(0, R_STEP // 2, multiply, 0, unroll=32)
 
 
 def make_left(arrival, blocks, halves):
@@ -323,14 +322,14 @@
 
 
 PARTS = 8
-UNROLL = 16
+UNROLL = 32
 TALL = B + 1
 
 
 def sums_kernel(
     moved_rows, columns, targets, left_hbm, halves, g0, g1, g2, g3, g4, g5, far,
     own, fine, s0, s1, s2, s3, s4, s5,
-    left, packed, double, acc0, acc1, moved, left_sem, table_sem, moved_sem,
+    left, packed, acc0, acc1, moved, left_sem, table_sem, moved_sem,
 ):
     ghosts = (g0, g1, g2, g3, g4, g5)
     sends = (s0, s1, s2, s3, s4, s5)
@@ -369,23 +368,24 @@
 
     lax.fori_loop(0, U_DEV + 1, clear, 0, unroll=5)
 
-    def expand(c, carry):
-        h = packed[pl.ds(pl.multiple_of(c * HALF, HALF), HALF), :]
-        turned = swap_lanes(h)
-        double[c, 0:HALF, :] = jnp.concatenate([h[:, :B], turned[:, B:]], axis=1)
-        double[c, HALF:, :] = jnp.concatenate([turned[:, :B], h[:, B:]], axis=1)
-        return carry
-
-    table_copies[0].wait()
-    lax.fori_loop(0, ROWS, expand, 0, unroll=8)
-    for copy in table_copies[1:]:
+    def tile(c):
+        return packed[pl.ds(pl.multiple_of(c * HALF, HALF), HALF), :]
+
+    def beside(p, q):
+        return jnp.concatenate(
+            [
+                jnp.concatenate([p[:, :B], q[:, :B]], axis=1),
+                jnp.concatenate([p[:, B:], q[:, B:]], axis=1),
+            ],
+            axis=0,
+        )
+
+    for copy in table_copies + moved_copies:
         copy.wait()
-    lax.fori_loop(ROWS, TABLE, expand, 0, unroll=8)
-    for copy in moved_copies:
-        copy.wait()
 
     def arrive(s, carry):
-        block = double[jnp.maximum(moved_rows[0, s], 0), :, :][:, :B]
+        own_tile = tile(jnp.maximum(moved_rows[0, s], 0))
+        block = jnp.concatenate([own_tile[:, :B], own_tile[:, B:]], axis=0)
         base = pl.multiple_of(s * ROW_LEN, HALF)
         h = moved[pl.ds(base + 3 * B, HALF), :]
         chunks = [moved[pl.ds(base + c * B, B), :] for c in range(3)]
@@ -401,7 +401,7 @@
         )
         return carry
 
-    lax.fori_loop(0, SENT, arrive, 0, unroll=4)
+    lax.fori_loop(0, SENT, arrive, 0, unroll=8)
 
     zero = jnp.zeros((B, LANES), bf16)
 
@@ -413,10 +413,9 @@
         for quad in range(2):
             some = cols[4 * quad : 4 * quad + 4]
             slots = slots_of[4 * quad : 4 * quad + 4]
-            tiles = [double[jnp.maximum(col, 0)] for col in some]
-            tiles += [zero] * (4 - len(tiles))
-            upper = jnp.concatenate([tiles[0][:, :B], tiles[2][:, B:]], axis=1)
-            lower = jnp.concatenate([tiles[1][:, :B], tiles[3][:, B:]], axis=1)
+            tiles = [tile(jnp.maximum(col, 0)) for col in some]
+            tiles += [zero[:HALF]] * (4 - len(tiles))
+            upper, lower = beside(tiles[0], tiles[2]), beside(tiles[1], tiles[3])
             weights = jnp.concatenate(
                 [
                     jnp.concatenate([upper, zero], axis=1),
@@ -476,7 +475,7 @@
                     sends[v - 1][at, lanes] = coarse
                 return carry
 
-            lax.fori_loop(0, HALF, gather, 0, unroll=8)
+            lax.fori_loop(0, HALF, gather, 0, unroll=16)
 
 
 def make_sums(moved_rows, columns, targets, left, halves, ghosts, far):
@@ -491,7 +490,6 @@
             scratch_shapes=[
                 pltpu.VMEM((4, ROWS + SENT, B, LANES), bf16),
                 pltpu.VMEM((TABLE * HALF, LANES), bf16),
-                pltpu.VMEM((TABLE, B, LANES), bf16),
             ]
             + [pltpu.VMEM(((U_DEV + 1) * TALL, LANES), f32)] * 2
             + [

time: 142 us -> 131 us (0.923)
  Pallas kernels: 77.7 us -> 66.7 us
    pallas_call x1, Pallas kernels: 33.5 us -> 26.7 us  [make_sums(): pl.pallas_call(sums_kernel, grid_spec=pltpu.PrefetchScalarGridSpec(num_sc...]
    pallas_call x1, Pallas kernels: 14.8 us -> 12.6 us  [pack(): pl.pallas_call(pack_kernel, grid_spec=pltpu.PrefetchScalarGridSpec(num_sc...]
    pallas_call x1, Pallas kernels: 25.6 us -> 23.6 us  [make_left(): pl.pallas_call(left_kernel, grid=(2, 2 * STEPS), in_specs=[whole((1, ROWS...]
where the time goes in v4:
time: 131 us; the launch traced here: 130 us
  Pallas kernels  66.7 us (51%)
  starting transfers between devices  39.8 us (30%)
  waiting for transfers between devices  19.7 us (15%)
  local copies, waits for them, and re-layouts  2.74 us (2%)
    ppermute x12, starting transfers between devices, shifted(): return lax.ppermute(value, axis, pairs)  33.8 us
    pallas_call x1, Pallas kernels, make_sums(): pl.pallas_call(sums_kernel, grid_spec=pltpu.PrefetchScalarGridSpec(num_sc...  26.7 us
    pallas_call x1, Pallas kernels, make_left(): pl.pallas_call(left_kernel, grid=(2, 2 * STEPS), in_specs=[whole((1, ROWS...  23.6 us
    ppermute x12, waiting for transfers between devices, shifted(): return lax.ppermute(value, axis, pairs)  19.7 us
    pallas_call x1, Pallas kernels, pack(): pl.pallas_call(pack_kernel, grid_spec=pltpu.PrefetchScalarGridSpec(num_sc...  12.6 us
    all_to_all x1, starting transfers between devices, one_shard(): lax.all_to_all(far.reshape(LAYERS, FAR * ROW_LEN, LANES), 'gz', split_axi...  6 us
    pallas_call x1, Pallas kernels, make_final(): pl.pallas_call(final_kernel, grid=(1,), in_specs=[pl.BlockSpec((1, U_DEV)...  3.82 us
    unnamed x20, local copies, waits for them, and re-layouts  2.66 us
  transfers between devices with their start and end apart: 13, of which 3 were waited for; matrix products, arithmetic and copies ran while one was open for 1% of the time, Pallas kernels for 18%

profile of v4, /device:TPU:23, one launch (start us, length us, event | category | flops | bytes accessed | tf_op | source)
XLA Modules:
  0.0 130.1 jit_solution(12924131087695589813)
XLA Ops:
  0.0 12.6 %pack.1 = (bf16[8192,128]{1,0:T(8,128)(2,1)}, bf16[2064,128]{1,0:T(8,128)(2,1)}, bf16[2064,128]{1,0:T(8,128)(2,1)}, bf16[2064,128]{1,0:T(8,128)(2,1)}, bf16[2064...) custom-call(s32[1]{0:T(128)} %bitcast.5.layer, ...), custom_call_target="tpu_custom_call" | custom-call | flops 2000000000 | bytes 23000000 | tf_op jit(solution)/shard_map/pack/pallas_call | solution.py:171
  12.6 6.0 %all-to-all-start = ((bf16[8,448,128]{2,1,0:T(8,128)(2,1)}), bf16[8,448,128]{2,1,0:T(8,128)(2,1)S(1)}, u32[]{:S(2)}, u32[]{:S(2)}) async-start(bf16[8,448,128]{2,1,0:T(8,128)(2,1)} %bitcast.14), calls=%async_computation | async-start | bytes 1835008 | tf_op jit(solution)/shard_map/all_to_all | solution.py:583
  18.6 2.1 %collective-permute-start = (bf16[2064,128]{1,0:T(8,128)(2,1)}, bf16[2064,128]{1,0:T(8,128)(2,1)}, u32[]{:S(2)}, u32[]{:S(2)}) collective-permute-start(bf16[2064,128]{1,0:T(8,128)(2,1)} %get-tuple-element.22), channel_id=1, source_target_pairs={{32,0},{64,32},{96,64},{33,1},{65,33},{97,65},{34,2},{66,34},{98,6... | collective-permute-start | bytes 1585160 | tf_op jit(solution)/shard_map/ppermute | solution.py:42
  20.6 4.0 %collective-permute-start.1 = (bf16[2064,128]{1,0:T(8,128)(2,1)}, bf16[2064,128]{1,0:T(8,128)(2,1)}, u32[]{:S(2)}, u32[]{:S(2)}) collective-permute-start(bf16[2064,128]{1,0:T(8,128)(2,1)} %get-tuple-element.23), channel_id=1, source_target_pairs={{0,32},{32,64},{64,96},{1,33},{33,65},{65,97},{2,34},{34,66},{66,9... | collective-permute-start | bytes 1585160 | tf_op jit(solution)/shard_map/ppermute | solution.py:42
  24.6 3.2 %collective-permute-start.2 = (bf16[2064,128]{1,0:T(8,128)(2,1)}, bf16[2064,128]{1,0:T(8,128)(2,1)}, u32[]{:S(2)}, u32[]{:S(2)}) collective-permute-start(bf16[2064,128]{1,0:T(8,128)(2,1)} %get-tuple-element.24), channel_id=1, source_target_pairs={{8,0},{16,8},{24,16},{9,1},{17,9},{25,17},{10,2},{18,10},{26,18},{... | collective-permute-start | bytes 1585160 | tf_op jit(solution)/shard_map/ppermute | solution.py:42
  27.9 2.7 %collective-permute-start.4 = (bf16[2960,128]{1,0:T(8,128)(2,1)}, bf16[2960,128]{1,0:T(8,128)(2,1)S(1)}, u32[]{:S(2)}, u32[]{:S(2)}) collective-permute-start(bf16[2960,128]{1,0:T(8,128)(2,1)} %get-tuple-element.26), channel_id=1, source_target_pairs={{1,0},{2,1},{3,2},{4,3},{5,4},{6,5},{7,6},{9,8},{10,9},{11,10},{12... | collective-permute-start | bytes 2273288 | tf_op jit(solution)/shard_map/ppermute | solution.py:42
  30.6 3.5 %collective-permute-start.5 = (bf16[2960,128]{1,0:T(8,128)(2,1)}, bf16[2960,128]{1,0:T(8,128)(2,1)}, u32[]{:S(2)}, u32[]{:S(2)}) collective-permute-start(bf16[2960,128]{1,0:T(8,128)(2,1)} %get-tuple-element.27), channel_id=1, source_target_pairs={{0,1},{1,2},{2,3},{3,4},{4,5},{5,6},{6,7},{8,9},{9,10},{10,11},{11... | collective-permute-start | bytes 2273288 | tf_op jit(solution)/shard_map/ppermute | solution.py:42
  34.2 0.0 copy-start.9
  34.2 23.6 %left.1.left_hbm = bf16[4,256,64,128]{3,2,1,0:T(8,128)(2,1)} custom-call(s32[1,256]{1,0:T(1,128)} %bitcast.17, bf16[64,448,256]{2,1,0:T(8,128)(2,1)} %bitcast.12, bf16[8192,128]{1,0:T(8,128)(2,1)} %get-tuple-element.21.halves), custom_call_target="tpu_custom_call" | custom-call | flops 12000000000 | bytes 60000000 | tf_op jit(solution)/shard_map/left/pallas_call | solution.py:294
  57.8 0.1 iota_add_fusion
  57.9 0.1 add.81
  58.0 1.3 collective-permute-start.3
  59.3 0.1 broadcast_compare_fusion
  59.4 0.2 select_reduce_fusion
  59.5 0.6 add_bitcast_fusion.moved_rows
  60.1 13.8 %collective-permute-done.3.g3 = bf16[2064,128]{1,0:T(8,128)(2,1)S(1)} collective-permute-done((bf16[2064,128]{1,0:T(8,128)(2,1)}, bf16[2064,128]{1,0:T(8,128)(2,1)S(1)}, u32[]{:S(2)}, u32[]{:S(2)}) %collective-permute-start.3) | collective-permute-done | bytes 528416 | tf_op jit(solution)/shard_map/ppermute | solution.py:42
  73.9 0.8 copy-done.2
  74.8 0.0 collective-permute-done.5.g5
  74.8 0.0 copy-start
  74.8 0.8 copy-done.1
  75.6 0.3 copy-done
  75.9 26.7 %sums.1 = (bf16[32,4096]{1,0:T(8,128)(2,1)}, bf16[32,4096]{1,0:T(8,128)(2,1)}, bf16[32,4096]{1,0:T(8,128)(2,1)}, bf16[32,4096]{1,0:T(8,128)(2,1)}, bf16[32,4096]...) custom-call(s32[1,24]{1,0:T(1,128)} %add_bitcast_fusion.moved_rows, ...), custom_call_target="tpu_custom_call" | custom-call | flops 8000000000 | bytes 30000000 | tf_op jit(solution)/shard_map/sums/pallas_call | solution.py:483
  102.7 1.9 %collective-permute-start.6 = (bf16[32,4096]{1,0:T(8,128)(2,1)}, bf16[32,4096]{1,0:T(8,128)(2,1)S(1)}, u32[]{:S(2)}, u32[]{:S(2)}) collective-permute-start(bf16[32,4096]{1,0:T(8,128)(2,1)} %get-tuple-element.31), channel_id=1, source_target_pairs={{0,32},{32,64},{64,96},{1,33},{33,65},{65,97},{2,34},{34,66},{66,9... | collective-permute-start | bytes 786440 | tf_op jit(solution)/shard_map/ppermute | solution.py:42
  104.6 3.4 %collective-permute-start.7 = (bf16[32,4096]{1,0:T(8,128)(2,1)}, bf16[32,4096]{1,0:T(8,128)(2,1)S(1)}, u32[]{:S(2)}, u32[]{:S(2)}) collective-permute-start(bf16[32,4096]{1,0:T(8,128)(2,1)} %get-tuple-element.32), channel_id=1, source_target_pairs={{32,0},{64,32},{96,64},{33,1},{65,33},{97,65},{34,2},{66,34},{98,6... | collective-permute-start | bytes 786440 | tf_op jit(solution)/shard_map/ppermute | solution.py:42
  108.0 1.3 collective-permute-start.8
  109.3 4.0 %collective-permute-start.9 = (bf16[32,4096]{1,0:T(8,128)(2,1)}, bf16[32,4096]{1,0:T(8,128)(2,1)S(1)}, u32[]{:S(2)}, u32[]{:S(2)}) collective-permute-start(bf16[32,4096]{1,0:T(8,128)(2,1)} %get-tuple-element.34), channel_id=1, source_target_pairs={{8,0},{16,8},{24,16},{9,1},{17,9},{25,17},{10,2},{18,10},{26,18},{... | collective-permute-start | bytes 786440 | tf_op jit(solution)/shard_map/ppermute | solution.py:42
  113.3 4.4 %collective-permute-start.10 = (bf16[32,4096]{1,0:T(8,128)(2,1)}, bf16[32,4096]{1,0:T(8,128)(2,1)S(1)}, u32[]{:S(2)}, u32[]{:S(2)}) collective-permute-start(bf16[32,4096]{1,0:T(8,128)(2,1)} %get-tuple-element.35), channel_id=1, source_target_pairs={{0,1},{1,2},{2,3},{3,4},{4,5},{5,6},{6,7},{8,9},{9,10},{10,11},{11... | collective-permute-start | bytes 786440 | tf_op jit(solution)/shard_map/ppermute | solution.py:42
  117.7 1.9 %collective-permute-start.11 = (bf16[32,4096]{1,0:T(8,128)(2,1)}, bf16[32,4096]{1,0:T(8,128)(2,1)S(1)}, u32[]{:S(2)}, u32[]{:S(2)}) collective-permute-start(bf16[32,4096]{1,0:T(8,128)(2,1)} %get-tuple-element.36), channel_id=1, source_target_pairs={{1,0},{2,1},{3,2},{4,3},{5,4},{6,5},{7,6},{9,8},{10,9},{11,10},{12... | collective-permute-start | bytes 786440 | tf_op jit(solution)/shard_map/ppermute | solution.py:42
  119.7 1.6 %collective-permute-done.10.r4 = bf16[32,4096]{1,0:T(8,128)(2,1)S(1)} collective-permute-done((bf16[32,4096]{1,0:T(8,128)(2,1)}, bf16[32,4096]{1,0:T(8,128)(2,1)S(1)}, u32[]{:S(2)}, u32[]{:S(2)}) %collective-permute-start.10) | collective-permute-done | bytes 262176 | tf_op jit(solution)/shard_map/ppermute | solution.py:42
  121.3 4.3 %collective-permute-done.11.r5 = bf16[32,4096]{1,0:T(8,128)(2,1)S(1)} collective-permute-done((bf16[32,4096]{1,0:T(8,128)(2,1)}, bf16[32,4096]{1,0:T(8,128)(2,1)S(1)}, u32[]{:S(2)}, u32[]{:S(2)}) %collective-permute-start.11) | collective-permute-done | bytes 262176 | tf_op jit(solution)/shard_map/ppermute | solution.py:42
  125.7 0.7 copy-done.8
  126.3 3.8 %final.1 = f32[64,4096]{1,0:T(8,128)} custom-call(s32[1,224]{1,0:T(1,128)} %touched.3, bf16[32,4096]{1,0:T(8,128)(2,1)} %get-tuple-element.29.own, bf16[32,4096]{1,0:T(8,128)(2,1)} %get-tuple-element.30.fine, bf16[32,4096]{1,0:T(8,128)(2,1)} %copy-done.3, bf16[32,4096]{1,0:T(8,128)(2,1)} %copy-done.4, bf16[32,4096]{1,0:T(8,128)(2,1)} %copy-done.5, ...), custom_call_target="tpu_custom_call" | custom-call | tf_op jit(solution)/shard_map/final/pallas_call | solution.py:551
  (26 shorter events, 0.1 us)
Async XLA Ops:
  12.6 62.2 %all-to-all-start = ((bf16[8,448,128]{2,1,0:T(8,128)(2,1)}), bf16[8,448,128]{2,1,0:T(8,128)(2,1)S(1)}, u32[]{:S(2)}, u32[]{:S(2)}) async-start(bf16[8,448,128]{2,1,0:T(8,128)(2,1)} %bitcast.14), calls=%async_computation | async-start | bytes 1835008 | tf_op jit(solution)/shard_map/all_to_all | solution.py:583
  18.6 39.4 %collective-permute-start = (bf16[2064,128]{1,0:T(8,128)(2,1)}, bf16[2064,128]{1,0:T(8,128)(2,1)}, u32[]{:S(2)}, u32[]{:S(2)}) collective-permute-start(bf16[2064,128]{1,0:T(8,128)(2,1)} %get-tuple-element.22), channel_id=1, source_target_pairs={{32,0},{64,32},{96,64},{33,1},{65,33},{97,65},{34,2},{66,34},{98,6... | collective-permute-start | bytes 1585160 | tf_op jit(solution)/shard_map/ppermute | solution.py:42
  20.6 39.5 %collective-permute-start.1 = (bf16[2064,128]{1,0:T(8,128)(2,1)}, bf16[2064,128]{1,0:T(8,128)(2,1)}, u32[]{:S(2)}, u32[]{:S(2)}) collective-permute-start(bf16[2064,128]{1,0:T(8,128)(2,1)} %get-tuple-element.23), channel_id=1, source_target_pairs={{0,32},{32,64},{64,96},{1,33},{33,65},{65,97},{2,34},{34,66},{66,9... | collective-permute-start | bytes 1585160 | tf_op jit(solution)/shard_map/ppermute | solution.py:42
  24.6 35.5 %collective-permute-start.2 = (bf16[2064,128]{1,0:T(8,128)(2,1)}, bf16[2064,128]{1,0:T(8,128)(2,1)}, u32[]{:S(2)}, u32[]{:S(2)}) collective-permute-start(bf16[2064,128]{1,0:T(8,128)(2,1)} %get-tuple-element.24), channel_id=1, source_target_pairs={{8,0},{16,8},{24,16},{9,1},{17,9},{25,17},{10,2},{18,10},{26,18},{... | collective-permute-start | bytes 1585160 | tf_op jit(solution)/shard_map/ppermute | solution.py:42
  27.9 46.0 %collective-permute-start.4 = (bf16[2960,128]{1,0:T(8,128)(2,1)}, bf16[2960,128]{1,0:T(8,128)(2,1)S(1)}, u32[]{:S(2)}, u32[]{:S(2)}) collective-permute-start(bf16[2960,128]{1,0:T(8,128)(2,1)} %get-tuple-element.26), channel_id=1, source_target_pairs={{1,0},{2,1},{3,2},{4,3},{5,4},{6,5},{7,6},{9,8},{10,9},{11,10},{12... | collective-permute-start | bytes 2273288 | tf_op jit(solution)/shard_map/ppermute | solution.py:42
  30.6 44.1 %collective-permute-start.5 = (bf16[2960,128]{1,0:T(8,128)(2,1)}, bf16[2960,128]{1,0:T(8,128)(2,1)}, u32[]{:S(2)}, u32[]{:S(2)}) collective-permute-start(bf16[2960,128]{1,0:T(8,128)(2,1)} %get-tuple-element.27), channel_id=1, source_target_pairs={{0,1},{1,2},{2,3},{3,4},{4,5},{5,6},{6,7},{8,9},{9,10},{10,11},{11... | collective-permute-start | bytes 2273288 | tf_op jit(solution)/shard_map/ppermute | solution.py:42
  34.2 25.2 %copy-start.9 = (s32[256]{0:T(256)S(1)}, s32[256]{0:T(256)}, u32[]{:S(2)}) copy-start(s32[256]{0:T(256)} %param.11) | copy-start | bytes 3076
  58.0 16.0 %collective-permute-start.3 = (bf16[2064,128]{1,0:T(8,128)(2,1)}, bf16[2064,128]{1,0:T(8,128)(2,1)S(1)}, u32[]{:S(2)}, u32[]{:S(2)}) collective-permute-start(bf16[2064,128]{1,0:T(8,128)(2,1)} %get-tuple-element.25), channel_id=1, source_target_pairs={{0,8},{8,16},{16,24},{1,9},{9,17},{17,25},{2,10},{10,18},{18,26},{... | collective-permute-start | bytes 1585160 | tf_op jit(solution)/shard_map/ppermute | solution.py:42
  73.9 0.8 copy-start.2
  74.8 0.9 copy-start.1
  74.8 1.2 copy-start
  102.7 15.0 %collective-permute-start.6 = (bf16[32,4096]{1,0:T(8,128)(2,1)}, bf16[32,4096]{1,0:T(8,128)(2,1)S(1)}, u32[]{:S(2)}, u32[]{:S(2)}) collective-permute-start(bf16[32,4096]{1,0:T(8,128)(2,1)} %get-tuple-element.31), channel_id=1, source_target_pairs={{0,32},{32,64},{64,96},{1,33},{33,65},{65,97},{2,34},{34,66},{66,9... | collective-permute-start | bytes 786440 | tf_op jit(solution)/shard_map/ppermute | solution.py:42
  104.6 15.1 %collective-permute-start.7 = (bf16[32,4096]{1,0:T(8,128)(2,1)}, bf16[32,4096]{1,0:T(8,128)(2,1)S(1)}, u32[]{:S(2)}, u32[]{:S(2)}) collective-permute-start(bf16[32,4096]{1,0:T(8,128)(2,1)} %get-tuple-element.32), channel_id=1, source_target_pairs={{32,0},{64,32},{96,64},{33,1},{65,33},{97,65},{34,2},{66,34},{98,6... | collective-permute-start | bytes 786440 | tf_op jit(solution)/shard_map/ppermute | solution.py:42
  108.0 11.7 %collective-permute-start.8 = (bf16[32,4096]{1,0:T(8,128)(2,1)}, bf16[32,4096]{1,0:T(8,128)(2,1)S(1)}, u32[]{:S(2)}, u32[]{:S(2)}) collective-permute-start(bf16[32,4096]{1,0:T(8,128)(2,1)} %get-tuple-element.33), channel_id=1, source_target_pairs={{0,8},{8,16},{16,24},{1,9},{9,17},{17,25},{2,10},{10,18},{18,26},{... | collective-permute-start | bytes 786440 | tf_op jit(solution)/shard_map/ppermute | solution.py:42
  109.3 10.4 %collective-permute-start.9 = (bf16[32,4096]{1,0:T(8,128)(2,1)}, bf16[32,4096]{1,0:T(8,128)(2,1)S(1)}, u32[]{:S(2)}, u32[]{:S(2)}) collective-permute-start(bf16[32,4096]{1,0:T(8,128)(2,1)} %get-tuple-element.34), channel_id=1, source_target_pairs={{8,0},{16,8},{24,16},{9,1},{17,9},{25,17},{10,2},{18,10},{26,18},{... | collective-permute-start | bytes 786440 | tf_op jit(solution)/shard_map/ppermute | solution.py:42
  113.3 8.0 %collective-permute-start.10 = (bf16[32,4096]{1,0:T(8,128)(2,1)}, bf16[32,4096]{1,0:T(8,128)(2,1)S(1)}, u32[]{:S(2)}, u32[]{:S(2)}) collective-permute-start(bf16[32,4096]{1,0:T(8,128)(2,1)} %get-tuple-element.35), channel_id=1, source_target_pairs={{0,1},{1,2},{2,3},{3,4},{4,5},{5,6},{6,7},{8,9},{9,10},{10,11},{11... | collective-permute-start | bytes 786440 | tf_op jit(solution)/shard_map/ppermute | solution.py:42
  117.7 7.9 %copy-start.3 = (bf16[32,4096]{1,0:T(8,128)(2,1)}, bf16[32,4096]{1,0:T(8,128)(2,1)S(1)}, u32[]{:S(2)}) copy-start(bf16[32,4096]{1,0:T(8,128)(2,1)S(1)} %collective-permute-done.6.r0) | copy-start | bytes 786436
  117.7 7.9 %collective-permute-start.11 = (bf16[32,4096]{1,0:T(8,128)(2,1)}, bf16[32,4096]{1,0:T(8,128)(2,1)S(1)}, u32[]{:S(2)}, u32[]{:S(2)}) collective-permute-start(bf16[32,4096]{1,0:T(8,128)(2,1)} %get-tuple-element.36), channel_id=1, source_target_pairs={{1,0},{2,1},{3,2},{4,3},{5,4},{6,5},{7,6},{9,8},{10,9},{11,10},{12... | collective-permute-start | bytes 786440 | tf_op jit(solution)/shard_map/ppermute | solution.py:42
  119.7 6.0 %copy-start.4 = (bf16[32,4096]{1,0:T(8,128)(2,1)}, bf16[32,4096]{1,0:T(8,128)(2,1)S(1)}, u32[]{:S(2)}) copy-start(bf16[32,4096]{1,0:T(8,128)(2,1)S(1)} %collective-permute-done.7.r1) | copy-start | bytes 786436
  119.7 6.0 %copy-start.5 = (bf16[32,4096]{1,0:T(8,128)(2,1)}, bf16[32,4096]{1,0:T(8,128)(2,1)S(1)}, u32[]{:S(2)}) copy-start(bf16[32,4096]{1,0:T(8,128)(2,1)S(1)} %collective-permute-done.8.r2) | copy-start | bytes 786436
  119.7 5.9 %copy-start.6 = (bf16[32,4096]{1,0:T(8,128)(2,1)}, bf16[32,4096]{1,0:T(8,128)(2,1)S(1)}, u32[]{:S(2)}) copy-start(bf16[32,4096]{1,0:T(8,128)(2,1)S(1)} %collective-permute-done.9.r3) | copy-start | bytes 786436
  121.3 4.3 %copy-start.7 = (bf16[32,4096]{1,0:T(8,128)(2,1)}, bf16[32,4096]{1,0:T(8,128)(2,1)S(1)}, u32[]{:S(2)}) copy-start(bf16[32,4096]{1,0:T(8,128)(2,1)S(1)} %collective-permute-done.10.r4) | copy-start | bytes 786436
  125.6 0.7 copy-start.8

commit v5 on v4

--- a/solution.py
+++ b/solution.py
@@ -216,31 +216,19 @@
 
     @pl.when((j == 0) & (step == 0))
     def _():
-        eye = (
-            lax.broadcasted_iota(jnp.int32, (B, B), 0)
-            == lax.broadcasted_iota(jnp.int32, (B, B), 1)
-        ).astype(bf16)
-
-        low = lower_lanes((B, LANES))
+        wide = (LANES, LANES)
+        eye = lax.broadcasted_iota(jnp.int32, wide, 0) == lax.broadcasted_iota(jnp.int32, wide, 1)
+        eye = eye.astype(f32).astype(bf16)
 
         def turn(n, carry):
-            tiles = []
-            for q in range(4):
-                h = halves[pl.ds(pl.multiple_of((n * 4 + q) * HALF, HALF), HALF), :]
-                tiles += [h[:, :B], h[:, B:]]
-            got = lax.dot_general(
-                eye,
-                jnp.concatenate(tiles, axis=0),
-                (((1,), (1,)), ((), ())),
-                preferred_element_type=f32,
-            )
-            for q in range(4):
-                pair = got[:, (q // 2) * LANES : (q // 2 + 1) * LANES]
-                mine = low if q % 2 == 0 else jnp.logical_not(low)
-                transposed[n * 4 + q] = jnp.where(mine, pair, 0.0).astype(bf16)
+            tiles = halves[pl.ds(pl.multiple_of(n * 8 * HALF, 8 * HALF), 8 * HALF), :]
+            got = lax.dot_general(eye, tiles, NT, preferred_element_type=f32).astype(bf16)
+            for g in range(2):
+                lanes = slice(g * LANES, (g + 1) * LANES)
+                transposed[2 * n + g] = jnp.concatenate([got[:B, lanes], got[B:, lanes]], axis=1)
             return carry
 
-        lax.fori_loop(0, ROWS // 4, turn, 0, unroll=8)
+        lax.fori_loop(0, ROWS // 8, turn, 0, unroll=8)
 
         down_rows = lax.broadcasted_iota(jnp.int32, square, 0)
         along = lax.broadcasted_iota(jnp.int32, square, 1)
@@ -268,25 +256,45 @@
     def _():
         relay(LANES + B)
 
-    @pl.when(step >= STEPS)
+    whose = lax.broadcasted_iota(jnp.int32, (B, 2 * LANES), 1) % LANES // HALF
+
+    def four(n):
+        i = (step - STEPS) * R_STEP + 4 * n
+        rows = [
+            jnp.concatenate(
+                [t[pl.ds(i + q, B, stride=SPAN), :].astype(bf16) for t in tables], axis=1
+            )
+            for q in range(4)
+        ]
+        weights = jnp.concatenate([r[:HALF] for r in rows] + [r[HALF:] for r in rows], axis=0)
+        base = transposed[(step - STEPS) * (R_STEP // 4) + n]
+        mine = [jnp.where(whose == q, base, jnp.zeros((), bf16)) for q in range(4)]
+        got = jnp.dot(jnp.concatenate(mine, axis=0), weights, preferred_element_type=f32)
+        return [got[q * B : (q + 1) * B].astype(bf16) for q in range(4)]
+
+    @pl.when((step >= STEPS) & (j == 0))
     def _():
         def multiply(n, carry):
-            i = (step - STEPS) * R_STEP + 2 * n
-            rows = [
-                jnp.concatenate(
-                    [t[pl.ds(i + q, B, stride=SPAN), :].astype(bf16) for t in tables], axis=1
+            for q, part in enumerate(four(n)):
+                left[0, 4 * n + q] = part[:, :LANES]
+                left[1, 4 * n + q] = part[:, LANES:]
+            return carry
+
+        lax.fori_loop(0, R_STEP // 4, multiply, 0, unroll=16)
+
+    @pl.when((step >= STEPS) & (j == 1))
+    def _():
+        def multiply(n, carry):
+            parts = four(n)
+            for q in range(4):
+                left[0, 4 * n + q] = parts[q][:, :LANES]
+            for h in range(2):
+                left[1, 2 * n + h] = jnp.concatenate(
+                    [p[:, LANES : LANES + B] for p in parts[2 * h : 2 * h + 2]], axis=1
                 )
-                for q in range(2)
-            ]
-            pairs = jnp.concatenate([transposed[i], transposed[i + 1]], axis=0)
-            got = jnp.dot(pairs, jnp.concatenate(rows, axis=0), preferred_element_type=f32)
-            for q in range(2):
-                part = got[q * B : (q + 1) * B]
-                left[0, 2 * n + q] = part[:, :LANES].astype(bf16)
-                left[1, 2 * n + q] = part[:, LANES:].astype(bf16)
             return carry
 
-        lax.fori_loop(0, R_STEP // 2, multiply, 0, unroll=32)
+        lax.fori_loop(0, R_STEP // 4, multiply, 0, unroll=16)
 
 
 def make_left(arrival, blocks, halves):
@@ -308,7 +316,7 @@
         scratch_shapes=[
             pltpu.VMEM((B * SPAN, LANES), f32),
             pltpu.VMEM((B * SPAN, LANES), f32),
-            pltpu.VMEM((ROWS, B, LANES), bf16),
+            pltpu.VMEM((ROWS // 4, B, 2 * LANES), bf16),
             pltpu.VMEM((ROWS, ROWS), bf16),
         ],
         compiler_params=pltpu.CompilerParams(
@@ -322,7 +330,6 @@
 
 
 PARTS = 8
-UNROLL = 32
 TALL = B + 1
 
 
@@ -383,76 +390,81 @@
     for copy in table_copies + moved_copies:
         copy.wait()
 
-    def arrive(s, carry):
-        own_tile = tile(jnp.maximum(moved_rows[0, s], 0))
-        block = jnp.concatenate([own_tile[:, :B], own_tile[:, B:]], axis=0)
-        base = pl.multiple_of(s * ROW_LEN, HALF)
-        h = moved[pl.ds(base + 3 * B, HALF), :]
-        chunks = [moved[pl.ds(base + c * B, B), :] for c in range(3)]
-        chunks.append(jnp.concatenate([h[:, :B], h[:, B:]], axis=0))
-        got = lax.dot_general(
-            block, jnp.concatenate(chunks, axis=1), (((0,), (0,)), ((), ())),
-            preferred_element_type=f32,
-        ).astype(bf16)
-        for c in range(3):
-            left[c, ROWS + s] = got[:, c * LANES : (c + 1) * LANES]
-        left[3, ROWS + s] = jnp.concatenate(
-            [got[:, 3 * LANES :], jnp.zeros((B, B), bf16)], axis=1
+    def arrive(m, carry):
+        last = []
+        for s in (2 * m, 2 * m + 1):
+            own_tile = tile(jnp.maximum(moved_rows[0, s], 0))
+            block = jnp.concatenate([own_tile[:, :B], own_tile[:, B:]], axis=0)
+            base = pl.multiple_of(s * ROW_LEN, HALF)
+            h = moved[pl.ds(base + 3 * B, HALF), :]
+            chunks = [moved[pl.ds(base + c * B, B), :] for c in range(3)]
+            chunks.append(jnp.concatenate([h[:, :B], h[:, B:]], axis=0))
+            got = lax.dot_general(
+                block, jnp.concatenate(chunks, axis=1), (((0,), (0,)), ((), ())),
+                preferred_element_type=f32,
+            ).astype(bf16)
+            for c in range(3):
+                left[c, ROWS + s] = got[:, c * LANES : (c + 1) * LANES]
+            last.append(got[:, 3 * LANES :])
+        left[3, ROWS + m] = jnp.concatenate(last, axis=1)
+        return carry
+
+    lax.fori_loop(0, SENT // 2, arrive, 0, unroll=6)
+
+    zero = jnp.zeros((B, LANES), bf16)
+
+    def quad(a, b, entries):
+        slots = [slot for slot, _ in entries]
+        tiles = [tile(col) for _, col in entries]
+        weights = jnp.concatenate(
+            [
+                jnp.concatenate([beside(tiles[0], tiles[2]), zero], axis=1),
+                jnp.concatenate([zero, beside(tiles[1], tiles[3])], axis=1),
+            ],
+            axis=0,
         )
-        return carry
-
-    lax.fori_loop(0, SENT, arrive, 0, unroll=8)
-
-    zero = jnp.zeros((B, LANES), bf16)
-
-    def row(i, n, valid):
-        cols = [columns[k, n] for k in range(NBR)]
-        slots_of = [
-            jnp.where((cols[k] >= 0) & valid, targets[k, n], U_DEV) for k in range(NBR)
-        ]
-        for quad in range(2):
-            some = cols[4 * quad : 4 * quad + 4]
-            slots = slots_of[4 * quad : 4 * quad + 4]
-            tiles = [tile(jnp.maximum(col, 0)) for col in some]
-            tiles += [zero[:HALF]] * (4 - len(tiles))
-            upper, lower = beside(tiles[0], tiles[2]), beside(tiles[1], tiles[3])
-            weights = jnp.concatenate(
+        rows = jnp.concatenate([a, b], axis=0)
+        got = jnp.dot(rows, weights, preferred_element_type=f32)
+        for side in range(2):
+            for part in range(2):
+                first = side * LANES + part * B
+                lanes = slice(part * B, (part + 1) * B)
+                value = got[part * B : (part + 1) * B, first : first + B]
+                totals[side][pl.ds(slots[side + 2 * part] * TALL, B), lanes] += value
+
+    def four_rows(i, pair, sources):
+        entries = []
+        for n, valid in sources:
+            cols = [columns[k, n] for k in range(NBR)]
+            entries.append(
                 [
-                    jnp.concatenate([upper, zero], axis=1),
-                    jnp.concatenate([zero, lower], axis=1),
-                ],
-                axis=0,
+                    (
+                        jnp.where((cols[k] >= 0) & valid, targets[k, n], U_DEV),
+                        jnp.maximum(cols[k], 0),
+                    )
+                    for k in range(NBR)
+                ]
             )
-            rows = jnp.concatenate([left[2 * quad, i], left[2 * quad + 1, i]], axis=0)
-            got = jnp.dot(rows, weights, preferred_element_type=f32)
-            for side in range(2):
-                for part in range(2):
-                    k = side + 2 * part
-                    if k < len(some):
-                        first = side * LANES + part * B
-                        lanes = slice(part * B, (part + 1) * B)
-                        value = got[part * B : (part + 1) * B, first : first + B]
-                        totals[side][pl.ds(slots[k] * TALL, B), lanes] += value
-
-    def some_rows(n, carry):
-        for r in range(UNROLL):
-            row(n * UNROLL + r, n * UNROLL + r, True)
-        return carry
+        for r in range(4):
+            quad(left[0, i + r], left[1, i + r], entries[r][:4])
+        for r in (0, 2):
+            quad(left[2, i + r], left[2, i + r + 1], entries[r][4:6] + entries[r + 1][4:6])
+        quad(left[3, pair], left[3, pair + 1], [e[6] for e in entries])
 
     def one_part(n, carry):
         left_copy(n).wait()
-        lax.fori_loop(n * (part // UNROLL), (n + 1) * (part // UNROLL), some_rows, 0)
+        for m in range(part // 4):
+            i = n * part + 4 * m
+            pair = (n >> 1) * R_STEP + (n & 1) * (part // 2) + 2 * m
+            four_rows(i, pair, [(i + r, True) for r in range(4)])
         return carry
 
     lax.fori_loop(0, PARTS, one_part, 0)
-
-    def more_rows(n, carry):
-        for r in range(8):
-            source = moved_rows[0, n * 8 + r]
-            row(ROWS + n * 8 + r, jnp.maximum(source, 0), source >= 0)
-        return carry
-
-    lax.fori_loop(0, SENT // 8, more_rows, 0)
+    for s in range(0, SENT, 4):
+        sources = [moved_rows[0, s + r] for r in range(4)]
+        four_rows(
+            ROWS + s, ROWS + s // 2, [(jnp.maximum(n, 0), n >= 0) for n in sources]
+        )
     low = lower_lanes((16, LANES))
 
     def summed(u, b):
@@ -475,7 +487,7 @@
                     sends[v - 1][at, lanes] = coarse
                 return carry
 
-            lax.fori_loop(0, HALF, gather, 0, unroll=16)
+            lax.fori_loop(0, HALF, gather, 0, unroll=32)
 
 
 def make_sums(moved_rows, columns, targets, left, halves, ghosts, far):

time: 131 us -> 127 us (0.969)
  Pallas kernels: 66.7 us -> 63 us
    pallas_call x1, Pallas kernels: 26.7 us -> 24.3 us  [make_sums(): pl.pallas_call(sums_kernel, grid_spec=pltpu.PrefetchScalarGridSpec(num_sc...]
where the time goes in v5:
time: 127 us; the launch traced here: 126 us
  Pallas kernels  63 us (50%)
  starting transfers between devices  39.8 us (31%)
  waiting for transfers between devices  19.7 us (16%)
  local copies, waits for them, and re-layouts  2.74 us (2%)
    ppermute x12, starting transfers between devices, shifted(): return lax.ppermute(value, axis, pairs)  33.8 us
    pallas_call x1, Pallas kernels, make_sums(): pl.pallas_call(sums_kernel, grid_spec=pltpu.PrefetchScalarGridSpec(num_sc...  24.3 us
    pallas_call x1, Pallas kernels, make_left(): pl.pallas_call(left_kernel, grid=(2, 2 * STEPS), in_specs=[whole((1, ROWS...  22.3 us
    ppermute x12, waiting for transfers between devices, shifted(): return lax.ppermute(value, axis, pairs)  19.7 us
    pallas_call x1, Pallas kernels, pack(): pl.pallas_call(pack_kernel, grid_spec=pltpu.PrefetchScalarGridSpec(num_sc...  12.6 us
    all_to_all x1, starting transfers between devices, one_shard(): lax.all_to_all(far.reshape(LAYERS, FAR * ROW_LEN, LANES), 'gz', split_axi...  6 us
    pallas_call x1, Pallas kernels, make_final(): pl.pallas_call(final_kernel, grid=(1,), in_specs=[pl.BlockSpec((1, U_DEV)...  3.82 us
    unnamed x20, local copies, waits for them, and re-layouts  2.66 us
  transfers between devices with their start and end apart: 13, of which 3 were waited for; matrix products, arithmetic and copies ran while one was open for 1% of the time, Pallas kernels for 18%

profile of v5, /device:TPU:23, one launch (start us, length us, event | category | flops | bytes accessed | tf_op | source)
XLA Modules:
  0.0 126.4 jit_solution(14110395139119282905)
XLA Ops:
  0.0 12.6 %pack.1 = (bf16[8192,128]{1,0:T(8,128)(2,1)}, bf16[2064,128]{1,0:T(8,128)(2,1)}, bf16[2064,128]{1,0:T(8,128)(2,1)}, bf16[2064,128]{1,0:T(8,128)(2,1)}, bf16[2064...) custom-call(s32[1]{0:T(128)} %bitcast.5.layer, ...), custom_call_target="tpu_custom_call" | custom-call | flops 2000000000 | bytes 23000000 | tf_op jit(solution)/shard_map/pack/pallas_call | solution.py:171
  12.6 6.0 %all-to-all-start = ((bf16[8,448,128]{2,1,0:T(8,128)(2,1)}), bf16[8,448,128]{2,1,0:T(8,128)(2,1)S(1)}, u32[]{:S(2)}, u32[]{:S(2)}) async-start(bf16[8,448,128]{2,1,0:T(8,128)(2,1)} %bitcast.14), calls=%async_computation | async-start | bytes 1835008 | tf_op jit(solution)/shard_map/all_to_all | solution.py:595
  18.6 2.1 %collective-permute-start = (bf16[2064,128]{1,0:T(8,128)(2,1)}, bf16[2064,128]{1,0:T(8,128)(2,1)}, u32[]{:S(2)}, u32[]{:S(2)}) collective-permute-start(bf16[2064,128]{1,0:T(8,128)(2,1)} %get-tuple-element.22), channel_id=1, source_target_pairs={{32,0},{64,32},{96,64},{33,1},{65,33},{97,65},{34,2},{66,34},{98,6... | collective-permute-start | bytes 1585160 | tf_op jit(solution)/shard_map/ppermute | solution.py:42
  20.6 4.0 %collective-permute-start.1 = (bf16[2064,128]{1,0:T(8,128)(2,1)}, bf16[2064,128]{1,0:T(8,128)(2,1)}, u32[]{:S(2)}, u32[]{:S(2)}) collective-permute-start(bf16[2064,128]{1,0:T(8,128)(2,1)} %get-tuple-element.23), channel_id=1, source_target_pairs={{0,32},{32,64},{64,96},{1,33},{33,65},{65,97},{2,34},{34,66},{66,9... | collective-permute-start | bytes 1585160 | tf_op jit(solution)/shard_map/ppermute | solution.py:42
  24.6 3.2 %collective-permute-start.2 = (bf16[2064,128]{1,0:T(8,128)(2,1)}, bf16[2064,128]{1,0:T(8,128)(2,1)}, u32[]{:S(2)}, u32[]{:S(2)}) collective-permute-start(bf16[2064,128]{1,0:T(8,128)(2,1)} %get-tuple-element.24), channel_id=1, source_target_pairs={{8,0},{16,8},{24,16},{9,1},{17,9},{25,17},{10,2},{18,10},{26,18},{... | collective-permute-start | bytes 1585160 | tf_op jit(solution)/shard_map/ppermute | solution.py:42
  27.9 2.7 %collective-permute-start.4 = (bf16[2960,128]{1,0:T(8,128)(2,1)}, bf16[2960,128]{1,0:T(8,128)(2,1)S(1)}, u32[]{:S(2)}, u32[]{:S(2)}) collective-permute-start(bf16[2960,128]{1,0:T(8,128)(2,1)} %get-tuple-element.26), channel_id=1, source_target_pairs={{1,0},{2,1},{3,2},{4,3},{5,4},{6,5},{7,6},{9,8},{10,9},{11,10},{12... | collective-permute-start | bytes 2273288 | tf_op jit(solution)/shard_map/ppermute | solution.py:42
  30.6 3.5 %collective-permute-start.5 = (bf16[2960,128]{1,0:T(8,128)(2,1)}, bf16[2960,128]{1,0:T(8,128)(2,1)}, u32[]{:S(2)}, u32[]{:S(2)}) collective-permute-start(bf16[2960,128]{1,0:T(8,128)(2,1)} %get-tuple-element.27), channel_id=1, source_target_pairs={{0,1},{1,2},{2,3},{3,4},{4,5},{5,6},{6,7},{8,9},{9,10},{10,11},{11... | collective-permute-start | bytes 2273288 | tf_op jit(solution)/shard_map/ppermute | solution.py:42
  34.2 0.0 copy-start.9
  34.2 22.3 %left.1.left_hbm = bf16[4,256,64,128]{3,2,1,0:T(8,128)(2,1)} custom-call(s32[1,256]{1,0:T(1,128)} %bitcast.17, bf16[64,448,256]{2,1,0:T(8,128)(2,1)} %bitcast.12, bf16[8192,128]{1,0:T(8,128)(2,1)} %get-tuple-element.21.halves), custom_call_target="tpu_custom_call" | custom-call | flops 12000000000 | bytes 60000000 | tf_op jit(solution)/shard_map/left/pallas_call | solution.py:302
  56.5 0.1 iota_add_fusion
  56.6 0.1 add.81
  56.7 0.0 collective-permute-done.g0
  56.7 1.3 %collective-permute-start.3 = (bf16[2064,128]{1,0:T(8,128)(2,1)}, bf16[2064,128]{1,0:T(8,128)(2,1)S(1)}, u32[]{:S(2)}, u32[]{:S(2)}) collective-permute-start(bf16[2064,128]{1,0:T(8,128)(2,1)} %get-tuple-element.25), channel_id=1, source_target_pairs={{0,8},{8,16},{16,24},{1,9},{9,17},{17,25},{2,10},{10,18},{18,26},{... | collective-permute-start | bytes 1585160 | tf_op jit(solution)/shard_map/ppermute | solution.py:42
  58.0 0.1 broadcast_compare_fusion
  58.1 0.2 select_reduce_fusion
  58.2 0.6 add_bitcast_fusion.moved_rows
  58.9 13.8 %collective-permute-done.3.g3 = bf16[2064,128]{1,0:T(8,128)(2,1)S(1)} collective-permute-done((bf16[2064,128]{1,0:T(8,128)(2,1)}, bf16[2064,128]{1,0:T(8,128)(2,1)S(1)}, u32[]{:S(2)}, u32[]{:S(2)}) %collective-permute-start.3) | collective-permute-done | bytes 528416 | tf_op jit(solution)/shard_map/ppermute | solution.py:42
  72.6 0.8 copy-done.2
  73.5 0.0 copy-start
  73.5 0.8 copy-done.1
  74.3 0.3 copy-done
  74.6 24.3 %sums.1 = (bf16[32,4096]{1,0:T(8,128)(2,1)}, bf16[32,4096]{1,0:T(8,128)(2,1)}, bf16[32,4096]{1,0:T(8,128)(2,1)}, bf16[32,4096]{1,0:T(8,128)(2,1)}, bf16[32,4096]...) custom-call(s32[1,24]{1,0:T(1,128)} %add_bitcast_fusion.moved_rows, ...), custom_call_target="tpu_custom_call" | custom-call | flops 8000000000 | bytes 30000000 | tf_op jit(solution)/shard_map/sums/pallas_call | solution.py:495
  99.0 1.9 %collective-permute-start.6 = (bf16[32,4096]{1,0:T(8,128)(2,1)}, bf16[32,4096]{1,0:T(8,128)(2,1)S(1)}, u32[]{:S(2)}, u32[]{:S(2)}) collective-permute-start(bf16[32,4096]{1,0:T(8,128)(2,1)} %get-tuple-element.31), channel_id=1, source_target_pairs={{0,32},{32,64},{64,96},{1,33},{33,65},{65,97},{2,34},{34,66},{66,9... | collective-permute-start | bytes 786440 | tf_op jit(solution)/shard_map/ppermute | solution.py:42
  100.9 3.4 %collective-permute-start.7 = (bf16[32,4096]{1,0:T(8,128)(2,1)}, bf16[32,4096]{1,0:T(8,128)(2,1)S(1)}, u32[]{:S(2)}, u32[]{:S(2)}) collective-permute-start(bf16[32,4096]{1,0:T(8,128)(2,1)} %get-tuple-element.32), channel_id=1, source_target_pairs={{32,0},{64,32},{96,64},{33,1},{65,33},{97,65},{34,2},{66,34},{98,6... | collective-permute-start | bytes 786440 | tf_op jit(solution)/shard_map/ppermute | solution.py:42
  104.2 1.3 %collective-permute-start.8 = (bf16[32,4096]{1,0:T(8,128)(2,1)}, bf16[32,4096]{1,0:T(8,128)(2,1)S(1)}, u32[]{:S(2)}, u32[]{:S(2)}) collective-permute-start(bf16[32,4096]{1,0:T(8,128)(2,1)} %get-tuple-element.33), channel_id=1, source_target_pairs={{0,8},{8,16},{16,24},{1,9},{9,17},{17,25},{2,10},{10,18},{18,26},{... | collective-permute-start | bytes 786440 | tf_op jit(solution)/shard_map/ppermute | solution.py:42
  105.5 4.0 %collective-permute-start.9 = (bf16[32,4096]{1,0:T(8,128)(2,1)}, bf16[32,4096]{1,0:T(8,128)(2,1)S(1)}, u32[]{:S(2)}, u32[]{:S(2)}) collective-permute-start(bf16[32,4096]{1,0:T(8,128)(2,1)} %get-tuple-element.34), channel_id=1, source_target_pairs={{8,0},{16,8},{24,16},{9,1},{17,9},{25,17},{10,2},{18,10},{26,18},{... | collective-permute-start | bytes 786440 | tf_op jit(solution)/shard_map/ppermute | solution.py:42
  109.6 4.4 %collective-permute-start.10 = (bf16[32,4096]{1,0:T(8,128)(2,1)}, bf16[32,4096]{1,0:T(8,128)(2,1)S(1)}, u32[]{:S(2)}, u32[]{:S(2)}) collective-permute-start(bf16[32,4096]{1,0:T(8,128)(2,1)} %get-tuple-element.35), channel_id=1, source_target_pairs={{0,1},{1,2},{2,3},{3,4},{4,5},{5,6},{6,7},{8,9},{9,10},{10,11},{11... | collective-permute-start | bytes 786440 | tf_op jit(solution)/shard_map/ppermute | solution.py:42
  114.0 1.9 %collective-permute-start.11 = (bf16[32,4096]{1,0:T(8,128)(2,1)}, bf16[32,4096]{1,0:T(8,128)(2,1)S(1)}, u32[]{:S(2)}, u32[]{:S(2)}) collective-permute-start(bf16[32,4096]{1,0:T(8,128)(2,1)} %get-tuple-element.36), channel_id=1, source_target_pairs={{1,0},{2,1},{3,2},{4,3},{5,4},{6,5},{7,6},{9,8},{10,9},{11,10},{12... | collective-permute-start | bytes 786440 | tf_op jit(solution)/shard_map/ppermute | solution.py:42
  116.0 1.6 %collective-permute-done.10.r4 = bf16[32,4096]{1,0:T(8,128)(2,1)S(1)} collective-permute-done((bf16[32,4096]{1,0:T(8,128)(2,1)}, bf16[32,4096]{1,0:T(8,128)(2,1)S(1)}, u32[]{:S(2)}, u32[]{:S(2)}) %collective-permute-start.10) | collective-permute-done | bytes 262176 | tf_op jit(solution)/shard_map/ppermute | solution.py:42
  117.6 4.3 %collective-permute-done.11.r5 = bf16[32,4096]{1,0:T(8,128)(2,1)S(1)} collective-permute-done((bf16[32,4096]{1,0:T(8,128)(2,1)}, bf16[32,4096]{1,0:T(8,128)(2,1)S(1)}, u32[]{:S(2)}, u32[]{:S(2)}) %collective-permute-start.11) | collective-permute-done | bytes 262176 | tf_op jit(solution)/shard_map/ppermute | solution.py:42
  122.0 0.7 copy-done.8
  122.6 3.8 %final.1 = f32[64,4096]{1,0:T(8,128)} custom-call(s32[1,224]{1,0:T(1,128)} %touched.3, bf16[32,4096]{1,0:T(8,128)(2,1)} %get-tuple-element.29.own, bf16[32,4096]{1,0:T(8,128)(2,1)} %get-tuple-element.30.fine, bf16[32,4096]{1,0:T(8,128)(2,1)} %copy-done.3, bf16[32,4096]{1,0:T(8,128)(2,1)} %copy-done.4, bf16[32,4096]{1,0:T(8,128)(2,1)} %copy-done.5, ...), custom_call_target="tpu_custom_call" | custom-call | tf_op jit(solution)/shard_map/final/pallas_call | solution.py:563
  (26 shorter events, 0.1 us)
Async XLA Ops:
  12.6 60.9 %all-to-all-start = ((bf16[8,448,128]{2,1,0:T(8,128)(2,1)}), bf16[8,448,128]{2,1,0:T(8,128)(2,1)S(1)}, u32[]{:S(2)}, u32[]{:S(2)}) async-start(bf16[8,448,128]{2,1,0:T(8,128)(2,1)} %bitcast.14), calls=%async_computation | async-start | bytes 1835008 | tf_op jit(solution)/shard_map/all_to_all | solution.py:595
  18.6 38.1 %collective-permute-start = (bf16[2064,128]{1,0:T(8,128)(2,1)}, bf16[2064,128]{1,0:T(8,128)(2,1)}, u32[]{:S(2)}, u32[]{:S(2)}) collective-permute-start(bf16[2064,128]{1,0:T(8,128)(2,1)} %get-tuple-element.22), channel_id=1, source_target_pairs={{32,0},{64,32},{96,64},{33,1},{65,33},{97,65},{34,2},{66,34},{98,6... | collective-permute-start | bytes 1585160 | tf_op jit(solution)/shard_map/ppermute | solution.py:42
  20.6 38.2 %collective-permute-start.1 = (bf16[2064,128]{1,0:T(8,128)(2,1)}, bf16[2064,128]{1,0:T(8,128)(2,1)}, u32[]{:S(2)}, u32[]{:S(2)}) collective-permute-start(bf16[2064,128]{1,0:T(8,128)(2,1)} %get-tuple-element.23), channel_id=1, source_target_pairs={{0,32},{32,64},{64,96},{1,33},{33,65},{65,97},{2,34},{34,66},{66,9... | collective-permute-start | bytes 1585160 | tf_op jit(solution)/shard_map/ppermute | solution.py:42
  24.6 34.2 %collective-permute-start.2 = (bf16[2064,128]{1,0:T(8,128)(2,1)}, bf16[2064,128]{1,0:T(8,128)(2,1)}, u32[]{:S(2)}, u32[]{:S(2)}) collective-permute-start(bf16[2064,128]{1,0:T(8,128)(2,1)} %get-tuple-element.24), channel_id=1, source_target_pairs={{8,0},{16,8},{24,16},{9,1},{17,9},{25,17},{10,2},{18,10},{26,18},{... | collective-permute-start | bytes 1585160 | tf_op jit(solution)/shard_map/ppermute | solution.py:42
  27.9 44.7 %collective-permute-start.4 = (bf16[2960,128]{1,0:T(8,128)(2,1)}, bf16[2960,128]{1,0:T(8,128)(2,1)S(1)}, u32[]{:S(2)}, u32[]{:S(2)}) collective-permute-start(bf16[2960,128]{1,0:T(8,128)(2,1)} %get-tuple-element.26), channel_id=1, source_target_pairs={{1,0},{2,1},{3,2},{4,3},{5,4},{6,5},{7,6},{9,8},{10,9},{11,10},{12... | collective-permute-start | bytes 2273288 | tf_op jit(solution)/shard_map/ppermute | solution.py:42
  30.6 42.8 %collective-permute-start.5 = (bf16[2960,128]{1,0:T(8,128)(2,1)}, bf16[2960,128]{1,0:T(8,128)(2,1)}, u32[]{:S(2)}, u32[]{:S(2)}) collective-permute-start(bf16[2960,128]{1,0:T(8,128)(2,1)} %get-tuple-element.27), channel_id=1, source_target_pairs={{0,1},{1,2},{2,3},{3,4},{4,5},{5,6},{6,7},{8,9},{9,10},{10,11},{11... | collective-permute-start | bytes 2273288 | tf_op jit(solution)/shard_map/ppermute | solution.py:42
  34.2 23.9 %copy-start.9 = (s32[256]{0:T(256)S(1)}, s32[256]{0:T(256)}, u32[]{:S(2)}) copy-start(s32[256]{0:T(256)} %param.11) | copy-start | bytes 3076
  56.7 16.0 %collective-permute-start.3 = (bf16[2064,128]{1,0:T(8,128)(2,1)}, bf16[2064,128]{1,0:T(8,128)(2,1)S(1)}, u32[]{:S(2)}, u32[]{:S(2)}) collective-permute-start(bf16[2064,128]{1,0:T(8,128)(2,1)} %get-tuple-element.25), channel_id=1, source_target_pairs={{0,8},{8,16},{16,24},{1,9},{9,17},{17,25},{2,10},{10,18},{18,26},{... | collective-permute-start | bytes 1585160 | tf_op jit(solution)/shard_map/ppermute | solution.py:42
  72.6 0.8 copy-start.2
  73.5 0.9 copy-start.1
  73.5 1.2 copy-start
  99.0 15.1 %collective-permute-start.6 = (bf16[32,4096]{1,0:T(8,128)(2,1)}, bf16[32,4096]{1,0:T(8,128)(2,1)S(1)}, u32[]{:S(2)}, u32[]{:S(2)}) collective-permute-start(bf16[32,4096]{1,0:T(8,128)(2,1)} %get-tuple-element.31), channel_id=1, source_target_pairs={{0,32},{32,64},{64,96},{1,33},{33,65},{65,97},{2,34},{34,66},{66,9... | collective-permute-start | bytes 786440 | tf_op jit(solution)/shard_map/ppermute | solution.py:42
  100.9 15.1 %collective-permute-start.7 = (bf16[32,4096]{1,0:T(8,128)(2,1)}, bf16[32,4096]{1,0:T(8,128)(2,1)S(1)}, u32[]{:S(2)}, u32[]{:S(2)}) collective-permute-start(bf16[32,4096]{1,0:T(8,128)(2,1)} %get-tuple-element.32), channel_id=1, source_target_pairs={{32,0},{64,32},{96,64},{33,1},{65,33},{97,65},{34,2},{66,34},{98,6... | collective-permute-start | bytes 786440 | tf_op jit(solution)/shard_map/ppermute | solution.py:42
  104.2 11.7 %collective-permute-start.8 = (bf16[32,4096]{1,0:T(8,128)(2,1)}, bf16[32,4096]{1,0:T(8,128)(2,1)S(1)}, u32[]{:S(2)}, u32[]{:S(2)}) collective-permute-start(bf16[32,4096]{1,0:T(8,128)(2,1)} %get-tuple-element.33), channel_id=1, source_target_pairs={{0,8},{8,16},{16,24},{1,9},{9,17},{17,25},{2,10},{10,18},{18,26},{... | collective-permute-start | bytes 786440 | tf_op jit(solution)/shard_map/ppermute | solution.py:42
  105.5 10.4 %collective-permute-start.9 = (bf16[32,4096]{1,0:T(8,128)(2,1)}, bf16[32,4096]{1,0:T(8,128)(2,1)S(1)}, u32[]{:S(2)}, u32[]{:S(2)}) collective-permute-start(bf16[32,4096]{1,0:T(8,128)(2,1)} %get-tuple-element.34), channel_id=1, source_target_pairs={{8,0},{16,8},{24,16},{9,1},{17,9},{25,17},{10,2},{18,10},{26,18},{... | collective-permute-start | bytes 786440 | tf_op jit(solution)/shard_map/ppermute | solution.py:42
  109.6 8.1 %collective-permute-start.10 = (bf16[32,4096]{1,0:T(8,128)(2,1)}, bf16[32,4096]{1,0:T(8,128)(2,1)S(1)}, u32[]{:S(2)}, u32[]{:S(2)}) collective-permute-start(bf16[32,4096]{1,0:T(8,128)(2,1)} %get-tuple-element.35), channel_id=1, source_target_pairs={{0,1},{1,2},{2,3},{3,4},{4,5},{5,6},{6,7},{8,9},{9,10},{10,11},{11... | collective-permute-start | bytes 786440 | tf_op jit(solution)/shard_map/ppermute | solution.py:42
  114.0 7.9 %copy-start.3 = (bf16[32,4096]{1,0:T(8,128)(2,1)}, bf16[32,4096]{1,0:T(8,128)(2,1)S(1)}, u32[]{:S(2)}) copy-start(bf16[32,4096]{1,0:T(8,128)(2,1)S(1)} %collective-permute-done.6.r0) | copy-start | bytes 786436
  114.0 7.9 %collective-permute-start.11 = (bf16[32,4096]{1,0:T(8,128)(2,1)}, bf16[32,4096]{1,0:T(8,128)(2,1)S(1)}, u32[]{:S(2)}, u32[]{:S(2)}) collective-permute-start(bf16[32,4096]{1,0:T(8,128)(2,1)} %get-tuple-element.36), channel_id=1, source_target_pairs={{1,0},{2,1},{3,2},{4,3},{5,4},{6,5},{7,6},{9,8},{10,9},{11,10},{12... | collective-permute-start | bytes 786440 | tf_op jit(solution)/shard_map/ppermute | solution.py:42
  116.0 6.0 %copy-start.4 = (bf16[32,4096]{1,0:T(8,128)(2,1)}, bf16[32,4096]{1,0:T(8,128)(2,1)S(1)}, u32[]{:S(2)}) copy-start(bf16[32,4096]{1,0:T(8,128)(2,1)S(1)} %collective-permute-done.7.r1) | copy-start | bytes 786436
  116.0 6.0 %copy-start.5 = (bf16[32,4096]{1,0:T(8,128)(2,1)}, bf16[32,4096]{1,0:T(8,128)(2,1)S(1)}, u32[]{:S(2)}) copy-start(bf16[32,4096]{1,0:T(8,128)(2,1)S(1)} %collective-permute-done.8.r2) | copy-start | bytes 786436
  116.0 5.9 %copy-start.6 = (bf16[32,4096]{1,0:T(8,128)(2,1)}, bf16[32,4096]{1,0:T(8,128)(2,1)S(1)}, u32[]{:S(2)}) copy-start(bf16[32,4096]{1,0:T(8,128)(2,1)S(1)} %collective-permute-done.9.r3) | copy-start | bytes 786436
  117.6 4.3 %copy-start.7 = (bf16[32,4096]{1,0:T(8,128)(2,1)}, bf16[32,4096]{1,0:T(8,128)(2,1)S(1)}, u32[]{:S(2)}) copy-start(bf16[32,4096]{1,0:T(8,128)(2,1)S(1)} %collective-permute-done.10.r4) | copy-start | bytes 786436
  121.9 0.7 copy-start.8

commit v6 on v5

--- a/solution.py
+++ b/solution.py
@@ -141,9 +141,11 @@
     lax.fori_loop(0, X_PARTS, some_planes, 0)
     for j in range(6):
         sends[j][GHOST_LEN:NEAR_AT, :] = extra
-        out_copies.append(pltpu.make_async_copy(sends[j], outs[j], out_sem.at[j]))
-        if j < 4:
-            out_copies[-1].start()
+        some = pl.ds(0, NEAR_AT)
+        out_copies.append(
+            pltpu.make_async_copy(sends[j].at[some], outs[j].at[some], out_sem.at[j])
+        )
+        out_copies[-1].start()
     for r in range(SENT):
         if r < LAYERS * FAR:
             out, base = far, r * ROW_LEN
@@ -157,9 +159,15 @@
         out[base + 3 * B : base + ROW_LEN, :] = jnp.concatenate(
             [got[3][:HALF, :B], got[3][HALF:, :B]], axis=1
         )
-    out_copies.append(pltpu.make_async_copy(far, far_out, out_sem.at[7]))
-    for copy in out_copies[5:]:
+    late_copies = [pltpu.make_async_copy(far, far_out, out_sem.at[7])]
+    for j in (4, 5):
+        some = pl.ds(NEAR_AT, NEAR * ROW_LEN)
+        late_copies.append(
+            pltpu.make_async_copy(sends[j].at[some], outs[j].at[some], out_sem.at[j + 4])
+        )
+    for copy in late_copies:
         copy.start()
+    out_copies += late_copies
     for copy in out_copies:
         copy.wait()
 
@@ -190,7 +198,7 @@
             + [
                 pltpu.SemaphoreType.DMA((P_PARTS,)),
                 pltpu.SemaphoreType.DMA((X_PARTS,)),
-                pltpu.SemaphoreType.DMA((8,)),
+                pltpu.SemaphoreType.DMA((10,)),
             ],
         ),
         out_shape=[jax.ShapeDtypeStruct(shape, bf16) for shape in shapes],
@@ -329,7 +337,7 @@
     )(arrival, blocks, halves)
 
 
-PARTS = 8
+PARTS = 4
 TALL = B + 1
 
 
@@ -455,7 +463,7 @@
         left_copy(n).wait()
         for m in range(part // 4):
             i = n * part + 4 * m
-            pair = (n >> 1) * R_STEP + (n & 1) * (part // 2) + 2 * m
+            pair = n * part + 2 * m
             four_rows(i, pair, [(i + r, True) for r in range(4)])
         return carry
 

time: 127 us -> 126 us (level)
  no operation moved by 1% of the time
where the time goes in v6:
time: 126 us; the launch traced here: 125 us
  Pallas kernels  61.8 us (49%)
  starting transfers between devices  39.8 us (32%)
  waiting for transfers between devices  19.7 us (16%)
  local copies, waits for them, and re-layouts  2.74 us (2%)
    ppermute x12, starting transfers between devices, shifted(): return lax.ppermute(value, axis, pairs)  33.8 us
    pallas_call x1, Pallas kernels, make_sums(): pl.pallas_call(sums_kernel, grid_spec=pltpu.PrefetchScalarGridSpec(num_sc...  23.1 us
    pallas_call x1, Pallas kernels, make_left(): pl.pallas_call(left_kernel, grid=(2, 2 * STEPS), in_specs=[whole((1, ROWS...  22.3 us
    ppermute x12, waiting for transfers between devices, shifted(): return lax.ppermute(value, axis, pairs)  19.7 us
    pallas_call x1, Pallas kernels, pack(): pl.pallas_call(pack_kernel, grid_spec=pltpu.PrefetchScalarGridSpec(num_sc...  12.6 us
    all_to_all x1, starting transfers between devices, one_shard(): lax.all_to_all(far.reshape(LAYERS, FAR * ROW_LEN, LANES), 'gz', split_axi...  6 us
    pallas_call x1, Pallas kernels, make_final(): pl.pallas_call(final_kernel, grid=(1,), in_specs=[pl.BlockSpec((1, U_DEV)...  3.82 us
    unnamed x20, local copies, waits for them, and re-layouts  2.66 us
  transfers between devices with their start and end apart: 13, of which 3 were waited for; matrix products, arithmetic and copies ran while one was open for 1% of the time, Pallas kernels for 18%

profile of v6, /device:TPU:23, one launch (start us, length us, event | category | flops | bytes accessed | tf_op | source)
XLA Modules:
  0.0 125.2 jit_solution(17472670566334406991)
XLA Ops:
  0.0 12.6 %pack.1 = (bf16[8192,128]{1,0:T(8,128)(2,1)}, bf16[2064,128]{1,0:T(8,128)(2,1)}, bf16[2064,128]{1,0:T(8,128)(2,1)}, bf16[2064,128]{1,0:T(8,128)(2,1)}, bf16[2064...) custom-call(s32[1]{0:T(128)} %bitcast.5.layer, ...), custom_call_target="tpu_custom_call" | custom-call | flops 2000000000 | bytes 23000000 | tf_op jit(solution)/shard_map/pack/pallas_call | solution.py:179
  12.6 6.0 %all-to-all-start = ((bf16[8,448,128]{2,1,0:T(8,128)(2,1)}), bf16[8,448,128]{2,1,0:T(8,128)(2,1)S(1)}, u32[]{:S(2)}, u32[]{:S(2)}) async-start(bf16[8,448,128]{2,1,0:T(8,128)(2,1)} %bitcast.14), calls=%async_computation | async-start | bytes 1835008 | tf_op jit(solution)/shard_map/all_to_all | solution.py:603
  18.6 2.1 %collective-permute-start = (bf16[2064,128]{1,0:T(8,128)(2,1)}, bf16[2064,128]{1,0:T(8,128)(2,1)}, u32[]{:S(2)}, u32[]{:S(2)}) collective-permute-start(bf16[2064,128]{1,0:T(8,128)(2,1)} %get-tuple-element.22), channel_id=1, source_target_pairs={{32,0},{64,32},{96,64},{33,1},{65,33},{97,65},{34,2},{66,34},{98,6... | collective-permute-start | bytes 1585160 | tf_op jit(solution)/shard_map/ppermute | solution.py:42
  20.6 4.0 %collective-permute-start.1 = (bf16[2064,128]{1,0:T(8,128)(2,1)}, bf16[2064,128]{1,0:T(8,128)(2,1)}, u32[]{:S(2)}, u32[]{:S(2)}) collective-permute-start(bf16[2064,128]{1,0:T(8,128)(2,1)} %get-tuple-element.23), channel_id=1, source_target_pairs={{0,32},{32,64},{64,96},{1,33},{33,65},{65,97},{2,34},{34,66},{66,9... | collective-permute-start | bytes 1585160 | tf_op jit(solution)/shard_map/ppermute | solution.py:42
  24.6 3.2 %collective-permute-start.2 = (bf16[2064,128]{1,0:T(8,128)(2,1)}, bf16[2064,128]{1,0:T(8,128)(2,1)}, u32[]{:S(2)}, u32[]{:S(2)}) collective-permute-start(bf16[2064,128]{1,0:T(8,128)(2,1)} %get-tuple-element.24), channel_id=1, source_target_pairs={{8,0},{16,8},{24,16},{9,1},{17,9},{25,17},{10,2},{18,10},{26,18},{... | collective-permute-start | bytes 1585160 | tf_op jit(solution)/shard_map/ppermute | solution.py:42
  27.9 2.7 %collective-permute-start.4 = (bf16[2960,128]{1,0:T(8,128)(2,1)}, bf16[2960,128]{1,0:T(8,128)(2,1)S(1)}, u32[]{:S(2)}, u32[]{:S(2)}) collective-permute-start(bf16[2960,128]{1,0:T(8,128)(2,1)} %get-tuple-element.26), channel_id=1, source_target_pairs={{1,0},{2,1},{3,2},{4,3},{5,4},{6,5},{7,6},{9,8},{10,9},{11,10},{12... | collective-permute-start | bytes 2273288 | tf_op jit(solution)/shard_map/ppermute | solution.py:42
  30.6 3.5 %collective-permute-start.5 = (bf16[2960,128]{1,0:T(8,128)(2,1)}, bf16[2960,128]{1,0:T(8,128)(2,1)}, u32[]{:S(2)}, u32[]{:S(2)}) collective-permute-start(bf16[2960,128]{1,0:T(8,128)(2,1)} %get-tuple-element.27), channel_id=1, source_target_pairs={{0,1},{1,2},{2,3},{3,4},{4,5},{5,6},{6,7},{8,9},{9,10},{10,11},{11... | collective-permute-start | bytes 2273288 | tf_op jit(solution)/shard_map/ppermute | solution.py:42
  34.2 0.0 copy-start.9
  34.2 22.3 %left.1.left_hbm = bf16[4,256,64,128]{3,2,1,0:T(8,128)(2,1)} custom-call(s32[1,256]{1,0:T(1,128)} %bitcast.17, bf16[64,448,256]{2,1,0:T(8,128)(2,1)} %bitcast.12, bf16[8192,128]{1,0:T(8,128)(2,1)} %get-tuple-element.21.halves), custom_call_target="tpu_custom_call" | custom-call | flops 12000000000 | bytes 60000000 | tf_op jit(solution)/shard_map/left/pallas_call | solution.py:310
  56.5 0.1 iota_add_fusion
  56.6 0.1 add.81
  56.7 0.0 collective-permute-done.g0
  56.7 1.3 %collective-permute-start.3 = (bf16[2064,128]{1,0:T(8,128)(2,1)}, bf16[2064,128]{1,0:T(8,128)(2,1)S(1)}, u32[]{:S(2)}, u32[]{:S(2)}) collective-permute-start(bf16[2064,128]{1,0:T(8,128)(2,1)} %get-tuple-element.25), channel_id=1, source_target_pairs={{0,8},{8,16},{16,24},{1,9},{9,17},{17,25},{2,10},{10,18},{18,26},{... | collective-permute-start | bytes 1585160 | tf_op jit(solution)/shard_map/ppermute | solution.py:42
  58.0 0.1 broadcast_compare_fusion
  58.1 0.2 select_reduce_fusion
  58.2 0.6 add_bitcast_fusion.moved_rows
  58.9 13.8 %collective-permute-done.3.g3 = bf16[2064,128]{1,0:T(8,128)(2,1)S(1)} collective-permute-done((bf16[2064,128]{1,0:T(8,128)(2,1)}, bf16[2064,128]{1,0:T(8,128)(2,1)S(1)}, u32[]{:S(2)}, u32[]{:S(2)}) %collective-permute-start.3) | collective-permute-done | bytes 528416 | tf_op jit(solution)/shard_map/ppermute | solution.py:42
  72.6 0.8 copy-done.2
  73.5 0.0 copy-start
  73.5 0.8 copy-done.1
  74.3 0.3 copy-done
  74.6 23.1 %sums.1 = (bf16[32,4096]{1,0:T(8,128)(2,1)}, bf16[32,4096]{1,0:T(8,128)(2,1)}, bf16[32,4096]{1,0:T(8,128)(2,1)}, bf16[32,4096]{1,0:T(8,128)(2,1)}, bf16[32,4096]...) custom-call(s32[1,24]{1,0:T(1,128)} %add_bitcast_fusion.moved_rows, ...), custom_call_target="tpu_custom_call" | custom-call | flops 8000000000 | bytes 30000000 | tf_op jit(solution)/shard_map/sums/pallas_call | solution.py:503
  97.7 1.9 %collective-permute-start.6 = (bf16[32,4096]{1,0:T(8,128)(2,1)}, bf16[32,4096]{1,0:T(8,128)(2,1)S(1)}, u32[]{:S(2)}, u32[]{:S(2)}) collective-permute-start(bf16[32,4096]{1,0:T(8,128)(2,1)} %get-tuple-element.31), channel_id=1, source_target_pairs={{0,32},{32,64},{64,96},{1,33},{33,65},{65,97},{2,34},{34,66},{66,9... | collective-permute-start | bytes 786440 | tf_op jit(solution)/shard_map/ppermute | solution.py:42
  99.7 3.4 %collective-permute-start.7 = (bf16[32,4096]{1,0:T(8,128)(2,1)}, bf16[32,4096]{1,0:T(8,128)(2,1)S(1)}, u32[]{:S(2)}, u32[]{:S(2)}) collective-permute-start(bf16[32,4096]{1,0:T(8,128)(2,1)} %get-tuple-element.32), channel_id=1, source_target_pairs={{32,0},{64,32},{96,64},{33,1},{65,33},{97,65},{34,2},{66,34},{98,6... | collective-permute-start | bytes 786440 | tf_op jit(solution)/shard_map/ppermute | solution.py:42
  103.0 1.3 %collective-permute-start.8 = (bf16[32,4096]{1,0:T(8,128)(2,1)}, bf16[32,4096]{1,0:T(8,128)(2,1)S(1)}, u32[]{:S(2)}, u32[]{:S(2)}) collective-permute-start(bf16[32,4096]{1,0:T(8,128)(2,1)} %get-tuple-element.33), channel_id=1, source_target_pairs={{0,8},{8,16},{16,24},{1,9},{9,17},{17,25},{2,10},{10,18},{18,26},{... | collective-permute-start | bytes 786440 | tf_op jit(solution)/shard_map/ppermute | solution.py:42
  104.3 4.0 %collective-permute-start.9 = (bf16[32,4096]{1,0:T(8,128)(2,1)}, bf16[32,4096]{1,0:T(8,128)(2,1)S(1)}, u32[]{:S(2)}, u32[]{:S(2)}) collective-permute-start(bf16[32,4096]{1,0:T(8,128)(2,1)} %get-tuple-element.34), channel_id=1, source_target_pairs={{8,0},{16,8},{24,16},{9,1},{17,9},{25,17},{10,2},{18,10},{26,18},{... | collective-permute-start | bytes 786440 | tf_op jit(solution)/shard_map/ppermute | solution.py:42
  108.3 4.4 %collective-permute-start.10 = (bf16[32,4096]{1,0:T(8,128)(2,1)}, bf16[32,4096]{1,0:T(8,128)(2,1)S(1)}, u32[]{:S(2)}, u32[]{:S(2)}) collective-permute-start(bf16[32,4096]{1,0:T(8,128)(2,1)} %get-tuple-element.35), channel_id=1, source_target_pairs={{0,1},{1,2},{2,3},{3,4},{4,5},{5,6},{6,7},{8,9},{9,10},{10,11},{11... | collective-permute-start | bytes 786440 | tf_op jit(solution)/shard_map/ppermute | solution.py:42
  112.8 1.9 %collective-permute-start.11 = (bf16[32,4096]{1,0:T(8,128)(2,1)}, bf16[32,4096]{1,0:T(8,128)(2,1)S(1)}, u32[]{:S(2)}, u32[]{:S(2)}) collective-permute-start(bf16[32,4096]{1,0:T(8,128)(2,1)} %get-tuple-element.36), channel_id=1, source_target_pairs={{1,0},{2,1},{3,2},{4,3},{5,4},{6,5},{7,6},{9,8},{10,9},{11,10},{12... | collective-permute-start | bytes 786440 | tf_op jit(solution)/shard_map/ppermute | solution.py:42
  114.8 1.6 %collective-permute-done.10.r4 = bf16[32,4096]{1,0:T(8,128)(2,1)S(1)} collective-permute-done((bf16[32,4096]{1,0:T(8,128)(2,1)}, bf16[32,4096]{1,0:T(8,128)(2,1)S(1)}, u32[]{:S(2)}, u32[]{:S(2)}) %collective-permute-start.10) | collective-permute-done | bytes 262176 | tf_op jit(solution)/shard_map/ppermute | solution.py:42
  116.4 4.3 %collective-permute-done.11.r5 = bf16[32,4096]{1,0:T(8,128)(2,1)S(1)} collective-permute-done((bf16[32,4096]{1,0:T(8,128)(2,1)}, bf16[32,4096]{1,0:T(8,128)(2,1)S(1)}, u32[]{:S(2)}, u32[]{:S(2)}) %collective-permute-start.11) | collective-permute-done | bytes 262176 | tf_op jit(solution)/shard_map/ppermute | solution.py:42
  120.7 0.7 copy-done.8
  121.4 3.8 %final.1 = f32[64,4096]{1,0:T(8,128)} custom-call(s32[1,224]{1,0:T(1,128)} %touched.3, bf16[32,4096]{1,0:T(8,128)(2,1)} %get-tuple-element.29.own, bf16[32,4096]{1,0:T(8,128)(2,1)} %get-tuple-element.30.fine, bf16[32,4096]{1,0:T(8,128)(2,1)} %copy-done.3, bf16[32,4096]{1,0:T(8,128)(2,1)} %copy-done.4, bf16[32,4096]{1,0:T(8,128)(2,1)} %copy-done.5, ...), custom_call_target="tpu_custom_call" | custom-call | tf_op jit(solution)/shard_map/final/pallas_call | solution.py:571
  (26 shorter events, 0.1 us)
Async XLA Ops:
  12.6 60.9 %all-to-all-start = ((bf16[8,448,128]{2,1,0:T(8,128)(2,1)}), bf16[8,448,128]{2,1,0:T(8,128)(2,1)S(1)}, u32[]{:S(2)}, u32[]{:S(2)}) async-start(bf16[8,448,128]{2,1,0:T(8,128)(2,1)} %bitcast.14), calls=%async_computation | async-start | bytes 1835008 | tf_op jit(solution)/shard_map/all_to_all | solution.py:603
  18.6 38.1 %collective-permute-start = (bf16[2064,128]{1,0:T(8,128)(2,1)}, bf16[2064,128]{1,0:T(8,128)(2,1)}, u32[]{:S(2)}, u32[]{:S(2)}) collective-permute-start(bf16[2064,128]{1,0:T(8,128)(2,1)} %get-tuple-element.22), channel_id=1, source_target_pairs={{32,0},{64,32},{96,64},{33,1},{65,33},{97,65},{34,2},{66,34},{98,6... | collective-permute-start | bytes 1585160 | tf_op jit(solution)/shard_map/ppermute | solution.py:42
  20.6 38.2 %collective-permute-start.1 = (bf16[2064,128]{1,0:T(8,128)(2,1)}, bf16[2064,128]{1,0:T(8,128)(2,1)}, u32[]{:S(2)}, u32[]{:S(2)}) collective-permute-start(bf16[2064,128]{1,0:T(8,128)(2,1)} %get-tuple-element.23), channel_id=1, source_target_pairs={{0,32},{32,64},{64,96},{1,33},{33,65},{65,97},{2,34},{34,66},{66,9... | collective-permute-start | bytes 1585160 | tf_op jit(solution)/shard_map/ppermute | solution.py:42
  24.6 34.2 %collective-permute-start.2 = (bf16[2064,128]{1,0:T(8,128)(2,1)}, bf16[2064,128]{1,0:T(8,128)(2,1)}, u32[]{:S(2)}, u32[]{:S(2)}) collective-permute-start(bf16[2064,128]{1,0:T(8,128)(2,1)} %get-tuple-element.24), channel_id=1, source_target_pairs={{8,0},{16,8},{24,16},{9,1},{17,9},{25,17},{10,2},{18,10},{26,18},{... | collective-permute-start | bytes 1585160 | tf_op jit(solution)/shard_map/ppermute | solution.py:42
  27.9 44.8 %collective-permute-start.4 = (bf16[2960,128]{1,0:T(8,128)(2,1)}, bf16[2960,128]{1,0:T(8,128)(2,1)S(1)}, u32[]{:S(2)}, u32[]{:S(2)}) collective-permute-start(bf16[2960,128]{1,0:T(8,128)(2,1)} %get-tuple-element.26), channel_id=1, source_target_pairs={{1,0},{2,1},{3,2},{4,3},{5,4},{6,5},{7,6},{9,8},{10,9},{11,10},{12... | collective-permute-start | bytes 2273288 | tf_op jit(solution)/shard_map/ppermute | solution.py:42
  30.6 42.8 %collective-permute-start.5 = (bf16[2960,128]{1,0:T(8,128)(2,1)}, bf16[2960,128]{1,0:T(8,128)(2,1)}, u32[]{:S(2)}, u32[]{:S(2)}) collective-permute-start(bf16[2960,128]{1,0:T(8,128)(2,1)} %get-tuple-element.27), channel_id=1, source_target_pairs={{0,1},{1,2},{2,3},{3,4},{4,5},{5,6},{6,7},{8,9},{9,10},{10,11},{11... | collective-permute-start | bytes 2273288 | tf_op jit(solution)/shard_map/ppermute | solution.py:42
  34.2 23.9 %copy-start.9 = (s32[256]{0:T(256)S(1)}, s32[256]{0:T(256)}, u32[]{:S(2)}) copy-start(s32[256]{0:T(256)} %param.11) | copy-start | bytes 3076
  56.7 16.0 %collective-permute-start.3 = (bf16[2064,128]{1,0:T(8,128)(2,1)}, bf16[2064,128]{1,0:T(8,128)(2,1)S(1)}, u32[]{:S(2)}, u32[]{:S(2)}) collective-permute-start(bf16[2064,128]{1,0:T(8,128)(2,1)} %get-tuple-element.25), channel_id=1, source_target_pairs={{0,8},{8,16},{16,24},{1,9},{9,17},{17,25},{2,10},{10,18},{18,26},{... | collective-permute-start | bytes 1585160 | tf_op jit(solution)/shard_map/ppermute | solution.py:42
  72.6 0.8 copy-start.2
  73.5 0.9 copy-start.1
  73.5 1.2 copy-start
  97.7 15.0 %collective-permute-start.6 = (bf16[32,4096]{1,0:T(8,128)(2,1)}, bf16[32,4096]{1,0:T(8,128)(2,1)S(1)}, u32[]{:S(2)}, u32[]{:S(2)}) collective-permute-start(bf16[32,4096]{1,0:T(8,128)(2,1)} %get-tuple-element.31), channel_id=1, source_target_pairs={{0,32},{32,64},{64,96},{1,33},{33,65},{65,97},{2,34},{34,66},{66,9... | collective-permute-start | bytes 786440 | tf_op jit(solution)/shard_map/ppermute | solution.py:42
  99.7 15.1 %collective-permute-start.7 = (bf16[32,4096]{1,0:T(8,128)(2,1)}, bf16[32,4096]{1,0:T(8,128)(2,1)S(1)}, u32[]{:S(2)}, u32[]{:S(2)}) collective-permute-start(bf16[32,4096]{1,0:T(8,128)(2,1)} %get-tuple-element.32), channel_id=1, source_target_pairs={{32,0},{64,32},{96,64},{33,1},{65,33},{97,65},{34,2},{66,34},{98,6... | collective-permute-start | bytes 786440 | tf_op jit(solution)/shard_map/ppermute | solution.py:42
  103.0 11.7 %collective-permute-start.8 = (bf16[32,4096]{1,0:T(8,128)(2,1)}, bf16[32,4096]{1,0:T(8,128)(2,1)S(1)}, u32[]{:S(2)}, u32[]{:S(2)}) collective-permute-start(bf16[32,4096]{1,0:T(8,128)(2,1)} %get-tuple-element.33), channel_id=1, source_target_pairs={{0,8},{8,16},{16,24},{1,9},{9,17},{17,25},{2,10},{10,18},{18,26},{... | collective-permute-start | bytes 786440 | tf_op jit(solution)/shard_map/ppermute | solution.py:42
  104.3 10.4 %collective-permute-start.9 = (bf16[32,4096]{1,0:T(8,128)(2,1)}, bf16[32,4096]{1,0:T(8,128)(2,1)S(1)}, u32[]{:S(2)}, u32[]{:S(2)}) collective-permute-start(bf16[32,4096]{1,0:T(8,128)(2,1)} %get-tuple-element.34), channel_id=1, source_target_pairs={{8,0},{16,8},{24,16},{9,1},{17,9},{25,17},{10,2},{18,10},{26,18},{... | collective-permute-start | bytes 786440 | tf_op jit(solution)/shard_map/ppermute | solution.py:42
  108.3 8.0 %collective-permute-start.10 = (bf16[32,4096]{1,0:T(8,128)(2,1)}, bf16[32,4096]{1,0:T(8,128)(2,1)S(1)}, u32[]{:S(2)}, u32[]{:S(2)}) collective-permute-start(bf16[32,4096]{1,0:T(8,128)(2,1)} %get-tuple-element.35), channel_id=1, source_target_pairs={{0,1},{1,2},{2,3},{3,4},{4,5},{5,6},{6,7},{8,9},{9,10},{10,11},{11... | collective-permute-start | bytes 786440 | tf_op jit(solution)/shard_map/ppermute | solution.py:42
  112.8 7.9 %copy-start.3 = (bf16[32,4096]{1,0:T(8,128)(2,1)}, bf16[32,4096]{1,0:T(8,128)(2,1)S(1)}, u32[]{:S(2)}) copy-start(bf16[32,4096]{1,0:T(8,128)(2,1)S(1)} %collective-permute-done.6.r0) | copy-start | bytes 786436
  112.8 7.9 %collective-permute-start.11 = (bf16[32,4096]{1,0:T(8,128)(2,1)}, bf16[32,4096]{1,0:T(8,128)(2,1)S(1)}, u32[]{:S(2)}, u32[]{:S(2)}) collective-permute-start(bf16[32,4096]{1,0:T(8,128)(2,1)} %get-tuple-element.36), channel_id=1, source_target_pairs={{1,0},{2,1},{3,2},{4,3},{5,4},{6,5},{7,6},{9,8},{10,9},{11,10},{12... | collective-permute-start | bytes 786440 | tf_op jit(solution)/shard_map/ppermute | solution.py:42
  114.7 6.0 %copy-start.4 = (bf16[32,4096]{1,0:T(8,128)(2,1)}, bf16[32,4096]{1,0:T(8,128)(2,1)S(1)}, u32[]{:S(2)}) copy-start(bf16[32,4096]{1,0:T(8,128)(2,1)S(1)} %collective-permute-done.7.r1) | copy-start | bytes 786436
  114.7 6.0 %copy-start.5 = (bf16[32,4096]{1,0:T(8,128)(2,1)}, bf16[32,4096]{1,0:T(8,128)(2,1)S(1)}, u32[]{:S(2)}) copy-start(bf16[32,4096]{1,0:T(8,128)(2,1)S(1)} %collective-permute-done.8.r2) | copy-start | bytes 786436
  114.8 5.9 %copy-start.6 = (bf16[32,4096]{1,0:T(8,128)(2,1)}, bf16[32,4096]{1,0:T(8,128)(2,1)S(1)}, u32[]{:S(2)}) copy-start(bf16[32,4096]{1,0:T(8,128)(2,1)S(1)} %collective-permute-done.9.r3) | copy-start | bytes 786436
  116.4 4.3 %copy-start.7 = (bf16[32,4096]{1,0:T(8,128)(2,1)}, bf16[32,4096]{1,0:T(8,128)(2,1)S(1)}, u32[]{:S(2)}) copy-start(bf16[32,4096]{1,0:T(8,128)(2,1)S(1)} %collective-permute-done.10.r4) | copy-start | bytes 786436
  120.7 0.7 copy-start.8
